TPU v7x, 768 devices: a whole 4x8x12 slice. The times are simulated.
768 devices in a mesh: dp: 48 (over z, y_hi), fsdp: 16 (over y_lo, x, core).
Axes of the slice: x: 4, y: 8 (y_hi: 4, y_lo: 2; y = y_hi * 2 + y_lo), z: 12, core: 2. Of those that a mesh axis runs over, the one named last changes fastest.
Arguments:
- tokens: bfloat16 [16, 48, 128, 4096], P('fsdp', 'dp'), may hold values from -6 to 6
- grad_out: bfloat16 [16, 48, 128, 4096], P('fsdp', 'dp'), may hold values from -6 to 6
- qkv_weight: bfloat16 [4096, 768], P('fsdp'), may hold values from -0.1875 to 0.1875
- out_weight: bfloat16 [4096, 512], P('fsdp'), may hold values from -0.25 to 0.25
- range_len: int32 [16, 48], P('fsdp'), may hold values from 1 to 192, 6144 in all within a row
- doc_start: int32 [16, 48, 128], P('fsdp', 'dp'), may hold values 0 or 1
Outputs:
- block_out: bfloat16 [16, 48, 128, 4096], P('fsdp', 'dp')
- tokens_grad: bfloat16 [16, 48, 128, 4096], P('fsdp', 'dp')
- qkv_grad: float32 [4096, 768], P('fsdp')
- out_grad: float32 [4096, 512], P('fsdp')
Inputs may be any that keep to these rules, and one draw needn't show every extreme that they name: `range_len`: in each pack some range has exactly 192 positions.
All inputs are finite; a program needn't handle non-finite values. No bound on the sum of `doc_start` on one device may be relied on, other than what follows from the above.
Results may differ from a plain program's by a relative error of at most 0.019.
The roundings to bfloat16 on the way count: a program that leaves them out, or rounds other values in their place, can miss the bound.
Values may be sent and summed in bfloat16 or wider, within the bound.
No kernel may reach another device: no remote copies, remote signals or barrier semaphores. Data moves between devices by JAX's collectives and lax.ppermute only.
A program may use at most 64 MiB of HBM per device.

v0:
```python
import jax
import jax.numpy as jnp
from jax import lax
from jax.sharding import PartitionSpec as P

QH = 4


def normalize(token_rows):
    values = token_rows.astype(jnp.float32)
    inverse = lax.rsqrt(jnp.mean(values * values, axis=-1, keepdims=True) + 1e-05)
    return (values * inverse, inverse)


def contract_rows(left, right):
    return lax.dot_general(
        left, right, (((0,), (0,)), ((), ())), preferred_element_type=jnp.float32
    )


def contract_cols(left, right):
    return lax.dot_general(
        left, right, (((1,), (1,)), ((), ())), preferred_element_type=jnp.float32
    )


def allowed_keys(position, is_live, flags):
    starts_here = (flags > 0) & is_live & (position > 0)
    before = position[None, :] <= position[:, None]
    doc_number = jnp.sum((before & starts_here[None, :]).astype(jnp.int32), axis=1, dtype=jnp.int32)
    allowed = (
        before & (doc_number[None, :] == doc_number[:, None]) & is_live[None, :] & is_live[:, None]
    )
    return allowed | (position[None, :] == position[:, None])


def split_heads(slot_block, heads):
    head_size = slot_block.shape[1] // (heads + 2)
    rows = slot_block.shape[0]
    queries = slot_block[:, : heads * head_size].reshape(rows * heads, head_size)
    key_rows = slot_block[:, heads * head_size : (heads + 1) * head_size]
    value_rows = slot_block[:, (heads + 1) * head_size :]
    return (queries, key_rows, value_rows, head_size)


def attend_forward(slot_block, allowed, heads):
    queries, key_rows, value_rows, head_size = split_heads(slot_block, heads)
    rows = slot_block.shape[0]
    scores = contract_cols(queries, key_rows) * head_size ** (-0.5)
    scores = jnp.where(jnp.repeat(allowed, heads, axis=0), scores, -1e30)
    row_max = jnp.max(scores, axis=-1, keepdims=True)
    exponent = jnp.exp(scores - row_max)
    weights = exponent / jnp.sum(exponent, axis=-1, keepdims=True)
    attended = jnp.dot(
        weights.astype(jnp.bfloat16), value_rows, preferred_element_type=jnp.float32
    ).astype(jnp.bfloat16)
    return (attended.reshape(rows, heads * head_size), weights)


def attend_backward(slot_block, grad_attended, attended, weights, heads):
    queries, key_rows, value_rows, head_size = split_heads(slot_block, heads)
    rows = slot_block.shape[0]
    grad_heads = grad_attended.reshape(rows * heads, head_size)
    attended_heads = attended.reshape(rows * heads, head_size)
    grad_weights = contract_cols(grad_heads, value_rows)
    row_delta = jnp.sum(
        grad_heads.astype(jnp.float32) * attended_heads.astype(jnp.float32), axis=-1, keepdims=True
    )
    grad_scores = (weights * (grad_weights - row_delta) * head_size ** (-0.5)).astype(jnp.bfloat16)
    grad_queries = jnp.dot(grad_scores, key_rows, preferred_element_type=jnp.float32).astype(
        jnp.bfloat16
    )
    grad_keys = contract_rows(grad_scores, queries).astype(jnp.bfloat16)
    grad_values = contract_rows(weights.astype(jnp.bfloat16), grad_heads).astype(jnp.bfloat16)
    return jnp.concatenate(
        [grad_queries.reshape(rows, heads * head_size), grad_keys, grad_values], axis=1
    )


def on_device(tokens, grad_out, qkv_weight, out_weight, range_len, doc_start):
    token_rows = tokens[0, 0]
    cot_rows = grad_out[0, 0]
    flag_rows = doc_start[0, 0].astype(jnp.bfloat16)
    lengths = range_len[0]
    row_count = token_rows.shape[0]
    model_width = token_rows.shape[1]
    qkv_width = qkv_weight.shape[1]
    out_width = out_weight.shape[1]
    groups = lax.axis_size("dp")
    owners = lax.axis_size("fsdp")
    my_index = lax.axis_index("dp")
    slot_count = 3 * row_count // 2 // groups
    total_slots = groups * slot_count
    range_end = jnp.cumsum(lengths, dtype=jnp.int32)
    starts = range_end - lengths
    pack_row = my_index + groups * jnp.arange(row_count, dtype=jnp.int32)
    target = jnp.sum(
        (range_end[None, :] <= pack_row[:, None]).astype(jnp.int32), axis=1, dtype=jnp.int32
    )
    range_ids = jnp.arange(groups, dtype=jnp.int32)
    range_first = jnp.sum(
        jnp.where(range_ids[None, :] == target[:, None], starts[None, :], 0),
        axis=1,
        dtype=jnp.int32,
    )
    flat_slot = target * slot_count + (pack_row - range_first) // groups
    routing = (jnp.arange(total_slots, dtype=jnp.int32)[:, None] == flat_slot[None, :]).astype(
        jnp.bfloat16
    )

    def to_slots(array):
        placed = jnp.dot(routing, array, preferred_element_type=jnp.float32).astype(jnp.bfloat16)
        return placed.reshape((groups, slot_count) + array.shape[1:])

    def from_slots(array):
        return contract_rows(routing, array.reshape(total_slots, -1)).astype(jnp.bfloat16)

    weight_in, weight_back = (
        lax.all_gather(qkv_weight, "fsdp", axis=0, tiled=True),
        lax.all_gather(out_weight, "fsdp", axis=0, tiled=True),
    )
    normed, inverse = normalize(token_rows)
    normed_b = normed.astype(jnp.bfloat16)
    projected = jnp.dot(normed_b, weight_in, preferred_element_type=jnp.float32).astype(
        jnp.bfloat16
    )
    grad_attn = jnp.dot(cot_rows, weight_back, preferred_element_type=jnp.float32).astype(
        jnp.bfloat16
    )
    my_start = starts[my_index]
    my_length = lengths[my_index]
    source_ids = jnp.arange(groups, dtype=jnp.int32)[:, None]
    slot_ids = jnp.arange(slot_count, dtype=jnp.int32)[None, :]
    position = ((source_ids - my_start) % groups + groups * slot_ids).reshape(total_slots)
    is_live = position < my_length
    got_qkv, got_flags = (
        lax.all_to_all(to_slots(projected), "dp", split_axis=0, concat_axis=0, tiled=True),
        lax.all_to_all(to_slots(flag_rows), "dp", split_axis=0, concat_axis=0, tiled=True),
    )
    allowed = allowed_keys(position, is_live, got_flags.reshape(total_slots))
    slot_block = got_qkv.reshape(total_slots, qkv_width)
    attended, weights = attend_forward(slot_block, allowed, QH)
    back_out = lax.all_to_all(
        attended.reshape(groups, slot_count, out_width),
        "dp",
        split_axis=0,
        concat_axis=0,
        tiled=True,
    )
    got_grad = lax.all_to_all(to_slots(grad_attn), "dp", split_axis=0, concat_axis=0, tiled=True)
    grad_block = attend_backward(
        slot_block, got_grad.reshape(total_slots, out_width), attended, weights, QH
    )
    back_grad = lax.all_to_all(
        grad_block.reshape(groups, slot_count, qkv_width),
        "dp",
        split_axis=0,
        concat_axis=0,
        tiled=True,
    )
    attended_rows = from_slots(back_out)
    grad_rows = from_slots(back_grad)
    result = (token_rows.astype(jnp.float32) + contract_cols(attended_rows, weight_back)).astype(
        jnp.bfloat16
    )
    grad_normed = contract_cols(grad_rows, weight_in)
    correction = jnp.mean(grad_normed * normed, axis=-1, keepdims=True)
    tokens_grad = (
        cot_rows.astype(jnp.float32) + inverse * (grad_normed - normed * correction)
    ).astype(jnp.bfloat16)
    share = model_width // owners
    normed_cols, cot_cols = (
        lax.all_to_all(normed_b, "fsdp", split_axis=1, concat_axis=0, tiled=True),
        lax.all_to_all(cot_rows, "fsdp", split_axis=1, concat_axis=0, tiled=True),
    )
    grad_all, att_all = (
        lax.all_gather(grad_rows, "fsdp", axis=0, tiled=True),
        lax.all_gather(attended_rows, "fsdp", axis=0, tiled=True),
    )
    batched = (((1,), (1,)), ((0,), (0,)))
    normed_part = normed_cols.reshape(owners, row_count, share)
    cot_part = cot_cols.reshape(owners, row_count, share)
    first = lax.dot_general(
        normed_part,
        grad_all.reshape(owners, row_count, qkv_width),
        batched,
        preferred_element_type=jnp.float32,
    )
    second = lax.dot_general(
        cot_part,
        att_all.reshape(owners, row_count, out_width),
        batched,
        preferred_element_type=jnp.float32,
    )
    rounded = lax.optimization_barrier(
        jnp.concatenate([first, second], axis=2).astype(jnp.bfloat16)
    )
    grad_shard = jnp.sum(rounded.astype(jnp.float32), axis=0)
    summed = lax.psum(grad_shard, "dp")
    return (
        result[None, None],
        tokens_grad[None, None],
        summed[:, :qkv_width],
        summed[:, qkv_width:],
    )


def solution(mesh):
    return jax.shard_map(
        on_device,
        mesh=mesh,
        in_specs=(
            P("fsdp", "dp", None, None),
            P("fsdp", "dp", None, None),
            P("fsdp", None),
            P("fsdp", None),
            P("fsdp", None),
            P("fsdp", "dp", None),
        ),
        out_specs=(
            P("fsdp", "dp", None, None),
            P("fsdp", "dp", None, None),
            P("fsdp", None),
            P("fsdp", None),
        ),
        check_vma=False,
    )
```

profile of v0, /device:TPU:16, one launch (start us, length us, event | category | flops | bytes accessed | tf_op | source)
XLA Modules:
  0.0 765.0 jit_solution(5484853623065522793)
XLA Ops:
  12.0 21.1 %all-to-all-start = ((bf16[48,1,4]{2,1,0:T(2,128)(2,1)}), bf16[48,1,4]{2,1,0:T(2,128)(2,1)S(1)}, u32[]{:S(2)}, u32[]{:S(2)}) async-start(bf16[48,1,4]{2,1,0:T(2,128)(2,1)} %all_to_all.51), calls=%async_computation | async-start | bytes 49152 | tf_op jit(solution)/shard_map/all_to_all | solution.py:138
  33.1 1.2 constant_dynamic-slice_fusion
  35.6 1.5 fusion.2
  37.2 25.1 %all-gather.7.cloned.1.call-done = bf16[4096,512]{1,0:T(8,128)(2,1)} async-done(((bf16[256,512]{1,0:T(8,128)(2,1)}), bf16[4096,512]{1,0:T(8,128)(2,1)}) %all-gather.7.cloned.1.call-update) | async-done | bytes 4194320 | tf_op jit(solution)/shard_map/all_gather | solution.py:120
  62.3 3.4 convolution_convert_fusion.4
  66.4 15.6 %all-to-all-start.3 = ((bf16[48,4,512]{2,1,0:T(4,128)(2,1)}), bf16[48,4,512]{2,1,0:T(4,128)(2,1)S(1)}, u32[]{:S(2)}, u32[]{:S(2)}) async-start(bf16[48,4,512]{2,1,0:T(4,128)(2,1)} %reshape.214), calls=%async_computation.3 | async-start | bytes 393216 | tf_op jit(solution)/shard_map/all_to_all | solution.py:150
  82.7 36.5 %all-gather.5.cloned.1.call-done = bf16[4096,768]{1,0:T(8,128)(2,1)} async-done(((bf16[256,768]{1,0:T(8,128)(2,1)}), bf16[4096,768]{1,0:T(8,128)(2,1)}) %all-gather.5.cloned.1.call-update) | async-done | bytes 6291472 | tf_op jit(solution)/shard_map/all_gather | solution.py:119
  119.2 4.1 convolution_convert_fusion.1
  124.1 14.5 %all-to-all-start.1 = ((bf16[48,4,768]{2,1,0:T(4,128)(2,1)}), bf16[48,4,768]{2,1,0:T(4,128)(2,1)S(1)}, u32[]{:S(2)}, u32[]{:S(2)}) async-start(bf16[48,4,768]{2,1,0:T(4,128)(2,1)} %reshape.210), calls=%async_computation.1 | async-start | bytes 589824 | tf_op jit(solution)/shard_map/all_to_all | solution.py:137
  141.0 17.5 %all-to-all-done.1 = bf16[48,4,768]{2,1,0:T(4,128)(2,1)S(1)} async-done(((bf16[48,4,768]{2,1,0:T(4,128)(2,1)}), bf16[48,4,768]{2,1,0:T(4,128)(2,1)S(1)}, u32[]{:S(2)}, u32[]{:S(2)}) %all-to-all-start.1) | async-done | bytes 294944 | tf_op jit(solution)/shard_map/all_to_all | solution.py:137
  159.8 21.9 %all_to_all.59 = bf16[48,4,512]{2,1,0:T(4,128)(2,1)S(1)} all-to-all(bf16[48,4,512]{2,1,0:T(4,128)(2,1)S(1)} %reshape_reshape.6), channel_id=1, replica_groups=mesh['dp'=48,'fsdp'=16] {'dp'}, dimensions={0} | all-to-all | bytes 393216 | tf_op jit(solution)/shard_map/all_to_all | solution.py:143
  182.7 1.1 fusion.7
  184.5 1.1 convolution_convert_fusion.3
  185.9 1.2 convolution_convert_fusion.10
  187.3 24.5 %all_to_all.60 = bf16[48,4,768]{2,1,0:T(4,128)(2,1)S(1)} all-to-all(bf16[48,4,768]{2,1,0:T(4,128)(2,1)S(1)} %pad_maximum_fusion.1), channel_id=1, replica_groups=mesh['dp'=48,'fsdp'=16] {'dp'}, dimensions={0} | all-to-all | bytes 589824 | tf_op jit(solution)/shard_map/all_to_all | solution.py:154
  213.5 1.3 copy.40
  214.8 4.3 all-to-all-start.6
  219.7 1.2 multiply_convert_fusion
  220.9 14.8 %all-to-all-done.6 = bf16[128,16,256]{2,0,1:T(8,128)(2,1)} async-done(((bf16[128,16,256]{2,0,1:T(8,128)(2,1)}), bf16[128,16,256]{2,0,1:T(8,128)(2,1)}, u32[]{:S(2)}, u32[]{:S(2)}) %all-to-all-start.6) | async-done | bytes 1048608 | tf_op jit(solution)/shard_map/all_to_all | solution.py:174
  235.7 3.8 all-to-all-start.5
  239.6 4.6 fusion.1
  244.2 5.2 convert_bitcast_fusion
  249.4 10.4 %all-to-all-done.5 = bf16[128,16,256]{0,2,1:T(8,128)(2,1)S(1)} async-done(((bf16[128,16,256]{0,2,1:T(8,128)(2,1)}), bf16[128,16,256]{0,2,1:T(8,128)(2,1)S(1)}, u32[]{:S(2)}, u32[]{:S(2)}) %all-to-all-start.5) | async-done | bytes 1048608 | tf_op jit(solution)/shard_map/all_to_all | solution.py:173
  259.9 18.1 %all-gather.9.cloned.1.call-done = bf16[2048,768]{1,0:T(8,128)(2,1)} async-done(((bf16[128,768]{1,0:T(8,128)(2,1)}), bf16[2048,768]{1,0:T(8,128)(2,1)}) %all-gather.9.cloned.1.call-update) | async-done | bytes 3145744 | tf_op jit(solution)/shard_map/all_gather | solution.py:177
  277.9 3.8 convolution_convert_fusion
  281.8 4.5 pad_maximum_fusion
  286.3 2.6 convert_reduce_fusion
  288.9 5.5 multiply_reduce_fusion
  294.4 1.6 fusion.10
  296.1 458.5 %all-reduce.2.cloned.1.call-done = f32[256,1280]{1,0:T(8,128)} async-done(((f32[256,1280]{1,0:T(8,128)}), f32[256,1280]{1,0:T(8,128)}) %all-reduce.2.cloned.1.call-update) | async-done | bytes 1310736 | tf_op jit(solution)/shard_map/psum | solution.py:199
  754.5 1.9 slice.27
  756.4 2.1 slice.26
  (80 shorter events, 16.3 us)
Async XLA Ops:
  7.2 55.1 %all-gather.7.cloned.1.call-start = ((), (), s32[]{:S(2)}) async-start(), calls=%async_computation.8 | async-start | bytes 4456448 | tf_op jit(solution)/shard_map/all_gather | solution.py:120
  7.9 111.3 %all-gather.5.cloned.1.call-start = ((), (), s32[]{:S(2)}) async-start(), calls=%async_computation.7 | async-start | bytes 6684672 | tf_op jit(solution)/shard_map/all_gather | solution.py:119
  12.0 54.4 %all-to-all-start = ((bf16[48,1,4]{2,1,0:T(2,128)(2,1)}), bf16[48,1,4]{2,1,0:T(2,128)(2,1)S(1)}, u32[]{:S(2)}, u32[]{:S(2)}) async-start(bf16[48,1,4]{2,1,0:T(2,128)(2,1)} %all_to_all.51), calls=%async_computation | async-start | bytes 49152 | tf_op jit(solution)/shard_map/all_to_all | solution.py:138
  37.1 82.1 %copy-start = (bf16[1,1,128,4096]{3,2,1,0:T(8,128)(2,1)S(1)}, bf16[1,1,128,4096]{3,2,1,0:T(8,128)(2,1)}, u32[]{:S(2)}) copy-start(bf16[1,1,128,4096]{3,2,1,0:T(8,128)(2,1)} %param.6) | copy-start | bytes 3145732
  66.4 57.7 %all-to-all-start.3 = ((bf16[48,4,512]{2,1,0:T(4,128)(2,1)}), bf16[48,4,512]{2,1,0:T(4,128)(2,1)S(1)}, u32[]{:S(2)}, u32[]{:S(2)}) async-start(bf16[48,4,512]{2,1,0:T(4,128)(2,1)} %reshape.214), calls=%async_computation.3 | async-start | bytes 393216 | tf_op jit(solution)/shard_map/all_to_all | solution.py:150
  124.1 34.4 %all-to-all-start.1 = ((bf16[48,4,768]{2,1,0:T(4,128)(2,1)}), bf16[48,4,768]{2,1,0:T(4,128)(2,1)S(1)}, u32[]{:S(2)}, u32[]{:S(2)}) async-start(bf16[48,4,768]{2,1,0:T(4,128)(2,1)} %reshape.210), calls=%async_computation.1 | async-start | bytes 589824 | tf_op jit(solution)/shard_map/all_to_all | solution.py:137
  138.6 105.6 %all-gather.11.cloned.1.call-start = ((), (), s32[]{:S(2)}) async-start(), calls=%async_computation.10 | async-start | bytes 2228224 | tf_op jit(solution)/shard_map/all_gather | solution.py:178
  158.6 24.1 %copy-start.6 = (bf16[192,768]{1,0:T(8,128)(2,1)}, bf16[192,768]{1,0:T(8,128)(2,1)S(1)}, u32[]{:S(2)}) copy-start(bf16[192,768]{1,0:T(8,128)(2,1)S(1)} %reshape.211) | copy-start | bytes 884740
  182.6 95.3 %all-gather.9.cloned.1.call-start = ((), (), s32[]{:S(2)}) async-start(), calls=%async_computation.9 | async-start | bytes 3342336 | tf_op jit(solution)/shard_map/all_gather | solution.py:177
  182.6 30.1 %copy-start.3 = (bf16[1,1,128,4096]{3,2,1,0:T(8,128)(2,1)S(1)}, bf16[1,1,128,4096]{3,2,1,0:T(8,128)(2,1)}, u32[]{:S(2)}) copy-start(bf16[1,1,128,4096]{3,2,1,0:T(8,128)(2,1)} %param.7) | copy-start | bytes 3145732
  183.8 0.7 copy-start.8
  214.8 20.9 %all-to-all-start.6 = ((bf16[128,16,256]{2,0,1:T(8,128)(2,1)}), bf16[128,16,256]{2,0,1:T(8,128)(2,1)}, u32[]{:S(2)}, u32[]{:S(2)}) async-start(bf16[128,16,256]{2,0,1:T(8,128)(2,1)} %copy.40), calls=%async_computation.6 | async-start | bytes 2097152 | tf_op jit(solution)/shard_map/all_to_all | solution.py:174
  219.7 19.9 %copy-start.7 = (bf16[128,512]{1,0:T(8,128)(2,1)S(1)}, bf16[128,512]{1,0:T(8,128)(2,1)}, u32[]{:S(2)}) copy-start(bf16[128,512]{1,0:T(8,128)(2,1)} %convolution_convert_fusion.8) | copy-start | bytes 393220
  235.7 24.2 %all-to-all-start.5 = ((bf16[128,16,256]{0,2,1:T(8,128)(2,1)}), bf16[128,16,256]{0,2,1:T(8,128)(2,1)S(1)}, u32[]{:S(2)}, u32[]{:S(2)}) async-start(bf16[128,16,256]{0,2,1:T(8,128)(2,1)} %multiply_convert_fusion), calls=%async_computation.5 | async-start | bytes 2097152 | tf_op jit(solution)/shard_map/all_to_all | solution.py:173
  239.5 515.0 %all-reduce.2.cloned.1.call-start = ((), (), s32[]{:S(2)}) async-start(), calls=%async_computation.11 | async-start | bytes 2621440 | tf_op jit(solution)/shard_map/psum | solution.py:199
  277.9 3.8 copy-start.2
  286.3 2.7 copy-start.5
  288.9 5.5 copy-start.1
  288.9 5.5 copy-start.4
Sparse Core Ops, SparseCore 0:
  10.4 51.8 all-gather.6
  64.7 54.4 all-gather.4
  182.7 34.9 all-gather.10
  220.5 57.3 all-gather.8
  289.0 465.4 all-reduce.1
where the time goes:
time: 767 us; the launch traced here: 765 us
  waiting for transfers between devices  582 us (76%)
  starting transfers between devices  59.6 us (8%)
  blocking collectives  46.3 us (6%)
  matrix products  33.4 us (4%)
  other arithmetic  15.4 us (2%)
  between operations  14.2 us (2%)
  local copies, waits for them, and re-layouts  13.9 us (2%)
    psum x1, waiting for transfers between devices, on_device(): summed = lax.psum(grad_shard, 'dp')  458 us
    all_gather x1, waiting for transfers between devices, on_device(): lax.all_gather(qkv_weight, 'fsdp', axis=0, tiled=True)  36.5 us
    all_gather x1, waiting for transfers between devices, on_device(): lax.all_gather(out_weight, 'fsdp', axis=0, tiled=True)  25.1 us
    all_to_all x1, blocking collectives, on_device(): lax.all_to_all(grad_block.reshape(groups, slot_count, qkv_width), 'dp', s...  24.5 us
    all_to_all x1, blocking collectives, on_device(): lax.all_to_all(attended.reshape(groups, slot_count, out_width), 'dp', spl...  21.9 us
    all_to_all x1, starting transfers between devices, on_device(): lax.all_to_all(to_slots(flag_rows), 'dp', split_axis=0, concat_axis=0, ti...  21.1 us
    all_gather x1, waiting for transfers between devices, on_device(): lax.all_gather(grad_rows, 'fsdp', axis=0, tiled=True)  18.1 us
    all_to_all x1, waiting for transfers between devices, on_device(): lax.all_to_all(to_slots(projected), 'dp', split_axis=0, concat_axis=0, ti...  17.5 us
  transfers between devices with their start and end apart: 10, of which 7 were waited for; matrix products, arithmetic and copies ran while one was open for 6% of the time, Pallas kernels for 0%

commit v1 on v0

--- a/solution.py
+++ b/solution.py
@@ -1,9 +1,12 @@
 import jax
 import jax.numpy as jnp
 from jax import lax
+from jax.sharding import Mesh
 from jax.sharding import PartitionSpec as P
 
 QH = 4
+DP = ("z", "yh")
+FSDP = ("yl", "x", "core")
 
 
 def normalize(token_rows):
@@ -86,9 +89,9 @@
     model_width = token_rows.shape[1]
     qkv_width = qkv_weight.shape[1]
     out_width = out_weight.shape[1]
-    groups = lax.axis_size("dp")
-    owners = lax.axis_size("fsdp")
-    my_index = lax.axis_index("dp")
+    groups = lax.axis_size(DP)
+    owners = lax.axis_size(FSDP)
+    my_index = lax.axis_index(DP)
     slot_count = 3 * row_count // 2 // groups
     total_slots = groups * slot_count
     range_end = jnp.cumsum(lengths, dtype=jnp.int32)
@@ -116,8 +119,8 @@
         return contract_rows(routing, array.reshape(total_slots, -1)).astype(jnp.bfloat16)
 
     weight_in, weight_back = (
-        lax.all_gather(qkv_weight, "fsdp", axis=0, tiled=True),
-        lax.all_gather(out_weight, "fsdp", axis=0, tiled=True),
+        lax.all_gather(qkv_weight, FSDP, axis=0, tiled=True),
+        lax.all_gather(out_weight, FSDP, axis=0, tiled=True),
     )
     normed, inverse = normalize(token_rows)
     normed_b = normed.astype(jnp.bfloat16)
@@ -133,33 +136,20 @@
     slot_ids = jnp.arange(slot_count, dtype=jnp.int32)[None, :]
     position = ((source_ids - my_start) % groups + groups * slot_ids).reshape(total_slots)
     is_live = position < my_length
-    got_qkv, got_flags = (
-        lax.all_to_all(to_slots(projected), "dp", split_axis=0, concat_axis=0, tiled=True),
-        lax.all_to_all(to_slots(flag_rows), "dp", split_axis=0, concat_axis=0, tiled=True),
-    )
+    got_flags = swap_dp(to_slots(flag_rows))
+    got_qkv = swap_dp(to_slots(projected))
     allowed = allowed_keys(position, is_live, got_flags.reshape(total_slots))
     slot_block = got_qkv.reshape(total_slots, qkv_width)
     attended, weights = attend_forward(slot_block, allowed, QH)
-    back_out = lax.all_to_all(
-        attended.reshape(groups, slot_count, out_width),
-        "dp",
-        split_axis=0,
-        concat_axis=0,
-        tiled=True,
-    )
-    got_grad = lax.all_to_all(to_slots(grad_attn), "dp", split_axis=0, concat_axis=0, tiled=True)
+    got_grad = swap_dp(to_slots(grad_attn))
     grad_block = attend_backward(
         slot_block, got_grad.reshape(total_slots, out_width), attended, weights, QH
     )
-    back_grad = lax.all_to_all(
-        grad_block.reshape(groups, slot_count, qkv_width),
-        "dp",
-        split_axis=0,
-        concat_axis=0,
-        tiled=True,
-    )
-    attended_rows = from_slots(back_out)
-    grad_rows = from_slots(back_grad)
+    both = jnp.concatenate([grad_block, attended], axis=1)
+    back = swap_dp(both.reshape(groups, slot_count, qkv_width + out_width))
+    both_rows = from_slots(back)
+    grad_rows = both_rows[:, :qkv_width]
+    attended_rows = both_rows[:, qkv_width:]
     result = (token_rows.astype(jnp.float32) + contract_cols(attended_rows, weight_back)).astype(
         jnp.bfloat16
     )
@@ -168,35 +158,19 @@
     tokens_grad = (
         cot_rows.astype(jnp.float32) + inverse * (grad_normed - normed * correction)
     ).astype(jnp.bfloat16)
-    share = model_width // owners
     normed_cols, cot_cols = (
-        lax.all_to_all(normed_b, "fsdp", split_axis=1, concat_axis=0, tiled=True),
-        lax.all_to_all(cot_rows, "fsdp", split_axis=1, concat_axis=0, tiled=True),
-    )
-    grad_all, att_all = (
-        lax.all_gather(grad_rows, "fsdp", axis=0, tiled=True),
-        lax.all_gather(attended_rows, "fsdp", axis=0, tiled=True),
-    )
-    batched = (((1,), (1,)), ((0,), (0,)))
-    normed_part = normed_cols.reshape(owners, row_count, share)
-    cot_part = cot_cols.reshape(owners, row_count, share)
-    first = lax.dot_general(
-        normed_part,
-        grad_all.reshape(owners, row_count, qkv_width),
-        batched,
-        preferred_element_type=jnp.float32,
-    )
-    second = lax.dot_general(
-        cot_part,
-        att_all.reshape(owners, row_count, out_width),
-        batched,
-        preferred_element_type=jnp.float32,
-    )
-    rounded = lax.optimization_barrier(
-        jnp.concatenate([first, second], axis=2).astype(jnp.bfloat16)
-    )
-    grad_shard = jnp.sum(rounded.astype(jnp.float32), axis=0)
-    summed = lax.psum(grad_shard, "dp")
+        lax.all_to_all(normed_b, FSDP, split_axis=1, concat_axis=0, tiled=True),
+        lax.all_to_all(cot_rows, FSDP, split_axis=1, concat_axis=0, tiled=True),
+    )
+    both_all = lax.all_gather(both_rows, FSDP, axis=0, tiled=True)
+    partial = jnp.concatenate(
+        [
+            contract_rows(normed_cols, both_all[:, :qkv_width]),
+            contract_rows(cot_cols, both_all[:, qkv_width:]),
+        ],
+        axis=1,
+    ).astype(jnp.bfloat16)
+    summed = sum_over_dp(partial, groups)
     return (
         result[None, None],
         tokens_grad[None, None],
@@ -205,23 +179,43 @@
     )
 
 
+def swap_dp(array):
+    return lax.all_to_all(array, DP, split_axis=0, concat_axis=0, tiled=True)
+
+
+def sum_over_dp(partial, groups):
+    rows, cols = partial.shape
+    tiles = (rows // 8) * (cols // 128)
+    each = -(-tiles // groups)
+    tiled = jnp.swapaxes(partial.reshape(rows // 8, 8, cols // 128, 128), 1, 2)
+    tiled = tiled.reshape(tiles, 8, 128)
+    tiled = jnp.pad(tiled, ((0, groups * each - tiles), (0, 0), (0, 0)))
+    got = swap_dp(tiled.reshape(groups, each, 8, 128))
+    mine = jnp.sum(got.astype(jnp.float32), axis=0).astype(jnp.bfloat16)
+    whole = lax.all_gather(mine, "yh", axis=0, tiled=True)
+    whole = lax.all_gather(whole, "z", axis=0, tiled=True)[:tiles]
+    whole = jnp.swapaxes(whole.reshape(rows // 8, cols // 128, 8, 128), 1, 2)
+    return whole.reshape(rows, cols).astype(jnp.float32)
+
+
 def solution(mesh):
+    fine = Mesh(mesh.devices.reshape(12, 4, 2, 4, 2), DP + FSDP)
     return jax.shard_map(
         on_device,
-        mesh=mesh,
+        mesh=fine,
         in_specs=(
-            P("fsdp", "dp", None, None),
-            P("fsdp", "dp", None, None),
-            P("fsdp", None),
-            P("fsdp", None),
-            P("fsdp", None),
-            P("fsdp", "dp", None),
+            P(FSDP, DP, None, None),
+            P(FSDP, DP, None, None),
+            P(FSDP, None),
+            P(FSDP, None),
+            P(FSDP, None),
+            P(FSDP, DP, None),
         ),
         out_specs=(
-            P("fsdp", "dp", None, None),
-            P("fsdp", "dp", None, None),
-            P("fsdp", None),
-            P("fsdp", None),
+            P(FSDP, DP, None, None),
+            P(FSDP, DP, None, None),
+            P(FSDP, None),
+            P(FSDP, None),
         ),
         check_vma=False,
     )

time: 767 us -> 346 us (0.45)
  waiting for transfers between devices: 582 us -> 148 us
  blocking collectives: 46.3 us -> 70.6 us
  matrix products: 33.4 us -> 24 us
    psum x1 -> x0, waiting for transfers between devices: 458 us -> none  [on_device(): summed = lax.psum(grad_shard, 'dp')]
    all_gather x0 -> x2, blocking collectives: none -> 39.4 us  [the longest x1 25.7 us: sum_over_dp(): whole = lax.all_gather(whole, 'z', axis=0, tiled=True)[:tiles]]
    all_to_all x5 -> x6, waiting for transfers between devices: 42.7 us -> 62.7 us  [the longest x4 40.3 us: swap_dp(): return lax.all_to_all(array, DP, split_axis=0, concat_axis=0, tiled=True)]
    all_to_all x2 -> x1, blocking collectives: 46.3 us -> 31.2 us  [swap_dp(): return lax.all_to_all(array, DP, split_axis=0, concat_axis=0, tiled=True)]
    dot_general x2 -> x0, matrix products: 9 us -> none  [the longest x1 5.18 us: on_device(): lax.dot_general(cot_part, att_all.reshape(owners, row_count, out_width),...]
    all_to_all x5 -> x6, starting transfers between devices: 59.4 us -> 66.1 us  [the longest x4 57.9 us: swap_dp(): return lax.all_to_all(array, DP, split_axis=0, concat_axis=0, tiled=True)]
    all_gather x4 -> x3, waiting for transfers between devices: 79.7 us -> 84.3 us  [the longest x1 36.8 us: on_device(): lax.all_gather(qkv_weight, FSDP, axis=0, tiled=True)]
  transfers between devices with their start and end apart: 10 -> 9, of which waited for: 7 -> 6; matrix products, arithmetic and copies ran while one was open for 6% -> 10% of each run, Pallas kernels for 0% -> 0%
where the time goes in v1:
time: 346 us; the launch traced here: 345 us
  waiting for transfers between devices  148 us (43%)
  blocking collectives  70.6 us (20%)
  starting transfers between devices  66.2 us (19%)
  matrix products  24 us (7%)
  between operations  14.1 us (4%)
  local copies, waits for them, and re-layouts  12.3 us (4%)
  other arithmetic  9.55 us (3%)
    all_to_all x4, starting transfers between devices, swap_dp(): return lax.all_to_all(array, DP, split_axis=0, concat_axis=0, tiled=True)  57.9 us
    all_to_all x4, waiting for transfers between devices, swap_dp(): return lax.all_to_all(array, DP, split_axis=0, concat_axis=0, tiled=True)  40.3 us
    all_gather x1, waiting for transfers between devices, on_device(): lax.all_gather(qkv_weight, FSDP, axis=0, tiled=True)  36.8 us
    all_to_all x1, blocking collectives, swap_dp(): return lax.all_to_all(array, DP, split_axis=0, concat_axis=0, tiled=True)  31.2 us
    all_gather x1, blocking collectives, sum_over_dp(): whole = lax.all_gather(whole, 'z', axis=0, tiled=True)[:tiles]  25.7 us
    all_gather x1, waiting for transfers between devices, on_device(): lax.all_gather(out_weight, FSDP, axis=0, tiled=True)  25.1 us
    all_to_all x1, waiting for transfers between devices, on_device(): lax.all_to_all(cot_rows, FSDP, split_axis=1, concat_axis=0, tiled=True)  22.4 us
    all_gather x1, waiting for transfers between devices, on_device(): both_all = lax.all_gather(both_rows, FSDP, axis=0, tiled=True)  22.3 us
  transfers between devices with their start and end apart: 9, of which 6 were waited for; matrix products, arithmetic and copies ran while one was open for 10% of the time, Pallas kernels for 0%

profile of v1, /device:TPU:16, one launch (start us, length us, event | category | flops | bytes accessed | tf_op | source)
XLA Modules:
  0.0 345.1 jit_solution(36434600179994053)
XLA Ops:
  10.5 0.8 fusion.38
  12.1 21.1 %all-to-all-start = ((bf16[48,1,4]{2,1,0:T(2,128)(2,1)}), bf16[48,1,4]{2,1,0:T(2,128)(2,1)S(1)}, u32[]{:S(2)}, u32[]{:S(2)}) async-start(bf16[48,1,4]{2,1,0:T(2,128)(2,1)} %all_to_all.57), calls=%async_computation | async-start | bytes 49152 | tf_op jit(solution)/shard_map/all_to_all | solution.py:183
  33.1 1.2 constant_dynamic-slice_fusion
  35.6 1.5 fusion.6
  37.2 25.1 %all-gather.6.cloned.1.call-done = bf16[4096,512]{1,0:T(8,128)(2,1)} async-done(((bf16[256,512]{1,0:T(8,128)(2,1)}), bf16[4096,512]{1,0:T(8,128)(2,1)}) %all-gather.6.cloned.1.call-update) | async-done | bytes 4194320 | tf_op jit(solution)/shard_map/all_gather | solution.py:123
  62.3 3.1 convolution_convert_fusion.4
  66.1 15.6 %all-to-all-start.2 = ((bf16[48,4,512]{2,1,0:T(4,128)(2,1)}), bf16[48,4,512]{2,1,0:T(4,128)(2,1)S(1)}, u32[]{:S(2)}, u32[]{:S(2)}) async-start(bf16[48,4,512]{2,1,0:T(4,128)(2,1)} %reshape.218), calls=%async_computation.2 | async-start | bytes 393216 | tf_op jit(solution)/shard_map/all_to_all | solution.py:183
  82.4 36.8 %all-gather.4.cloned.1.call-done = bf16[4096,768]{1,0:T(8,128)(2,1)} async-done(((bf16[256,768]{1,0:T(8,128)(2,1)}), bf16[4096,768]{1,0:T(8,128)(2,1)}) %all-gather.4.cloned.1.call-update) | async-done | bytes 6291472 | tf_op jit(solution)/shard_map/all_gather | solution.py:122
  119.2 4.1 %convolution_convert_fusion.1 = bf16[192,768]{1,0:T(8,128)(2,1)S(1)} fusion(bf16[4096,768]{1,0:T(8,128)(2,1)} %all-gather.4.cloned.1.call-done, bf16[1,1,128,4096]{3,2,1,0:T(8,128)(2,1)S(1)} %copy-done, f32[128]{0:T(128)S(1)} %add_rsqrt_fusion, s32[128]{0:T(128)S(1)} %fusion.48), kind=kOutput, calls=%fused_computation.24 | convolution fusion | flops 844898304 | bytes 7635968 | tf_op jit(solution)/shard_map/dot_general | solution.py:115
  124.1 14.4 %all-to-all-start.1 = ((bf16[48,4,768]{2,1,0:T(4,128)(2,1)}), bf16[48,4,768]{2,1,0:T(4,128)(2,1)S(1)}, u32[]{:S(2)}, u32[]{:S(2)}) async-start(bf16[48,4,768]{2,1,0:T(4,128)(2,1)} %reshape.215), calls=%async_computation.1 | async-start | bytes 589824 | tf_op jit(solution)/shard_map/all_to_all | solution.py:183
  140.9 17.5 %all-to-all-done.1 = bf16[48,4,768]{2,1,0:T(4,128)(2,1)S(1)} async-done(((bf16[48,4,768]{2,1,0:T(4,128)(2,1)}), bf16[48,4,768]{2,1,0:T(4,128)(2,1)S(1)}, u32[]{:S(2)}, u32[]{:S(2)}) %all-to-all-start.1) | async-done | bytes 294944 | tf_op jit(solution)/shard_map/all_to_all | solution.py:183
  161.0 31.2 %all_to_all.65 = bf16[48,4,1280]{2,1,0:T(4,128)(2,1)S(1)} all-to-all(bf16[48,4,1280]{2,1,0:T(4,128)(2,1)S(1)} %pad_maximum_fusion.1), channel_id=1, replica_groups=mesh['z'=12,'yh'=4,'yl'=2,'x'=4,'core'=2] {'z','yh'}, dimensions={0} | all-to-all | bytes 983040 | tf_op jit(solution)/shard_map/all_to_all | solution.py:183
  192.4 1.0 convolution_convert_fusion
  193.5 1.3 copy.41
  194.8 3.7 %all-to-all-start.5 = ((bf16[128,16,256]{0,2,1:T(8,128)(2,1)}), bf16[128,16,256]{0,2,1:T(8,128)(2,1)S(1)}, u32[]{:S(2)}, u32[]{:S(2)}) async-start(bf16[128,16,256]{0,2,1:T(8,128)(2,1)} %bitcast.87), calls=%async_computation.5 | async-start | bytes 2097152 | tf_op jit(solution)/shard_map/all_to_all | solution.py:163
  198.8 2.1 fusion.7
  201.0 22.4 %all-to-all-done.5 = bf16[128,16,256]{0,2,1:T(8,128)(2,1)S(1)} async-done(((bf16[128,16,256]{0,2,1:T(8,128)(2,1)}), bf16[128,16,256]{0,2,1:T(8,128)(2,1)S(1)}, u32[]{:S(2)}, u32[]{:S(2)}) %all-to-all-start.5) | async-done | bytes 1048608 | tf_op jit(solution)/shard_map/all_to_all | solution.py:163
  223.4 4.5 %all-to-all-start.4 = ((bf16[128,16,256]{2,0,1:T(8,128)(2,1)}), bf16[128,16,256]{2,0,1:T(8,128)(2,1)}, u32[]{:S(2)}, u32[]{:S(2)}) async-start(bf16[128,16,256]{2,0,1:T(8,128)(2,1)} %fusion.7), calls=%async_computation.4 | async-start | bytes 2097152 | tf_op jit(solution)/shard_map/all_to_all | solution.py:162
  227.9 1.3 copy.42
  229.2 22.3 %all-gather.8.cloned.1.call-done = bf16[2048,1280]{1,0:T(8,128)(2,1)} async-done(((bf16[128,1280]{1,0:T(8,128)(2,1)}), bf16[2048,1280]{1,0:T(8,128)(2,1)}) %all-gather.8.cloned.1.call-update) | async-done | bytes 5242896 | tf_op jit(solution)/shard_map/all_gather | solution.py:165
  251.5 2.6 fusion.19
  254.1 3.2 fusion.12
  257.4 0.9 pad.4
  258.3 6.8 %all-to-all-start.6 = ((bf16[48,7,8,128]{3,2,1,0:T(8,128)(2,1)}), bf16[48,7,8,128]{3,2,1,0:T(8,128)(2,1)S(1)}, u32[]{:S(2)}, u32[]{:S(2)}) async-start(bf16[48,7,8,128]{3,2,1,0:T(8,128)(2,1)} %bitcast.88), calls=%async_computation.6 | async-start | bytes 1376256 | tf_op jit(solution)/shard_map/all_to_all | solution.py:183
  265.1 5.1 %multiply_reduce_fusion = (f32[128]{0:T(128)S(1)}, f32[128,4096]{1,0:T(8,128)S(1)}) fusion(bf16[1,1,128,4096]{3,2,1,0:T(8,128)(2,1)S(1)} %copy-done, f32[128]{0:T(128)S(1)} %add_rsqrt_fusion, bf16[4096,768]{1,0:T(8,128)(2,1)} %all-gather.4.cloned.1.call-done, bf16[128,1280]{1,0:T(8,128)(2,1)S(1)} %copy-done.3), kind=kOutput, calls=%fused_computation.14 | convolution fusion | flops 807403392 | bytes 9634816 | tf_op jit(solution)/shard_map/dot_general | solution.py:25
  270.3 2.5 fusion.1
  272.8 1.6 fusion.24
  274.4 22.8 %all-to-all-done.6 = bf16[48,7,8,128]{3,2,1,0:T(8,128)(2,1)S(1)} async-done(((bf16[48,7,8,128]{3,2,1,0:T(8,128)(2,1)}), bf16[48,7,8,128]{3,2,1,0:T(8,128)(2,1)S(1)}, u32[]{:S(2)}, u32[]{:S(2)}) %all-to-all-start.6) | async-done | bytes 688160 | tf_op jit(solution)/shard_map/all_to_all | solution.py:183
  297.3 13.7 %all_gather.18 = bf16[28,8,128]{2,1,0:T(8,128)(2,1)S(1)} all-gather(bf16[7,8,128]{2,1,0:T(8,128)(2,1)S(1)} %reduce_sum.82), channel_id=1, replica_groups=mesh['z'=12,'yh'=4,'yl'=2,'x'=4,'core'=2] {'yh'}, dimensions={0}, use_global_device_ids=true | all-gather | bytes 71680 | tf_op jit(solution)/shard_map/all_gather | solution.py:195
  311.0 25.7 %all_gather.19 = bf16[336,8,128]{2,1,0:T(8,128)(2,1)S(1)} all-gather(bf16[28,8,128]{2,1,0:T(8,128)(2,1)S(1)} %all_gather.18), channel_id=1, replica_groups=mesh['z'=12,'yh'=4,'yl'=2,'x'=4,'core'=2] {'z'}, dimensions={0}, use_global_device_ids=true | all-gather | bytes 745472 | tf_op jit(solution)/shard_map/all_gather | solution.py:196
  336.8 0.9 slice.51
  337.7 0.9 slice.52
  (68 shorter events, 13.1 us)
Async XLA Ops:
  7.2 55.1 %copy-start.2 = (bf16[1,1,128,4096]{3,2,1,0:T(8,128)(2,1)S(1)}, bf16[1,1,128,4096]{3,2,1,0:T(8,128)(2,1)}, u32[]{:S(2)}) copy-start(bf16[1,1,128,4096]{3,2,1,0:T(8,128)(2,1)} %param.7) | copy-start | bytes 3145732
  7.2 55.1 %all-gather.6.cloned.1.call-start = ((), (), s32[]{:S(2)}) async-start(), calls=%async_computation.8 | async-start | bytes 4456448 | tf_op jit(solution)/shard_map/all_gather | solution.py:123
  7.9 111.3 %all-gather.4.cloned.1.call-start = ((), (), s32[]{:S(2)}) async-start(), calls=%async_computation.7 | async-start | bytes 6684672 | tf_op jit(solution)/shard_map/all_gather | solution.py:122
  12.1 54.1 %all-to-all-start = ((bf16[48,1,4]{2,1,0:T(2,128)(2,1)}), bf16[48,1,4]{2,1,0:T(2,128)(2,1)S(1)}, u32[]{:S(2)}, u32[]{:S(2)}) async-start(bf16[48,1,4]{2,1,0:T(2,128)(2,1)} %all_to_all.57), calls=%async_computation | async-start | bytes 49152 | tf_op jit(solution)/shard_map/all_to_all | solution.py:183
  37.2 82.1 %copy-start = (bf16[1,1,128,4096]{3,2,1,0:T(8,128)(2,1)S(1)}, bf16[1,1,128,4096]{3,2,1,0:T(8,128)(2,1)}, u32[]{:S(2)}) copy-start(bf16[1,1,128,4096]{3,2,1,0:T(8,128)(2,1)} %param.6) | copy-start | bytes 3145732
  66.1 58.0 %all-to-all-start.2 = ((bf16[48,4,512]{2,1,0:T(4,128)(2,1)}), bf16[48,4,512]{2,1,0:T(4,128)(2,1)S(1)}, u32[]{:S(2)}, u32[]{:S(2)}) async-start(bf16[48,4,512]{2,1,0:T(4,128)(2,1)} %reshape.218), calls=%async_computation.2 | async-start | bytes 393216 | tf_op jit(solution)/shard_map/all_to_all | solution.py:183
  124.1 34.3 %all-to-all-start.1 = ((bf16[48,4,768]{2,1,0:T(4,128)(2,1)}), bf16[48,4,768]{2,1,0:T(4,128)(2,1)S(1)}, u32[]{:S(2)}, u32[]{:S(2)}) async-start(bf16[48,4,768]{2,1,0:T(4,128)(2,1)} %reshape.215), calls=%async_computation.1 | async-start | bytes 589824 | tf_op jit(solution)/shard_map/all_to_all | solution.py:183
  138.5 113.0 %all-gather.8.cloned.1.call-start = ((), (), s32[]{:S(2)}) async-start(), calls=%async_computation.9 | async-start | bytes 5570560 | tf_op jit(solution)/shard_map/all_gather | solution.py:165
  194.8 28.6 %all-to-all-start.5 = ((bf16[128,16,256]{0,2,1:T(8,128)(2,1)}), bf16[128,16,256]{0,2,1:T(8,128)(2,1)S(1)}, u32[]{:S(2)}, u32[]{:S(2)}) async-start(bf16[128,16,256]{0,2,1:T(8,128)(2,1)} %bitcast.87), calls=%async_computation.5 | async-start | bytes 2097152 | tf_op jit(solution)/shard_map/all_to_all | solution.py:163
  223.4 30.8 %all-to-all-start.4 = ((bf16[128,16,256]{2,0,1:T(8,128)(2,1)}), bf16[128,16,256]{2,0,1:T(8,128)(2,1)}, u32[]{:S(2)}, u32[]{:S(2)}) async-start(bf16[128,16,256]{2,0,1:T(8,128)(2,1)} %fusion.7), calls=%async_computation.4 | async-start | bytes 2097152 | tf_op jit(solution)/shard_map/all_to_all | solution.py:162
  257.4 7.8 %copy-start.3 = (bf16[128,1280]{1,0:T(8,128)(2,1)S(1)}, bf16[128,1280]{1,0:T(8,128)(2,1)}, u32[]{:S(2)}) copy-start(bf16[128,1280]{1,0:T(8,128)(2,1)} %convolution_convert_fusion) | copy-start | bytes 983044
  258.3 38.8 %all-to-all-start.6 = ((bf16[48,7,8,128]{3,2,1,0:T(8,128)(2,1)}), bf16[48,7,8,128]{3,2,1,0:T(8,128)(2,1)S(1)}, u32[]{:S(2)}, u32[]{:S(2)}) async-start(bf16[48,7,8,128]{3,2,1,0:T(8,128)(2,1)} %bitcast.88), calls=%async_computation.6 | async-start | bytes 1376256 | tf_op jit(solution)/shard_map/all_to_all | solution.py:183
  265.1 5.2 %copy-start.1 = (bf16[4096,512]{1,0:T(8,128)(2,1)S(1)}, bf16[4096,512]{1,0:T(8,128)(2,1)}, u32[]{:S(2)}) copy-start(bf16[4096,512]{1,0:T(8,128)(2,1)} %all-gather.6.cloned.1.call-done) | copy-start | bytes 12582916
Sparse Core Ops, SparseCore 0:
  10.4 51.8 all-gather.5
  64.7 54.4 all-gather.3
  193.6 57.8 all-gather.7

commit v2 on v1

v2 whole, which is shorter than its diff:
```python
import functools

import jax
import jax.numpy as jnp
from jax import lax
from jax.experimental import pallas as pl
from jax.experimental.pallas import tpu as pltpu
from jax.sharding import Mesh
from jax.sharding import PartitionSpec as P


QH = 4
DP = ("z", "yh")
FINE = (12, 4, 2, 4, 2)
FSDP = ("yl", "x", "core")


def prepare_kernel(places, tokens, cot, normed, keep, send):
    width = tokens.shape[1]
    share = keep.shape[3] // 2
    values = tokens[...].astype(jnp.float32)
    squares = jnp.sum(values * values, axis=-1, keepdims=True)
    normed[...] = (values * lax.rsqrt(squares / width + 1e-05)).astype(jnp.bfloat16)
    number = 0
    for out in (keep, send):
        for dy in range(out.shape[0]):
            for dx in range(out.shape[1]):
                columns = pl.ds(pl.multiple_of(places[number] * share, 128), share)
                out[dy, dx, :, :share] = normed[:, columns]
                out[dy, dx, :, share:] = cot[:, columns]
                number += 1


def contract_rows(left, right):
    return lax.dot_general(
        left, right, (((0,), (0,)), ((), ())), preferred_element_type=jnp.float32
    )


def contract_cols(left, right):
    return lax.dot_general(
        left, right, (((1,), (1,)), ((), ())), preferred_element_type=jnp.float32
    )


def attention_kernel(heads, length, place_col, place_row, got, out):
    size = got.shape[1] // (2 * heads + 3)
    wide = heads * size
    keys = got[:, wide : wide + size]
    values = got[:, wide + size : wide + 2 * size]
    flags = got[:, 2 * wide + 2 * size :].astype(jnp.float32)
    at_col, at_row = (place_col[...], place_row[...])
    live_col, live_row = (at_col < length[0], at_row < length[0])
    begin_col = (flags[:, :1] > 0) & live_col & (at_col > 0)
    begin_row = (flags.T[:1, :] > 0) & live_row & (at_row > 0)
    before = at_row <= at_col
    after = at_col <= at_row
    count_col = jnp.sum(jnp.where(before & begin_row, 1.0, 0.0), axis=1, keepdims=True)
    count_row = jnp.sum(jnp.where(after & begin_col, 1.0, 0.0), axis=0, keepdims=True)
    allowed = (before & (count_col == count_row) & live_col & live_row) | (at_row == at_col)
    scale = size ** (-0.5)
    grad_keys, grad_values = (0.0, 0.0)
    for head in range(heads):
        columns = slice(head * size, (head + 1) * size)
        queries = got[:, columns]
        grads = got[:, wide + 2 * size + head * size : wide + 2 * size + (head + 1) * size]
        scores = jnp.where(allowed, contract_cols(queries, keys) * scale, -1e30)
        exponent = jnp.exp(scores - jnp.max(scores, axis=-1, keepdims=True))
        weights = exponent / jnp.sum(exponent, axis=-1, keepdims=True)
        weights_b = weights.astype(jnp.bfloat16)
        attended = jnp.dot(weights_b, values, preferred_element_type=jnp.float32)
        attended = attended.astype(jnp.bfloat16)
        delta = jnp.sum(
            grads.astype(jnp.float32) * attended.astype(jnp.float32), axis=-1, keepdims=True
        )
        grad_scores = weights * (contract_cols(grads, values) - delta) * scale
        grad_scores = grad_scores.astype(jnp.bfloat16)
        out[:, columns] = jnp.dot(
            grad_scores, keys, preferred_element_type=jnp.float32
        ).astype(jnp.bfloat16)
        grad_keys += contract_rows(grad_scores, queries)
        grad_values += contract_rows(weights_b, grads)
        shifted = slice(wide + 2 * size + head * size, wide + 2 * size + (head + 1) * size)
        out[:, shifted] = attended
    out[:, wide : wide + size] = grad_keys.astype(jnp.bfloat16)
    out[:, wide + size : wide + 2 * size] = grad_values.astype(jnp.bfloat16)


def spread_kernel(split, whole, first, second):
    share = first.shape[0]
    for at in range(0, first.shape[1] + second.shape[1], 128):
        piece = whole[at // 128 * share : at // 128 * share + share, :].astype(jnp.float32)
        if at < split:
            first[:, at : at + 128] = piece
        else:
            second[:, at - split : at - split + 128] = piece


def shift_x(array, step):
    size = lax.axis_size("x")
    return lax.ppermute(array, "x", [(i, (i + step) % size) for i in range(size)])


def shift_y(array, step):
    size = lax.axis_size(("yh", "yl"))
    return lax.ppermute(array, ("yh", "yl"), [(i, (i + step) % size) for i in range(size)])


def swap_y(array):
    return lax.ppermute(array, "yl", [(0, 1), (1, 0)])


def swap_core(array):
    return lax.ppermute(array, "core", [(0, 1), (1, 0)])


def place(dx, dy, dc):
    yl = (lax.axis_index("yl") + dy) % 2
    x = (lax.axis_index("x") + dx) % lax.axis_size("x")
    core = (lax.axis_index("core") + dc) % 2
    return ((yl * lax.axis_size("x") + x) * 2 + core).astype(jnp.int32)


def label_blocks(groups):
    arrays, pieces, places = [], [], []
    for dc, array, parts in groups:
        row = 0
        for dx, dy, sub, rows in parts:
            pieces.append((len(arrays), row, sub, rows))
            places.append((dx % 4, dy, dc))
            row += rows
        arrays.append(array)
    return (arrays, pieces, places)


def place_all(offsets):
    return jnp.stack([place(*offset) for offset in offsets])


def spread_cols(keep, send):
    other = swap_core(send)
    across_0 = swap_y(keep[1])
    across_1 = swap_y(other[1])
    return (keep[0], other[0], across_0, across_1)


def spread_cols_x(here):
    quads = [[part[dx] for part in here] for dx in range(4)]
    up = jnp.stack(quads[1] + quads[2][:2])
    down = jnp.stack(quads[3] + quads[2][2:])
    up = shift_x(up, 1)
    down = shift_x(down, -1)
    far_up = shift_x(up[4:], 1)
    far_down = shift_x(down[4:], -1)
    sources = [(0, 0), (0, 1), (1, 0), (1, 1)]
    arrays = [*here, up, down, far_up, far_down]
    pieces = [(number, 0, (0, *source)) for number, source in enumerate(sources)]
    pieces += [(4, number, (3, *source)) for number, source in enumerate(sources)]
    pieces += [(5, number, (1, *source)) for number, source in enumerate(sources)]
    pieces += [(6, number, (2, *source)) for number, source in enumerate(sources[:2])]
    pieces += [(7, number, (2, *source)) for number, source in enumerate(sources[2:])]
    return (arrays, pieces)


def gather_weights(block, beside):
    half = block.shape[0] // 2
    full = 2 * half
    left = shift_x(block, 1)
    right = shift_x(block, -1)
    across_a = shift_y(block[:half], 1)
    across_b = shift_y(block[half:], -1)
    other_0 = swap_core(block)
    left, right, across_a, across_b, other_0, beside = lax.optimization_barrier(
        (left, right, across_a, across_b, other_0, beside)
    )
    left_y = shift_y(left, 1)
    right_y = shift_y(right, -1)
    far_a = shift_x(left[:half], 1)
    far_b = shift_x(right[half:], -1)
    other_1 = swap_core(jnp.concatenate([left, right, across_a, across_b], axis=0))
    far_y_a = shift_y(far_a, 1)
    far_y_b = shift_y(far_b, -1)
    other_2 = swap_core(jnp.concatenate([left_y, right_y, far_a, far_b], axis=0))
    other_3 = swap_core(jnp.concatenate([far_y_a, far_y_b], axis=0))
    parts_1 = [(-1, 0, 0, full), (1, 0, 0, full), (0, 1, 0, half), (0, 1, half, half)]
    parts_2 = [(-1, 1, 0, full), (1, 1, 0, full), (2, 0, 0, half), (2, 0, half, half)]
    parts_3 = [(2, 1, 0, half), (2, 1, half, half)]
    mine = [block, left, right, across_a, across_b, left_y, right_y, far_a, far_b]
    mine += [far_y_a, far_y_b]
    own_parts = [(0, 0, 0, full)] + parts_1 + parts_2 + parts_3
    groups = [(0, array, [part]) for array, part in zip(mine, own_parts)]
    groups += [
        (1, other_0, [(0, 0, 0, full)]),
        (1, other_1, parts_1),
        (1, other_2, parts_2),
        (1, other_3, parts_3),
    ]
    return (*label_blocks(groups), beside)


def gather_rows(block):
    half = block.shape[0] // 2
    full = 2 * half
    left = shift_x(block, 1)
    right = shift_x(block, -1)
    across = swap_y(block)
    other_0 = swap_core(block)
    right_y = swap_y(right)
    left_y = shift_x(across, 1)
    far = shift_x(right, -1)
    other_1 = swap_core(jnp.concatenate([left, right, across], axis=0))
    far_y_a = swap_y(far[:half])
    far_y_b = shift_x(left_y[half:], 1)
    other_2 = swap_core(jnp.concatenate([right_y, left_y, far], axis=0))
    other_3 = swap_core(jnp.concatenate([far_y_a, far_y_b], axis=0))
    parts_1 = [(-1, 0, 0, full), (1, 0, 0, full), (0, 1, 0, full)]
    parts_2 = [(1, 1, 0, full), (-1, 1, 0, full), (2, 0, 0, full)]
    parts_3 = [(2, 1, 0, half), (2, 1, half, half)]
    mine = [block, left, right, across, right_y, left_y, far, far_y_a, far_y_b]
    own_parts = [(0, 0, 0, full)] + parts_1 + parts_2 + parts_3
    groups = [(0, array, [part]) for array, part in zip(mine, own_parts)]
    groups += [
        (1, other_0, [(0, 0, 0, full)]),
        (1, other_1, parts_1),
        (1, other_2, parts_2),
        (1, other_3, parts_3),
    ]
    return label_blocks(groups)


def project_kernel(pieces, share, split, places, normed, cot, routing, flags, *refs):
    blocks, (out, total) = (refs[:-2], refs[-2:])
    for number, (which, row, sub, rows) in enumerate(pieces):
        columns = pl.ds(pl.multiple_of(places[number] * share + sub, 128), rows)
        first = jnp.dot(
            normed[:, columns],
            blocks[which][row : row + rows, :split],
            preferred_element_type=jnp.float32,
        )
        second = jnp.dot(
            cot[:, columns],
            blocks[which][row : row + rows, split:],
            preferred_element_type=jnp.float32,
        )
        if number == 0:
            total[:, :split] = first
            total[:, split:] = second
        else:
            total[:, :split] += first
            total[:, split:] += second
    width = total.shape[1]
    out[:, :width] = jnp.dot(
        routing[...], total[...].astype(jnp.bfloat16), preferred_element_type=jnp.float32
    ).astype(jnp.bfloat16)
    out[:, width:] = jnp.dot(
        routing[...], flags[...], preferred_element_type=jnp.float32
    ).astype(jnp.bfloat16)


def finish_kernel(pieces, share, split, places, both, tokens, cot, *refs):
    blocks, (result, grad, back) = (refs[:-3], refs[-3:])
    grad_rows = both[:, :split]
    attended = both[:, split:]
    rows_cols = (((1,), (1,)), ((), ()))
    for number, (which, row, sub, rows) in enumerate(pieces):
        columns = pl.ds(pl.multiple_of(places[number] * share + sub, 128), rows)
        back[:, columns] = lax.dot_general(
            grad_rows,
            blocks[which][row : row + rows, :split],
            rows_cols,
            preferred_element_type=jnp.float32,
        )
        added = lax.dot_general(
            attended,
            blocks[which][row : row + rows, split:],
            rows_cols,
            preferred_element_type=jnp.float32,
        )
        result[:, columns] = (tokens[:, columns].astype(jnp.float32) + added).astype(jnp.bfloat16)
    width = tokens.shape[1]
    values = tokens[...].astype(jnp.float32)
    squares = jnp.sum(values * values, axis=-1, keepdims=True)
    inverse = lax.rsqrt(squares / width + 1e-05)
    normed = values * inverse
    correction = jnp.sum(back[...] * normed, axis=-1, keepdims=True) / width
    grad[...] = (
        cot[...].astype(jnp.float32) + inverse * (back[...] - normed * correction)
    ).astype(jnp.bfloat16)


def weight_grad_kernel(row_pieces, col_pieces, split, *refs):
    inputs, (out, rows_all, cols_all) = (refs[:-3], refs[-3:])
    col_count = 1 + max(which for which, _, _ in col_pieces)
    share = cols_all.shape[1] // 2
    count = inputs[0].shape[1]
    for which, index, to in col_pieces:
        cols_all[to : to + count, :] = inputs[which][index]
    for which, row, to, rows in row_pieces:
        rows_all[to : to + rows, :] = inputs[col_count + which][row : row + rows, :]
    first = contract_rows(cols_all[:, :share], rows_all[:, :split]).astype(jnp.bfloat16)
    second = contract_rows(cols_all[:, share:], rows_all[:, split:]).astype(jnp.bfloat16)
    step = 128
    width = rows_all.shape[1]
    for at in range(0, width, step):
        piece = first[:, at : at + step] if at < split else second[:, at - split : at - split + step]
        out[at // step * share : at // step * share + share, :] = piece
    filled = width // step * share
    if filled < out.shape[0]:
        out[filled:, :] = jnp.zeros((out.shape[0] - filled, step), jnp.bfloat16)


def call(kernel, places, operands, out_shape, scratch, flops, read):
    vmem = pl.BlockSpec(memory_space=pltpu.VMEM)
    smem = [] if places is None else [pl.BlockSpec(memory_space=pltpu.SMEM)]
    return pl.pallas_call(
        kernel,
        out_shape=out_shape,
        in_specs=smem + [vmem] * len(operands),
        out_specs=jax.tree.map(lambda _: vmem, out_shape),
        scratch_shapes=scratch,
        cost_estimate=pl.CostEstimate(flops=flops, bytes_accessed=read, transcendentals=0),
    )(*([] if places is None else [places]), *operands)


def on_device(tokens, grad_out, qkv_weight, out_weight, range_len, doc_start):
    token_rows = tokens[0, 0]
    cot_rows = grad_out[0, 0]
    flag_rows = doc_start[0, 0].astype(jnp.bfloat16)
    lengths = range_len[0]
    row_count = token_rows.shape[0]
    model_width = token_rows.shape[1]
    qkv_width = qkv_weight.shape[1]
    out_width = out_weight.shape[1]
    groups = lax.axis_size(DP)
    owners = lax.axis_size(FSDP)
    my_index = lax.axis_index(DP)
    slot_count = 3 * row_count // 2 // groups
    total_slots = groups * slot_count
    range_end = jnp.cumsum(lengths, dtype=jnp.int32)
    starts = range_end - lengths
    pack_row = my_index + groups * jnp.arange(row_count, dtype=jnp.int32)
    target = jnp.sum(
        (range_end[None, :] <= pack_row[:, None]).astype(jnp.int32), axis=1, dtype=jnp.int32
    )
    range_ids = jnp.arange(groups, dtype=jnp.int32)
    range_first = jnp.sum(
        jnp.where(range_ids[None, :] == target[:, None], starts[None, :], 0),
        axis=1,
        dtype=jnp.int32,
    )
    flat_slot = target * slot_count + (pack_row - range_first) // groups
    routing = (jnp.arange(total_slots, dtype=jnp.int32)[:, None] == flat_slot[None, :]).astype(
        jnp.bfloat16
    )

    def from_slots(array):
        return contract_rows(routing, array.reshape(total_slots, -1)).astype(jnp.bfloat16)

    width = qkv_width + out_width
    share = model_width // owners
    order = [(dx, dy, dc) for dc in range(2) for dy in range(2) for dx in range(4)]
    piece = jax.ShapeDtypeStruct((2, 4, row_count, 2 * share), jnp.bfloat16)
    normed_b, keep, send = call(
        prepare_kernel,
        place_all(order),
        [token_rows, cot_rows],
        [jax.ShapeDtypeStruct((row_count, model_width), jnp.bfloat16), piece, piece],
        [],
        4 * row_count * model_width,
        10 * row_count * model_width,
    )
    flag_cols = jnp.broadcast_to(flag_rows[:, None], (row_count, 128))
    my_start = starts[my_index]
    my_length = lengths[my_index]
    source_ids = jnp.arange(groups, dtype=jnp.int32)[:, None]
    slot_ids = jnp.arange(slot_count, dtype=jnp.int32)[None, :]
    position = ((source_ids - my_start) % groups + groups * slot_ids).reshape(total_slots)
    blocks, pieces, offsets, beside = gather_weights(
        jnp.concatenate([qkv_weight, out_weight], axis=1),
        (normed_b, keep, send, flag_cols, routing, position),
    )
    normed_b, keep, send, flag_cols, routing, position = beside
    places = place_all(offsets)
    slots = call(
        functools.partial(project_kernel, pieces, share, qkv_width),
        places,
        [normed_b, cot_rows, routing, flag_cols, *blocks],
        jax.ShapeDtypeStruct((total_slots, width + 128), jnp.bfloat16),
        [pltpu.VMEM((row_count, width), jnp.float32)],
        2 * row_count * model_width * width,
        2 * model_width * width,
    )
    slots, keep, send = lax.optimization_barrier((slots, keep, send))
    got = swap_dp(slots.reshape(groups, slot_count, width + 128))
    here = spread_cols(keep, send)
    got = got.reshape(total_slots, width + 128)
    both = call(
        functools.partial(attention_kernel, QH),
        my_length[None],
        [position[:, None], position[None, :], got],
        jax.ShapeDtypeStruct((total_slots, width), jnp.bfloat16),
        [],
        18 * total_slots * total_slots * out_width,
        4 * total_slots * width,
    )
    both, here = lax.optimization_barrier((both, here))
    back = swap_dp(both.reshape(groups, slot_count, width))
    cols, col_pieces = spread_cols_x(here)
    back, cols = lax.optimization_barrier((back, cols))
    both_rows = from_slots(back)
    row_blocks, row_pieces, row_offsets = gather_rows(both_rows)
    at = {offset: number * row_count for number, offset in enumerate(order)}
    row_pieces = [
        (which, row, at[offset] + sub, rows)
        for (which, row, sub, rows), offset in zip(row_pieces, row_offsets)
    ]
    col_pieces = [(which, index, at[offset]) for which, index, offset in col_pieces]
    each = -(-share * width // (128 * 8 * groups)) * 8
    partial = call(
        functools.partial(weight_grad_kernel, row_pieces, col_pieces, qkv_width),
        None,
        [*cols, *row_blocks],
        jax.ShapeDtypeStruct((groups * each, 128), jnp.bfloat16),
        [
            pltpu.VMEM((owners * row_count, width), jnp.bfloat16),
            pltpu.VMEM((owners * row_count, 2 * share), jnp.bfloat16),
        ],
        2 * owners * row_count * width * share,
        2 * owners * row_count * (width + 2 * share),
    )
    partial, both_late = lax.optimization_barrier((partial, both_rows))
    summed = sum_over_dp(partial.reshape(groups, each, 128))
    result, tokens_grad = call(
        functools.partial(finish_kernel, pieces, share, qkv_width),
        places,
        [both_late, token_rows, cot_rows, *blocks],
        [jax.ShapeDtypeStruct((row_count, model_width), jnp.bfloat16)] * 2,
        [pltpu.VMEM((row_count, model_width), jnp.float32)],
        2 * row_count * model_width * width,
        2 * model_width * width,
    )

    qkv_grad, out_grad = call(
        functools.partial(spread_kernel, qkv_width),
        None,
        [summed],
        [
            jax.ShapeDtypeStruct((share, qkv_width), jnp.float32),
            jax.ShapeDtypeStruct((share, out_width), jnp.float32),
        ],
        [],
        share * width,
        6 * share * width,
    )
    return (result[None, None], tokens_grad[None, None], qkv_grad, out_grad)


def swap_dp(array):
    return lax.all_to_all(array, DP, split_axis=0, concat_axis=0, tiled=True)


def sum_over_dp(partial):
    groups, each, lanes = partial.shape
    rows, cols = (lax.axis_size("z"), lax.axis_size("yh"))
    ordered = jnp.swapaxes(partial.reshape(cols, rows, each, lanes), 0, 1)
    got = swap_dp(ordered.reshape(groups, each, lanes))
    mine = jnp.sum(got.astype(jnp.float32), axis=0).astype(jnp.bfloat16)
    whole = lax.all_gather(mine, "z", axis=0, tiled=True)
    return lax.all_gather(whole, "yh", axis=0, tiled=True)


def solution(mesh):
    fine = Mesh(mesh.devices.reshape(FINE), DP + FSDP)
    return jax.shard_map(
        on_device,
        mesh=fine,
        in_specs=(
            P(FSDP, DP, None, None),
            P(FSDP, DP, None, None),
            P(FSDP, None),
            P(FSDP, None),
            P(FSDP, None),
            P(FSDP, DP, None),
        ),
        out_specs=(
            P(FSDP, DP, None, None),
            P(FSDP, DP, None, None),
            P(FSDP, None),
            P(FSDP, None),
        ),
        check_vma=False,
    )
```

time: 346 us -> 357 us (1.032)
  the two profiles are of different devices: /device:TPU:16 before, /device:TPU:24 now
where the time goes in v2:
time: 357 us; the launch traced here: 355 us
  starting transfers between devices  129 us (36%)
  blocking collectives  87.3 us (24%)
  waiting for transfers between devices  69.6 us (19%)
  Pallas kernels  35.6 us (10%)
  local copies, waits for them, and re-layouts  24.8 us (7%)
  other arithmetic  6.94 us (2%)
    all_to_all x1, blocking collectives, swap_dp(): return lax.all_to_all(array, DP, split_axis=0, concat_axis=0, tiled=True)  46.6 us
    ppermute x13, starting transfers between devices, shift_x(): lax.ppermute(array, 'x', [(i, (i + step) % size) for i in range(size)])  44 us
    pallas_call x6, Pallas kernels, call(): pl.pallas_call(kernel, out_shape=out_shape, in_specs=smem + [vmem] * len(...  35.6 us
    all_to_all x2, starting transfers between devices, swap_dp(): return lax.all_to_all(array, DP, split_axis=0, concat_axis=0, tiled=True)  31.8 us
    ppermute x13, waiting for transfers between devices, shift_x(): lax.ppermute(array, 'x', [(i, (i + step) % size) for i in range(size)])  30.8 us
    all_gather x1, blocking collectives, sum_over_dp(): whole = lax.all_gather(mine, 'z', axis=0, tiled=True)  22.4 us
    ppermute x6, starting transfers between devices, shift_y(): lax.ppermute(array, ('yh', 'yl'), [(i, (i + step) % size) for i in range(...  21.2 us
    all_gather x1, blocking collectives, sum_over_dp(): return lax.all_gather(whole, 'yh', axis=0, tiled=True)  18.2 us
  transfers between devices with their start and end apart: 35, of which 17 were waited for; matrix products, arithmetic and copies ran while one was open for 6% of the time, Pallas kernels for 3%

profile of v2, /device:TPU:24, one launch (start us, length us, event | category | flops | bytes accessed | tf_op | source)
XLA Modules:
  0.0 355.3 jit_solution(4661742320398264955)
XLA Ops:
  2.7 3.4 collective-permute-start
  6.1 3.7 %collective-permute-start.1 = (bf16[256,1280]{1,0:T(8,128)(2,1)S(1)}, bf16[256,1280]{1,0:T(8,128)(2,1)S(1)}, u32[]{:S(2)}, u32[]{:S(2)}) collective-permute-start(bf16[256,1280]{1,0:T(8,128)(2,1)S(1)} %constant_dynamic-update-slice_fusion.refs_0_), channel_id=1, source_target_pairs={{0,6},{2,0},{4,2},{6,4},{1,7},{3,1},{5,3},{7,5},{8,14},{10,8},{12,... | collective-permute-start | bytes 1966088 | tf_op jit(solution)/shard_map/ppermute | solution.py:101
  11.7 4.7 %collective-permute-start.2 = (bf16[128,1280]{1,0:T(8,128)(2,1)S(1)}, bf16[128,1280]{1,0:T(8,128)(2,1)}, u32[]{:S(2)}, u32[]{:S(2)}) collective-permute-start(bf16[128,1280]{1,0:T(8,128)(2,1)S(1)} %get-tuple-element.83), channel_id=1, source_target_pairs={{0,8},{8,16},{16,24},{24,32},{32,40},{40,48},{48,56},{56,0},{1,9},... | collective-permute-start | bytes 983048 | tf_op jit(solution)/shard_map/ppermute | solution.py:106
  21.1 3.8 %shard_map.93 = (bf16[128,4096]{1,0:T(8,128)(2,1)}, bf16[2,4,128,512]{3,2,1,0:T(8,128)(2,1)}, bf16[2,4,128,512]{3,2,1,0:T(8,128)(2,1)}) custom-call(s32[16]{0:T(128)} %stack.99.places, bf16[128,4096]{1,0:T(8,128)(2,1)} %bitcast.52, bf16[128,4096]{1,0:T(8,128)(2,1)} %bitcast.49), custom_call_target="tpu_custom_call" | custom-call | flops 2097152 | bytes 5242880 | tf_op jit(solution)/shard_map/pallas_call | solution.py:315
  25.5 4.0 %collective-permute-done.3.refs_4_ = bf16[128,1280]{1,0:T(8,128)(2,1)} collective-permute-done((bf16[128,1280]{1,0:T(8,128)(2,1)S(1)}, bf16[128,1280]{1,0:T(8,128)(2,1)}, u32[]{:S(2)}, u32[]{:S(2)}) %collective-permute-start.3) | collective-permute-done | bytes 327712 | tf_op jit(solution)/shard_map/ppermute | solution.py:106
  33.0 3.9 %collective-permute-start.6 = (bf16[256,1280]{1,0:T(8,128)(2,1)S(1)}, bf16[256,1280]{1,0:T(8,128)(2,1)S(1)}, u32[]{:S(2)}, u32[]{:S(2)}) collective-permute-start(bf16[256,1280]{1,0:T(8,128)(2,1)S(1)} %collective-permute-done.1.refs_2_), channel_id=1, source_target_pairs={{0,56},{8,0},{16,8},{24,16},{32,24},{40,32},{48,40},{56,48},{1,57}... | collective-permute-start | bytes 1966088 | tf_op jit(solution)/shard_map/ppermute | solution.py:106
  37.0 3.5 collective-permute-start.8
  47.3 4.4 %collective-permute-done.7.refs_7_ = bf16[128,1280]{1,0:T(8,128)(2,1)S(1)} collective-permute-done((bf16[128,1280]{1,0:T(8,128)(2,1)S(1)}, bf16[128,1280]{1,0:T(8,128)(2,1)S(1)}, u32[]{:S(2)}, u32[]{:S(2)}) %collective-permute-start.7) | collective-permute-done | bytes 327712 | tf_op jit(solution)/shard_map/ppermute | solution.py:101
  55.5 3.0 collective-permute-start.10
  58.5 5.7 %collective-permute-start.9 = (bf16[128,1280]{1,0:T(8,128)(2,1)S(1)}, bf16[128,1280]{1,0:T(8,128)(2,1)S(1)}, u32[]{:S(2)}, u32[]{:S(2)}) collective-permute-start(bf16[128,1280]{1,0:T(8,128)(2,1)S(1)} %collective-permute-done.7.refs_7_), channel_id=1, source_target_pairs={{0,8},{8,16},{16,24},{24,32},{32,40},{40,48},{48,56},{56,0},{1,9},... | collective-permute-start | bytes 983048 | tf_op jit(solution)/shard_map/ppermute | solution.py:106
  64.2 6.4 %collective-permute-done.10.refs_10_ = bf16[128,1280]{1,0:T(8,128)(2,1)S(1)} collective-permute-done((bf16[128,1280]{1,0:T(8,128)(2,1)S(1)}, bf16[128,1280]{1,0:T(8,128)(2,1)S(1)}, u32[]{:S(2)}, u32[]{:S(2)}) %collective-permute-start.10) | collective-permute-done | bytes 327712 | tf_op jit(solution)/shard_map/ppermute | solution.py:106
  78.4 8.0 %shard_map.94 = bf16[192,1408]{1,0:T(8,128)(2,1)} custom-call(s32[22]{0:T(128)} %stack.98.places, bf16[128,4096]{1,0:T(8,128)(2,1)} %get-tuple-element.45.normed, bf16[128,4096]{1,0:T(8,128)(2,1)} %bitcast.50, bf16[192,128]{1,0:T(8,128)(2,1)} %fusion.routing, bf16[128,128]{1,0:T(8,128)(2,1)} %broadcast_in_dim.24.flags, bf16[256,1280]{1,0:T(8,128)(2,1)} %copy-done, ...), custom_call_target="tpu_custom_call" | custom-call | flops 1342177280 | bytes 10485760 | tf_op jit(solution)/shard_map/pallas_call | solution.py:315
  90.5 17.6 %all-to-all-start = ((bf16[48,4,1408]{2,1,0:T(4,128)(2,1)}), bf16[48,4,1408]{2,1,0:T(4,128)(2,1)S(1)}, u32[]{:S(2)}, u32[]{:S(2)}) async-start(bf16[48,4,1408]{2,1,0:T(4,128)(2,1)} %reshape.94), calls=%async_computation | async-start | bytes 1081344 | tf_op jit(solution)/shard_map/all_to_all | solution.py:459
  108.2 4.8 %collective-permute-start.15 = (bf16[4,128,512]{2,1,0:T(8,128)(2,1)S(1)}, bf16[4,128,512]{2,1,0:T(8,128)(2,1)S(1)}, u32[]{:S(2)}, u32[]{:S(2)}) collective-permute-start(bf16[4,128,512]{2,1,0:T(8,128)(2,1)S(1)} %get-tuple-element.80), channel_id=1, source_target_pairs={{0,8},{8,0},{1,9},{9,1},{2,10},{10,2},{3,11},{11,3},{4,12},{12,4},... | collective-permute-start | bytes 1572872 | tf_op jit(solution)/shard_map/ppermute | solution.py:110
  118.5 17.3 %all-to-all-done = bf16[48,4,1408]{2,1,0:T(4,128)(2,1)S(1)} async-done(((bf16[48,4,1408]{2,1,0:T(4,128)(2,1)}), bf16[48,4,1408]{2,1,0:T(4,128)(2,1)S(1)}, u32[]{:S(2)}, u32[]{:S(2)}) %all-to-all-start) | async-done | bytes 540704 | tf_op jit(solution)/shard_map/all_to_all | solution.py:459
  136.7 5.5 %shard_map.95 = bf16[192,1280]{1,0:T(8,128)(2,1)} custom-call(s32[1]{0:T(128)} %bitcast.16.length, s32[192,1]{1,0:T(8,128)} %copy.15.place_col, s32[1,192]{1,0:T(1,128)} %bitcast.57, bf16[192,1408]{1,0:T(8,128)(2,1)} %reshape.95.got), custom_call_target="tpu_custom_call" | custom-call | flops 339738624 | bytes 983040 | tf_op jit(solution)/shard_map/pallas_call | solution.py:315
  142.3 4.0 %collective-permute-done.16.refs_3_ = bf16[4,128,512]{2,1,0:T(8,128)(2,1)S(1)} collective-permute-done((bf16[4,128,512]{2,1,0:T(8,128)(2,1)}, bf16[4,128,512]{2,1,0:T(8,128)(2,1)S(1)}, u32[]{:S(2)}, u32[]{:S(2)}) %collective-permute-start.16) | collective-permute-done | bytes 524320 | tf_op jit(solution)/shard_map/ppermute | solution.py:110
  149.0 14.3 %all-to-all-start.1 = ((bf16[48,4,1280]{2,1,0:T(4,128)(2,1)}), bf16[48,4,1280]{2,1,0:T(4,128)(2,1)S(1)}, u32[]{:S(2)}, u32[]{:S(2)}) async-start(bf16[48,4,1280]{2,1,0:T(4,128)(2,1)} %reshape.96), calls=%async_computation.1 | async-start | bytes 983040 | tf_op jit(solution)/shard_map/all_to_all | solution.py:459
  170.2 4.9 %collective-permute-start.18 = (bf16[6,128,512]{2,1,0:T(8,128)(2,1)}, bf16[6,128,512]{2,1,0:T(8,128)(2,1)S(1)}, u32[]{:S(2)}, u32[]{:S(2)}) collective-permute-start(bf16[6,128,512]{2,1,0:T(8,128)(2,1)} %get-tuple-element.84), channel_id=1, source_target_pairs={{0,6},{2,0},{4,2},{6,4},{1,7},{3,1},{5,3},{7,5},{8,14},{10,8},{12,... | collective-permute-start | bytes 2359304 | tf_op jit(solution)/shard_map/ppermute | solution.py:101
  175.1 15.1 %collective-permute-done.17.refs_4_ = bf16[6,128,512]{2,1,0:T(8,128)(2,1)S(1)} collective-permute-done((bf16[6,128,512]{2,1,0:T(8,128)(2,1)}, bf16[6,128,512]{2,1,0:T(8,128)(2,1)S(1)}, u32[]{:S(2)}, u32[]{:S(2)}) %collective-permute-start.17) | collective-permute-done | bytes 786464 | tf_op jit(solution)/shard_map/ppermute | solution.py:101
  192.3 5.1 %collective-permute-start.20 = (bf16[2,128,512]{2,1,0:T(8,128)(2,1)S(1)}, bf16[2,128,512]{2,1,0:T(8,128)(2,1)}, u32[]{:S(2)}, u32[]{:S(2)}) collective-permute-start(bf16[2,128,512]{2,1,0:T(8,128)(2,1)S(1)} %slice.101), channel_id=1, source_target_pairs={{0,6},{2,0},{4,2},{6,4},{1,7},{3,1},{5,3},{7,5},{8,14},{10,8},{12,... | collective-permute-start | bytes 786440 | tf_op jit(solution)/shard_map/ppermute | solution.py:101
  197.4 2.8 collective-permute-done.19.refs_6_
  201.9 5.7 %collective-permute-start.22 = (bf16[128,1280]{1,0:T(8,128)(2,1)S(1)}, bf16[128,1280]{1,0:T(8,128)(2,1)S(1)}, u32[]{:S(2)}, u32[]{:S(2)}) collective-permute-start(bf16[128,1280]{1,0:T(8,128)(2,1)S(1)} %convolution_convert_fusion.refs_8_.both), channel_id=1, source_target_pairs={{0,6},{2,0},{4,2},{6,4},{1,7},{3,1},{5,3},{7,5},{8,14},{10,8},{12,... | collective-permute-start | bytes 983048 | tf_op jit(solution)/shard_map/ppermute | solution.py:101
  212.2 5.6 %collective-permute-start.26 = (bf16[128,1280]{1,0:T(8,128)(2,1)S(1)}, bf16[128,1280]{1,0:T(8,128)(2,1)S(1)}, u32[]{:S(2)}, u32[]{:S(2)}) collective-permute-start(bf16[128,1280]{1,0:T(8,128)(2,1)S(1)} %collective-permute-done.22.refs_10_), channel_id=1, source_target_pairs={{0,6},{2,0},{4,2},{6,4},{1,7},{3,1},{5,3},{7,5},{8,14},{10,8},{12,... | collective-permute-start | bytes 983048 | tf_op jit(solution)/shard_map/ppermute | solution.py:101
  219.7 2.9 collective-permute-start.24
  224.7 3.2 collective-permute-done.25.refs_13_
  239.2 4.0 %collective-permute-done.28.refs_16_ = bf16[64,1280]{1,0:T(8,128)(2,1)S(1)} collective-permute-done((bf16[64,1280]{1,0:T(8,128)(2,1)S(1)}, bf16[64,1280]{1,0:T(8,128)(2,1)S(1)}, u32[]{:S(2)}, u32[]{:S(2)}) %collective-permute-start.28) | collective-permute-done | bytes 163872 | tf_op jit(solution)/shard_map/ppermute | solution.py:101
  248.5 6.1 %shard_map.96 = bf16[2688,128]{1,0:T(8,128)(2,1)} custom-call(bf16[4,128,512]{2,1,0:T(8,128)(2,1)} %copy-done.6, bf16[4,128,512]{2,1,0:T(8,128)(2,1)} %copy-done.7, bf16[4,128,512]{2,1,0:T(8,128)(2,1)} %copy-done.16, bf16[4,128,512]{2,1,0:T(8,128)(2,1)} %copy-done.17, bf16[6,128,512]{2,1,0:T(8,128)(2,1)} %copy-done.18, bf16[6,128,512]{2,1,0:T(8,128)(2,1)} %copy-done.19, ...), custom_call_target="tpu_custom_call" | custom-call | flops 1342177280 | bytes 7340032 | tf_op jit(solution)/shard_map/pallas_call | solution.py:315
  255.7 46.6 %all_to_all.15 = bf16[48,56,128]{2,1,0:T(8,128)(2,1)S(1)} all-to-all(bf16[48,56,128]{2,1,0:T(8,128)(2,1)S(1)} %bitcast.54), channel_id=1, replica_groups=mesh['z'=12,'yh'=4,'yl'=2,'x'=4,'core'=2] {'z','yh'}, dimensions={0} | all-to-all | bytes 1376256 | tf_op jit(solution)/shard_map/all_to_all | solution.py:459
  302.5 22.4 %all_gather.6 = bf16[672,128]{1,0:T(8,128)(2,1)S(1)} all-gather(bf16[56,128]{1,0:T(8,128)(2,1)S(1)} %reduce_sum.32), channel_id=1, replica_groups=mesh['z'=12,'yh'=4,'yl'=2,'x'=4,'core'=2] {'z'}, dimensions={0}, use_global_device_ids=true | all-gather | bytes 186368 | tf_op jit(solution)/shard_map/all_gather | solution.py:468
  324.9 18.2 %all_gather.7.whole = bf16[2688,128]{1,0:T(8,128)(2,1)} all-gather(bf16[672,128]{1,0:T(8,128)(2,1)S(1)} %all_gather.6), channel_id=1, replica_groups=mesh['z'=12,'yh'=4,'yl'=2,'x'=4,'core'=2] {'yh'}, dimensions={0}, use_global_device_ids=true | all-gather | bytes 860160 | tf_op jit(solution)/shard_map/all_gather | solution.py:469
  343.1 10.0 %shard_map.97 = (bf16[128,4096]{1,0:T(8,128)(2,1)}, bf16[128,4096]{1,0:T(8,128)(2,1)}) custom-call(s32[22]{0:T(128)} %stack.98.places, bf16[128,1280]{1,0:T(8,128)(2,1)} %copy-done.10, bf16[128,4096]{1,0:T(8,128)(2,1)} %bitcast.53, bf16[128,4096]{1,0:T(8,128)(2,1)} %bitcast.51, bf16[256,1280]{1,0:T(8,128)(2,1)} %copy-done, bf16[256,1280]{1,0:T(8,128)(2,1)} %copy-done.1, ...), custom_call_target="tpu_custom_call" | custom-call | flops 1342177280 | bytes 10485760 | tf_op jit(solution)/shard_map/pallas_call | solution.py:315
  (170 shorter events, 83.1 us)
Async XLA Ops:
  2.7 26.8 %collective-permute-start = (bf16[256,1280]{1,0:T(8,128)(2,1)S(1)}, bf16[256,1280]{1,0:T(8,128)(2,1)S(1)}, u32[]{:S(2)}, u32[]{:S(2)}) collective-permute-start(bf16[256,1280]{1,0:T(8,128)(2,1)S(1)} %constant_dynamic-update-slice_fusion.refs_0_), channel_id=1, source_target_pairs={{0,2},{2,4},{4,6},{6,0},{1,3},{3,5},{5,7},{7,1},{8,10},{10,12},{12... | collective-permute-start | bytes 1966088 | tf_op jit(solution)/shard_map/ppermute | solution.py:101
  6.1 23.4 %collective-permute-start.1 = (bf16[256,1280]{1,0:T(8,128)(2,1)S(1)}, bf16[256,1280]{1,0:T(8,128)(2,1)S(1)}, u32[]{:S(2)}, u32[]{:S(2)}) collective-permute-start(bf16[256,1280]{1,0:T(8,128)(2,1)S(1)} %constant_dynamic-update-slice_fusion.refs_0_), channel_id=1, source_target_pairs={{0,6},{2,0},{4,2},{6,4},{1,7},{3,1},{5,3},{7,5},{8,14},{10,8},{12,... | collective-permute-start | bytes 1966088 | tf_op jit(solution)/shard_map/ppermute | solution.py:101
  9.7 19.8 %collective-permute-start.4 = (bf16[256,1280]{1,0:T(8,128)(2,1)S(1)}, bf16[256,1280]{1,0:T(8,128)(2,1)S(1)}, u32[]{:S(2)}, u32[]{:S(2)}) collective-permute-start(bf16[256,1280]{1,0:T(8,128)(2,1)S(1)} %constant_dynamic-update-slice_fusion.refs_0_), channel_id=1, source_target_pairs={{0,1},{1,0},{2,3},{3,2},{4,5},{5,4},{6,7},{7,6},{8,9},{9,8},{10,11... | collective-permute-start | bytes 1966088 | tf_op jit(solution)/shard_map/ppermute | solution.py:114
  11.7 13.8 %collective-permute-start.2 = (bf16[128,1280]{1,0:T(8,128)(2,1)S(1)}, bf16[128,1280]{1,0:T(8,128)(2,1)}, u32[]{:S(2)}, u32[]{:S(2)}) collective-permute-start(bf16[128,1280]{1,0:T(8,128)(2,1)S(1)} %get-tuple-element.83), channel_id=1, source_target_pairs={{0,8},{8,16},{16,24},{24,32},{32,40},{40,48},{48,56},{56,0},{1,9},... | collective-permute-start | bytes 983048 | tf_op jit(solution)/shard_map/ppermute | solution.py:106
  16.4 13.0 %collective-permute-start.3 = (bf16[128,1280]{1,0:T(8,128)(2,1)S(1)}, bf16[128,1280]{1,0:T(8,128)(2,1)}, u32[]{:S(2)}, u32[]{:S(2)}) collective-permute-start(bf16[128,1280]{1,0:T(8,128)(2,1)S(1)} %get-tuple-element.82), channel_id=1, source_target_pairs={{0,56},{8,0},{16,8},{24,16},{32,24},{40,32},{48,40},{56,48},{1,57}... | collective-permute-start | bytes 983048 | tf_op jit(solution)/shard_map/ppermute | solution.py:106
  31.1 20.6 %collective-permute-start.5 = (bf16[256,1280]{1,0:T(8,128)(2,1)S(1)}, bf16[256,1280]{1,0:T(8,128)(2,1)S(1)}, u32[]{:S(2)}, u32[]{:S(2)}) collective-permute-start(bf16[256,1280]{1,0:T(8,128)(2,1)S(1)} %collective-permute-done.refs_1_), channel_id=1, source_target_pairs={{0,8},{8,16},{16,24},{24,32},{32,40},{40,48},{48,56},{56,0},{1,9},... | collective-permute-start | bytes 1966088 | tf_op jit(solution)/shard_map/ppermute | solution.py:106
  33.0 19.1 %collective-permute-start.6 = (bf16[256,1280]{1,0:T(8,128)(2,1)S(1)}, bf16[256,1280]{1,0:T(8,128)(2,1)S(1)}, u32[]{:S(2)}, u32[]{:S(2)}) collective-permute-start(bf16[256,1280]{1,0:T(8,128)(2,1)S(1)} %collective-permute-done.1.refs_2_), channel_id=1, source_target_pairs={{0,56},{8,0},{16,8},{24,16},{32,24},{40,32},{48,40},{56,48},{1,57}... | collective-permute-start | bytes 1966088 | tf_op jit(solution)/shard_map/ppermute | solution.py:106
  37.0 10.3 %collective-permute-start.8 = (bf16[128,1280]{1,0:T(8,128)(2,1)S(1)}, bf16[128,1280]{1,0:T(8,128)(2,1)S(1)}, u32[]{:S(2)}, u32[]{:S(2)}) collective-permute-start(bf16[128,1280]{1,0:T(8,128)(2,1)S(1)} %slice.75), channel_id=1, source_target_pairs={{0,6},{2,0},{4,2},{6,4},{1,7},{3,1},{5,3},{7,5},{8,14},{10,8},{12,... | collective-permute-start | bytes 983048 | tf_op jit(solution)/shard_map/ppermute | solution.py:101
  40.5 11.2 %collective-permute-start.7 = (bf16[128,1280]{1,0:T(8,128)(2,1)S(1)}, bf16[128,1280]{1,0:T(8,128)(2,1)S(1)}, u32[]{:S(2)}, u32[]{:S(2)}) collective-permute-start(bf16[128,1280]{1,0:T(8,128)(2,1)S(1)} %slice.74), channel_id=1, source_target_pairs={{0,2},{2,4},{4,6},{6,0},{1,3},{3,5},{5,7},{7,1},{8,10},{10,12},{12... | collective-permute-start | bytes 983048 | tf_op jit(solution)/shard_map/ppermute | solution.py:101
  45.4 31.8 %collective-permute-start.11 = (bf16[768,1280]{1,0:T(8,128)(2,1)}, bf16[768,1280]{1,0:T(8,128)(2,1)}, u32[]{:S(2)}, u32[]{:S(2)}) collective-permute-start(bf16[768,1280]{1,0:T(8,128)(2,1)} %pad_maximum_fusion), channel_id=1, source_target_pairs={{0,1},{1,0},{2,3},{3,2},{4,5},{5,4},{6,7},{7,6},{8,9},{9,8},{10,11... | collective-permute-start | bytes 5898248 | tf_op jit(solution)/shard_map/ppermute | solution.py:114
  53.6 23.6 %collective-permute-start.12 = (bf16[768,1280]{1,0:T(8,128)(2,1)}, bf16[768,1280]{1,0:T(8,128)(2,1)S(1)}, u32[]{:S(2)}, u32[]{:S(2)}) collective-permute-start(bf16[768,1280]{1,0:T(8,128)(2,1)} %pad_maximum_fusion.1), channel_id=1, source_target_pairs={{0,1},{1,0},{2,3},{3,2},{4,5},{5,4},{6,7},{7,6},{8,9},{9,8},{10,11... | collective-permute-start | bytes 5898248 | tf_op jit(solution)/shard_map/ppermute | solution.py:114
  55.5 15.2 %collective-permute-start.10 = (bf16[128,1280]{1,0:T(8,128)(2,1)S(1)}, bf16[128,1280]{1,0:T(8,128)(2,1)S(1)}, u32[]{:S(2)}, u32[]{:S(2)}) collective-permute-start(bf16[128,1280]{1,0:T(8,128)(2,1)S(1)} %collective-permute-done.8.refs_8_), channel_id=1, source_target_pairs={{0,56},{8,0},{16,8},{24,16},{32,24},{40,32},{48,40},{56,48},{1,57}... | collective-permute-start | bytes 983048 | tf_op jit(solution)/shard_map/ppermute | solution.py:106
  58.5 13.3 %collective-permute-start.9 = (bf16[128,1280]{1,0:T(8,128)(2,1)S(1)}, bf16[128,1280]{1,0:T(8,128)(2,1)S(1)}, u32[]{:S(2)}, u32[]{:S(2)}) collective-permute-start(bf16[128,1280]{1,0:T(8,128)(2,1)S(1)} %collective-permute-done.7.refs_7_), channel_id=1, source_target_pairs={{0,8},{8,16},{16,24},{24,32},{32,40},{40,48},{48,56},{56,0},{1,9},... | collective-permute-start | bytes 983048 | tf_op jit(solution)/shard_map/ppermute | solution.py:106
  86.4 26.7 %collective-permute-start.14 = (bf16[2,4,128,512]{3,2,1,0:T(8,128)(2,1)}, bf16[2,4,128,512]{3,2,1,0:T(8,128)(2,1)}, u32[]{:S(2)}, u32[]{:S(2)}) collective-permute-start(bf16[2,4,128,512]{3,2,1,0:T(8,128)(2,1)} %get-tuple-element.57), channel_id=1, source_target_pairs={{0,1},{1,0},{2,3},{3,2},{4,5},{5,4},{6,7},{7,6},{8,9},{9,8},{10,11... | collective-permute-start | bytes 3145736 | tf_op jit(solution)/shard_map/ppermute | solution.py:114
  90.5 45.2 %all-to-all-start = ((bf16[48,4,1408]{2,1,0:T(4,128)(2,1)}), bf16[48,4,1408]{2,1,0:T(4,128)(2,1)S(1)}, u32[]{:S(2)}, u32[]{:S(2)}) async-start(bf16[48,4,1408]{2,1,0:T(4,128)(2,1)} %reshape.94), calls=%async_computation | async-start | bytes 1081344 | tf_op jit(solution)/shard_map/all_to_all | solution.py:459
  108.2 34.0 %collective-permute-start.15 = (bf16[4,128,512]{2,1,0:T(8,128)(2,1)S(1)}, bf16[4,128,512]{2,1,0:T(8,128)(2,1)S(1)}, u32[]{:S(2)}, u32[]{:S(2)}) collective-permute-start(bf16[4,128,512]{2,1,0:T(8,128)(2,1)S(1)} %get-tuple-element.80), channel_id=1, source_target_pairs={{0,8},{8,0},{1,9},{9,1},{2,10},{10,2},{3,11},{11,3},{4,12},{12,4},... | collective-permute-start | bytes 1572872 | tf_op jit(solution)/shard_map/ppermute | solution.py:110
  115.2 31.0 %collective-permute-start.16 = (bf16[4,128,512]{2,1,0:T(8,128)(2,1)}, bf16[4,128,512]{2,1,0:T(8,128)(2,1)S(1)}, u32[]{:S(2)}, u32[]{:S(2)}) collective-permute-start(bf16[4,128,512]{2,1,0:T(8,128)(2,1)} %get-tuple-element.78), channel_id=1, source_target_pairs={{0,8},{8,0},{1,9},{9,1},{2,10},{10,2},{3,11},{11,3},{4,12},{12,4},... | collective-permute-start | bytes 1572872 | tf_op jit(solution)/shard_map/ppermute | solution.py:110
  149.0 52.5 %all-to-all-start.1 = ((bf16[48,4,1280]{2,1,0:T(4,128)(2,1)}), bf16[48,4,1280]{2,1,0:T(4,128)(2,1)S(1)}, u32[]{:S(2)}, u32[]{:S(2)}) async-start(bf16[48,4,1280]{2,1,0:T(4,128)(2,1)} %reshape.96), calls=%async_computation.1 | async-start | bytes 983040 | tf_op jit(solution)/shard_map/all_to_all | solution.py:459
  168.1 22.2 %collective-permute-start.17 = (bf16[6,128,512]{2,1,0:T(8,128)(2,1)}, bf16[6,128,512]{2,1,0:T(8,128)(2,1)S(1)}, u32[]{:S(2)}, u32[]{:S(2)}) collective-permute-start(bf16[6,128,512]{2,1,0:T(8,128)(2,1)} %slice_dynamic-update-slice_fusion.6), channel_id=1, source_target_pairs={{0,2},{2,4},{4,6},{6,0},{1,3},{3,5},{5,7},{7,1},{8,10},{10,12},{12... | collective-permute-start | bytes 2359304 | tf_op jit(solution)/shard_map/ppermute | solution.py:101
  170.2 22.0 %collective-permute-start.18 = (bf16[6,128,512]{2,1,0:T(8,128)(2,1)}, bf16[6,128,512]{2,1,0:T(8,128)(2,1)S(1)}, u32[]{:S(2)}, u32[]{:S(2)}) collective-permute-start(bf16[6,128,512]{2,1,0:T(8,128)(2,1)} %get-tuple-element.84), channel_id=1, source_target_pairs={{0,6},{2,0},{4,2},{6,4},{1,7},{3,1},{5,3},{7,5},{8,14},{10,8},{12,... | collective-permute-start | bytes 2359304 | tf_op jit(solution)/shard_map/ppermute | solution.py:101
  190.3 9.9 %collective-permute-start.19 = (bf16[2,128,512]{2,1,0:T(8,128)(2,1)S(1)}, bf16[2,128,512]{2,1,0:T(8,128)(2,1)S(1)}, u32[]{:S(2)}, u32[]{:S(2)}) collective-permute-start(bf16[2,128,512]{2,1,0:T(8,128)(2,1)S(1)} %slice.100), channel_id=1, source_target_pairs={{0,2},{2,4},{4,6},{6,0},{1,3},{3,5},{5,7},{7,1},{8,10},{10,12},{12... | collective-permute-start | bytes 786440 | tf_op jit(solution)/shard_map/ppermute | solution.py:101
  192.3 9.2 %collective-permute-start.20 = (bf16[2,128,512]{2,1,0:T(8,128)(2,1)S(1)}, bf16[2,128,512]{2,1,0:T(8,128)(2,1)}, u32[]{:S(2)}, u32[]{:S(2)}) collective-permute-start(bf16[2,128,512]{2,1,0:T(8,128)(2,1)S(1)} %slice.101), channel_id=1, source_target_pairs={{0,6},{2,0},{4,2},{6,4},{1,7},{3,1},{5,3},{7,5},{8,14},{10,8},{12,... | collective-permute-start | bytes 786440 | tf_op jit(solution)/shard_map/ppermute | solution.py:101
  201.9 10.3 %collective-permute-start.22 = (bf16[128,1280]{1,0:T(8,128)(2,1)S(1)}, bf16[128,1280]{1,0:T(8,128)(2,1)S(1)}, u32[]{:S(2)}, u32[]{:S(2)}) collective-permute-start(bf16[128,1280]{1,0:T(8,128)(2,1)S(1)} %convolution_convert_fusion.refs_8_.both), channel_id=1, source_target_pairs={{0,6},{2,0},{4,2},{6,4},{1,7},{3,1},{5,3},{7,5},{8,14},{10,8},{12,... | collective-permute-start | bytes 983048 | tf_op jit(solution)/shard_map/ppermute | solution.py:101
  207.6 10.2 %collective-permute-start.23 = (bf16[128,1280]{1,0:T(8,128)(2,1)S(1)}, bf16[128,1280]{1,0:T(8,128)(2,1)S(1)}, u32[]{:S(2)}, u32[]{:S(2)}) collective-permute-start(bf16[128,1280]{1,0:T(8,128)(2,1)S(1)} %convolution_convert_fusion.refs_8_.both), channel_id=1, source_target_pairs={{0,8},{8,0},{1,9},{9,1},{2,10},{10,2},{3,11},{11,3},{4,12},{12,4},... | collective-permute-start | bytes 983048 | tf_op jit(solution)/shard_map/ppermute | solution.py:110
  209.6 13.1 %collective-permute-start.21 = (bf16[128,1280]{1,0:T(8,128)(2,1)S(1)}, bf16[128,1280]{1,0:T(8,128)(2,1)S(1)}, u32[]{:S(2)}, u32[]{:S(2)}) collective-permute-start(bf16[128,1280]{1,0:T(8,128)(2,1)S(1)} %convolution_convert_fusion.refs_8_.both), channel_id=1, source_target_pairs={{0,2},{2,4},{4,6},{6,0},{1,3},{3,5},{5,7},{7,1},{8,10},{10,12},{12... | collective-permute-start | bytes 983048 | tf_op jit(solution)/shard_map/ppermute | solution.py:101
  212.2 12.5 %collective-permute-start.26 = (bf16[128,1280]{1,0:T(8,128)(2,1)S(1)}, bf16[128,1280]{1,0:T(8,128)(2,1)S(1)}, u32[]{:S(2)}, u32[]{:S(2)}) collective-permute-start(bf16[128,1280]{1,0:T(8,128)(2,1)S(1)} %collective-permute-done.22.refs_10_), channel_id=1, source_target_pairs={{0,6},{2,0},{4,2},{6,4},{1,7},{3,1},{5,3},{7,5},{8,14},{10,8},{12,... | collective-permute-start | bytes 983048 | tf_op jit(solution)/shard_map/ppermute | solution.py:101
  217.8 10.2 %collective-permute-start.25 = (bf16[128,1280]{1,0:T(8,128)(2,1)S(1)}, bf16[128,1280]{1,0:T(8,128)(2,1)S(1)}, u32[]{:S(2)}, u32[]{:S(2)}) collective-permute-start(bf16[128,1280]{1,0:T(8,128)(2,1)S(1)} %collective-permute-done.23.refs_11_), channel_id=1, source_target_pairs={{0,2},{2,4},{4,6},{6,0},{1,3},{3,5},{5,7},{7,1},{8,10},{10,12},{12... | collective-permute-start | bytes 983048 | tf_op jit(solution)/shard_map/ppermute | solution.py:101
  219.7 9.0 %collective-permute-start.24 = (bf16[128,1280]{1,0:T(8,128)(2,1)S(1)}, bf16[128,1280]{1,0:T(8,128)(2,1)S(1)}, u32[]{:S(2)}, u32[]{:S(2)}) collective-permute-start(bf16[128,1280]{1,0:T(8,128)(2,1)S(1)} %collective-permute-done.22.refs_10_), channel_id=1, source_target_pairs={{0,8},{8,0},{1,9},{9,1},{2,10},{10,2},{3,11},{11,3},{4,12},{12,4},... | collective-permute-start | bytes 983048 | tf_op jit(solution)/shard_map/ppermute | solution.py:110
  222.8 24.0 %collective-permute-start.30 = (bf16[384,1280]{1,0:T(8,128)(2,1)S(1)}, bf16[384,1280]{1,0:T(8,128)(2,1)}, u32[]{:S(2)}, u32[]{:S(2)}) collective-permute-start(bf16[384,1280]{1,0:T(8,128)(2,1)S(1)} %pad_maximum_fusion.2), channel_id=1, source_target_pairs={{0,1},{1,0},{2,3},{3,2},{4,5},{5,4},{6,7},{7,6},{8,9},{9,8},{10,11... | collective-permute-start | bytes 2949128 | tf_op jit(solution)/shard_map/ppermute | solution.py:114
  228.8 18.0 %collective-permute-start.31 = (bf16[384,1280]{1,0:T(8,128)(2,1)S(1)}, bf16[384,1280]{1,0:T(8,128)(2,1)S(1)}, u32[]{:S(2)}, u32[]{:S(2)}) collective-permute-start(bf16[384,1280]{1,0:T(8,128)(2,1)S(1)} %pad_maximum_fusion.3), channel_id=1, source_target_pairs={{0,1},{1,0},{2,3},{3,2},{4,5},{5,4},{6,7},{7,6},{8,9},{9,8},{10,11... | collective-permute-start | bytes 2949128 | tf_op jit(solution)/shard_map/ppermute | solution.py:114
  233.5 9.7 %collective-permute-start.28 = (bf16[64,1280]{1,0:T(8,128)(2,1)S(1)}, bf16[64,1280]{1,0:T(8,128)(2,1)S(1)}, u32[]{:S(2)}, u32[]{:S(2)}) collective-permute-start(bf16[64,1280]{1,0:T(8,128)(2,1)S(1)} %slice.103), channel_id=1, source_target_pairs={{0,2},{2,4},{4,6},{6,0},{1,3},{3,5},{5,7},{7,1},{8,10},{10,12},{12... | collective-permute-start | bytes 491528 | tf_op jit(solution)/shard_map/ppermute | solution.py:101
  235.5 9.7 %collective-permute-start.29 = (bf16[128,1280]{1,0:T(8,128)(2,1)S(1)}, bf16[128,1280]{1,0:T(8,128)(2,1)S(1)}, u32[]{:S(2)}, u32[]{:S(2)}) collective-permute-start(bf16[128,1280]{1,0:T(8,128)(2,1)S(1)} %convolution_convert_fusion.refs_8_.both), channel_id=1, source_target_pairs={{0,1},{1,0},{2,3},{3,2},{4,5},{5,4},{6,7},{7,6},{8,9},{9,8},{10,11... | collective-permute-start | bytes 983048 | tf_op jit(solution)/shard_map/ppermute | solution.py:114
  (38 other events, 714.1 us)

commit v3 on v2

--- a/solution.py
+++ b/solution.py
@@ -101,9 +101,22 @@
     return lax.ppermute(array, "x", [(i, (i + step) % size) for i in range(size)])
 
 
-def shift_y(array, step):
+def along_x(array):
+    size = lax.axis_size("x")
+    pairs = []
+    for i in range(size):
+        pairs.append((2 * i, (i + 1) % size * 2))
+        pairs.append((2 * i + 1, (i - 1) % size * 2 + 1))
+    return lax.ppermute(array, ("x", "core"), pairs)
+
+
+def along_y(array):
     size = lax.axis_size(("yh", "yl"))
-    return lax.ppermute(array, ("yh", "yl"), [(i, (i + step) % size) for i in range(size)])
+    pairs = []
+    for i in range(size):
+        pairs.append((2 * i, (i + 1) % size * 2))
+        pairs.append((2 * i + 1, (i - 1) % size * 2 + 1))
+    return lax.ppermute(array, ("yh", "yl", "core"), pairs)
 
 
 def swap_y(array):
@@ -137,65 +150,86 @@
     return jnp.stack([place(*offset) for offset in offsets])
 
 
-def spread_cols(keep, send):
-    other = swap_core(send)
-    across_0 = swap_y(keep[1])
-    across_1 = swap_y(other[1])
-    return (keep[0], other[0], across_0, across_1)
-
-
-def spread_cols_x(here):
-    quads = [[part[dx] for part in here] for dx in range(4)]
-    up = jnp.stack(quads[1] + quads[2][:2])
-    down = jnp.stack(quads[3] + quads[2][2:])
+def pack_kernel(keep, other, across, up, down):
+    half = across.shape[0] // 2
+    for out, dx, tail in ((up, 1, (keep[0, 2], other[0, 2])), (down, 3, (across[2], across[half + 2]))):
+        out[0] = keep[0, dx]
+        out[1] = other[0, dx]
+        out[2] = across[dx]
+        out[3] = across[half + dx]
+        out[4] = tail[0]
+        out[5] = tail[1]
+
+
+def spread_cols(keep, other, ahead):
+    piece = keep.shape[2:]
+    across = swap_y(ahead)
+    up, down = call(
+        pack_kernel,
+        None,
+        [keep, other, across],
+        [jax.ShapeDtypeStruct((6, *piece), jnp.bfloat16)] * 2,
+        [],
+        keep.size,
+        12 * keep.size,
+    )
     up = shift_x(up, 1)
     down = shift_x(down, -1)
     far_up = shift_x(up[4:], 1)
     far_down = shift_x(down[4:], -1)
     sources = [(0, 0), (0, 1), (1, 0), (1, 1)]
-    arrays = [*here, up, down, far_up, far_down]
-    pieces = [(number, 0, (0, *source)) for number, source in enumerate(sources)]
-    pieces += [(4, number, (3, *source)) for number, source in enumerate(sources)]
-    pieces += [(5, number, (1, *source)) for number, source in enumerate(sources)]
-    pieces += [(6, number, (2, *source)) for number, source in enumerate(sources[:2])]
-    pieces += [(7, number, (2, *source)) for number, source in enumerate(sources[2:])]
+    arrays = [keep, other, across, up, down, far_up, far_down]
+    pieces = [(0, (0, 0), (0, 0, 0)), (1, (0, 0), (0, 0, 1))]
+    pieces += [(2, (0,), (0, 1, 0)), (2, (4,), (0, 1, 1))]
+    pieces += [(3, (number,), (3, *source)) for number, source in enumerate(sources)]
+    pieces += [(4, (number,), (1, *source)) for number, source in enumerate(sources)]
+    pieces += [(5, (number,), (2, *source)) for number, source in enumerate(sources[:2])]
+    pieces += [(6, (number,), (2, *source)) for number, source in enumerate(sources[2:])]
     return (arrays, pieces)
 
 
-def gather_weights(block, beside):
-    half = block.shape[0] // 2
-    full = 2 * half
-    left = shift_x(block, 1)
-    right = shift_x(block, -1)
-    across_a = shift_y(block[:half], 1)
-    across_b = shift_y(block[half:], -1)
+def gather_weights(block, first_dot, beside):
+    rows = block.shape[0]
+    sign = 1 - 2 * lax.axis_index("core")
     other_0 = swap_core(block)
-    left, right, across_a, across_b, other_0, beside = lax.optimization_barrier(
-        (left, right, across_a, across_b, other_0, beside)
-    )
-    left_y = shift_y(left, 1)
-    right_y = shift_y(right, -1)
-    far_a = shift_x(left[:half], 1)
-    far_b = shift_x(right[half:], -1)
-    other_1 = swap_core(jnp.concatenate([left, right, across_a, across_b], axis=0))
-    far_y_a = shift_y(far_a, 1)
-    far_y_b = shift_y(far_b, -1)
-    other_2 = swap_core(jnp.concatenate([left_y, right_y, far_a, far_b], axis=0))
-    other_3 = swap_core(jnp.concatenate([far_y_a, far_y_b], axis=0))
-    parts_1 = [(-1, 0, 0, full), (1, 0, 0, full), (0, 1, 0, half), (0, 1, half, half)]
-    parts_2 = [(-1, 1, 0, full), (1, 1, 0, full), (2, 0, 0, half), (2, 0, half, half)]
-    parts_3 = [(2, 1, 0, half), (2, 1, half, half)]
-    mine = [block, left, right, across_a, across_b, left_y, right_y, far_a, far_b]
-    mine += [far_y_a, far_y_b]
-    own_parts = [(0, 0, 0, full)] + parts_1 + parts_2 + parts_3
-    groups = [(0, array, [part]) for array, part in zip(mine, own_parts)]
-    groups += [
-        (1, other_0, [(0, 0, 0, full)]),
-        (1, other_1, parts_1),
-        (1, other_2, parts_2),
-        (1, other_3, parts_3),
+    across = along_y(block)
+    chip = jnp.concatenate([block, other_0], axis=0)
+    side = along_x(chip)
+    side, across, beside = lax.optimization_barrier((side, across, beside))
+    side_y = along_y(side)
+    far = along_x(side[:rows])
+    other_1 = swap_core(jnp.concatenate([side, across], axis=0))
+    groups = [
+        (block, [(0, 0, 0)]),
+        (other_0, [(0, 0, 1)]),
+        (side, [(-sign, 0, 0), (-sign, 0, 1)]),
+        (across, [(0, 1, 0)]),
+        (other_1, [(sign, 0, 1), (sign, 0, 0), (0, 1, 1)]),
     ]
-    return (*label_blocks(groups), beside)
+    early = number_blocks(groups, rows)
+    total = first_dot(beside, *early)
+    far, total = lax.optimization_barrier((far, total))
+    far_y = along_y(far)
+    other_2 = swap_core(jnp.concatenate([side_y, far], axis=0))
+    other_3 = swap_core(far_y)
+    groups = [
+        (side_y, [(-sign, 1, 0), (-sign, 1, 1)]),
+        (far, [(2, 0, 0)]),
+        (far_y, [(2, 1, 0)]),
+        (other_2, [(sign, 1, 1), (sign, 1, 0), (2, 0, 1)]),
+        (other_3, [(2, 1, 1)]),
+    ]
+    return (early, number_blocks(groups, rows), total, beside)
+
+
+def number_blocks(groups, rows):
+    arrays, pieces, places = [], [], []
+    for array, offsets in groups:
+        for number, offset in enumerate(offsets):
+            pieces.append((len(arrays), number * rows, 0, rows))
+            places.append(place(*offset))
+        arrays.append(array)
+    return (arrays, pieces, jnp.stack(places))
 
 
 def gather_rows(block):
@@ -228,8 +262,7 @@
     return label_blocks(groups)
 
 
-def project_kernel(pieces, share, split, places, normed, cot, routing, flags, *refs):
-    blocks, (out, total) = (refs[:-2], refs[-2:])
+def add_products(pieces, share, split, places, normed, cot, blocks, total, fresh):
     for number, (which, row, sub, rows) in enumerate(pieces):
         columns = pl.ds(pl.multiple_of(places[number] * share + sub, 128), rows)
         first = jnp.dot(
@@ -242,12 +275,22 @@
             blocks[which][row : row + rows, split:],
             preferred_element_type=jnp.float32,
         )
-        if number == 0:
+        if fresh and number == 0:
             total[:, :split] = first
             total[:, split:] = second
         else:
             total[:, :split] += first
             total[:, split:] += second
+
+
+def first_kernel(pieces, share, split, places, normed, cot, *refs):
+    add_products(pieces, share, split, places, normed, cot, refs[:-1], refs[-1], True)
+
+
+def project_kernel(pieces, share, split, places, normed, cot, begun, routing, flags, *refs):
+    blocks, (out, total) = (refs[:-2], refs[-2:])
+    total[...] = begun[...]
+    add_products(pieces, share, split, places, normed, cot, blocks, total, False)
     width = total.shape[1]
     out[:, :width] = jnp.dot(
         routing[...], total[...].astype(jnp.bfloat16), preferred_element_type=jnp.float32
@@ -292,7 +335,7 @@
     inputs, (out, rows_all, cols_all) = (refs[:-3], refs[-3:])
     col_count = 1 + max(which for which, _, _ in col_pieces)
     share = cols_all.shape[1] // 2
-    count = inputs[0].shape[1]
+    count = inputs[0].shape[2]
     for which, index, to in col_pieces:
         cols_all[to : to + count, :] = inputs[which][index]
     for which, row, to, rows in row_pieces:
@@ -375,24 +418,41 @@
     source_ids = jnp.arange(groups, dtype=jnp.int32)[:, None]
     slot_ids = jnp.arange(slot_count, dtype=jnp.int32)[None, :]
     position = ((source_ids - my_start) % groups + groups * slot_ids).reshape(total_slots)
-    blocks, pieces, offsets, beside = gather_weights(
+    other = swap_core(send)
+    ahead = jnp.concatenate([keep[1], other[1]], axis=0)
+
+    def first_dot(beside, arrays, pieces, places):
+        return call(
+            functools.partial(first_kernel, pieces, share, qkv_width),
+            places,
+            [beside[0], cot_rows, *arrays],
+            jax.ShapeDtypeStruct((row_count, width), jnp.float32),
+            [],
+            row_count * model_width * width,
+            model_width * width,
+        )
+
+    early, late, begun, beside = gather_weights(
         jnp.concatenate([qkv_weight, out_weight], axis=1),
-        (normed_b, keep, send, flag_cols, routing, position),
-    )
-    normed_b, keep, send, flag_cols, routing, position = beside
-    places = place_all(offsets)
+        first_dot,
+        (normed_b, keep, other, ahead, flag_cols, routing, position),
+    )
+    normed_b, keep, other, ahead, flag_cols, routing, position = beside
     slots = call(
-        functools.partial(project_kernel, pieces, share, qkv_width),
-        places,
-        [normed_b, cot_rows, routing, flag_cols, *blocks],
+        functools.partial(project_kernel, late[1], share, qkv_width),
+        late[2],
+        [normed_b, cot_rows, begun, routing, flag_cols, *late[0]],
         jax.ShapeDtypeStruct((total_slots, width + 128), jnp.bfloat16),
         [pltpu.VMEM((row_count, width), jnp.float32)],
-        2 * row_count * model_width * width,
-        2 * model_width * width,
-    )
-    slots, keep, send = lax.optimization_barrier((slots, keep, send))
+        row_count * model_width * width,
+        model_width * width,
+    )
+    blocks = [*early[0], *late[0]]
+    pieces = early[1] + [(len(early[0]) + which, *rest) for which, *rest in late[1]]
+    places = jnp.concatenate([early[2], late[2]])
+    slots, keep, other, ahead = lax.optimization_barrier((slots, keep, other, ahead))
     got = swap_dp(slots.reshape(groups, slot_count, width + 128))
-    here = spread_cols(keep, send)
+    cols, col_pieces = spread_cols(keep, other, ahead)
     got = got.reshape(total_slots, width + 128)
     both = call(
         functools.partial(attention_kernel, QH),
@@ -403,9 +463,7 @@
         18 * total_slots * total_slots * out_width,
         4 * total_slots * width,
     )
-    both, here = lax.optimization_barrier((both, here))
     back = swap_dp(both.reshape(groups, slot_count, width))
-    cols, col_pieces = spread_cols_x(here)
     back, cols = lax.optimization_barrier((back, cols))
     both_rows = from_slots(back)
     row_blocks, row_pieces, row_offsets = gather_rows(both_rows)
@@ -460,13 +518,9 @@
 
 
 def sum_over_dp(partial):
-    groups, each, lanes = partial.shape
-    rows, cols = (lax.axis_size("z"), lax.axis_size("yh"))
-    ordered = jnp.swapaxes(partial.reshape(cols, rows, each, lanes), 0, 1)
-    got = swap_dp(ordered.reshape(groups, each, lanes))
+    got = swap_dp(partial)
     mine = jnp.sum(got.astype(jnp.float32), axis=0).astype(jnp.bfloat16)
-    whole = lax.all_gather(mine, "z", axis=0, tiled=True)
-    return lax.all_gather(whole, "yh", axis=0, tiled=True)
+    return swap_dp(jnp.broadcast_to(mine[None], partial.shape)).reshape(-1, partial.shape[2])
 
 
 def solution(mesh):

time: 357 us -> 342 us (0.958)
  the two profiles are of different devices: /device:TPU:24 before, /device:TPU:8 now
where the time goes in v3:
time: 342 us; the launch traced here: 341 us
  waiting for transfers between devices  114 us (33%)
  starting transfers between devices  106 us (31%)
  blocking collectives  47.7 us (14%)
  Pallas kernels  41.6 us (12%)
  local copies, waits for them, and re-layouts  21.1 us (6%)
  other arithmetic  8.34 us (2%)
    all_to_all x1, blocking collectives, swap_dp(): return lax.all_to_all(array, DP, split_axis=0, concat_axis=0, tiled=True)  47.7 us
    all_to_all x3, waiting for transfers between devices, swap_dp(): return lax.all_to_all(array, DP, split_axis=0, concat_axis=0, tiled=True)  44.9 us
    pallas_call x8, Pallas kernels, call(): pl.pallas_call(kernel, out_shape=out_shape, in_specs=smem + [vmem] * len(...  41.6 us
    ppermute x9, starting transfers between devices, shift_x(): lax.ppermute(array, 'x', [(i, (i + step) % size) for i in range(size)])  30.7 us
    ppermute x9, waiting for transfers between devices, shift_x(): lax.ppermute(array, 'x', [(i, (i + step) % size) for i in range(size)])  26.1 us
    ppermute x9, starting transfers between devices, swap_core(): return lax.ppermute(array, 'core', [(0, 1), (1, 0)])  25.8 us
    ppermute x2, waiting for transfers between devices, along_x(): return lax.ppermute(array, ('x', 'core'), pairs)  22.4 us
    all_to_all x3, starting transfers between devices, swap_dp(): return lax.all_to_all(array, DP, split_axis=0, concat_axis=0, tiled=True)  22.2 us
  transfers between devices with their start and end apart: 30, of which 16 were waited for; matrix products, arithmetic and copies ran while one was open for 4% of the time, Pallas kernels for 8%

profile of v3, /device:TPU:8, one launch (start us, length us, event | category | flops | bytes accessed | tf_op | source)
XLA Modules:
  0.0 340.7 jit_solution(8884337472412647946)
XLA Ops:
  4.6 3.5 %collective-permute-start.2 = (bf16[256,1280]{1,0:T(8,128)(2,1)S(1)}, bf16[256,1280]{1,0:T(8,128)(2,1)}, u32[]{:S(2)}, u32[]{:S(2)}) collective-permute-start(bf16[256,1280]{1,0:T(8,128)(2,1)S(1)} %constant_dynamic-update-slice_fusion.refs_0_), channel_id=1, source_target_pairs={{0,8},{1,57},{8,16},{9,1},{16,24},{17,9},{24,32},{25,17},{32,40},{... | collective-permute-start | bytes 1966088 | tf_op jit(solution)/shard_map/ppermute | solution.py:119
  8.8 3.8 %shard_map.93 = (bf16[128,4096]{1,0:T(8,128)(2,1)}, bf16[2,4,128,512]{3,2,1,0:T(8,128)(2,1)}, bf16[2,4,128,512]{3,2,1,0:T(8,128)(2,1)}) custom-call(s32[16]{0:T(128)} %stack.113.places, bf16[128,4096]{1,0:T(8,128)(2,1)} %bitcast.55, bf16[128,4096]{1,0:T(8,128)(2,1)} %bitcast.51), custom_call_target="tpu_custom_call" | custom-call | flops 2097152 | bytes 5242880 | tf_op jit(solution)/shard_map/pallas_call | solution.py:358
  12.6 10.1 %collective-permute-start.3 = (bf16[2,4,128,512]{3,2,1,0:T(8,128)(2,1)}, bf16[2,4,128,512]{3,2,1,0:T(8,128)(2,1)}, u32[]{:S(2)}, u32[]{:S(2)}) collective-permute-start(bf16[2,4,128,512]{3,2,1,0:T(8,128)(2,1)} %get-tuple-element.40), channel_id=1, source_target_pairs={{0,1},{1,0},{2,3},{3,2},{4,5},{5,4},{6,7},{7,6},{8,9},{9,8},{10,11... | collective-permute-start | bytes 3145736 | tf_op jit(solution)/shard_map/ppermute | solution.py:127
  31.6 16.0 %collective-permute-done.1.refs_2_ = bf16[512,1280]{1,0:T(8,128)(2,1)S(1)} collective-permute-done((bf16[512,1280]{1,0:T(8,128)(2,1)}, bf16[512,1280]{1,0:T(8,128)(2,1)S(1)}, u32[]{:S(2)}, u32[]{:S(2)}) %collective-permute-start.1) | collective-permute-done | bytes 1310752 | tf_op jit(solution)/shard_map/ppermute | solution.py:110
  48.4 2.5 pad_maximum_fusion
  58.4 4.9 %shard_map.94.begun = f32[128,1280]{1,0:T(8,128)} custom-call(s32[8]{0:T(128)} %stack.115.places, bf16[128,4096]{1,0:T(8,128)(2,1)} %get-tuple-element.42.normed, bf16[128,4096]{1,0:T(8,128)(2,1)} %bitcast.52, bf16[256,1280]{1,0:T(8,128)(2,1)} %copy-done.2, bf16[256,1280]{1,0:T(8,128)(2,1)} %copy-done.4, bf16[512,1280]{1,0:T(8,128)(2,1)} %copy-done, ...), custom_call_target="tpu_custom_call" | custom-call | flops 671088640 | bytes 5242880 | tf_op jit(solution)/shard_map/pallas_call | solution.py:358
  63.3 6.3 %collective-permute-done.4.refs_1_.refs_6_ = bf16[256,1280]{1,0:T(8,128)(2,1)S(1)} collective-permute-done((bf16[256,1280]{1,0:T(8,128)(2,1)}, bf16[256,1280]{1,0:T(8,128)(2,1)S(1)}, u32[]{:S(2)}, u32[]{:S(2)}) %collective-permute-start.4) | collective-permute-done | bytes 655392 | tf_op jit(solution)/shard_map/ppermute | solution.py:110
  69.6 2.7 collective-permute-done.6.refs_0_.refs_5_
  77.8 10.6 %collective-permute-done.7.refs_2_.refs_7_ = bf16[256,1280]{1,0:T(8,128)(2,1)S(1)} collective-permute-done((bf16[256,1280]{1,0:T(8,128)(2,1)S(1)}, bf16[256,1280]{1,0:T(8,128)(2,1)S(1)}, u32[]{:S(2)}, u32[]{:S(2)}) %collective-permute-start.7) | collective-permute-done | bytes 655392 | tf_op jit(solution)/shard_map/ppermute | solution.py:119
  93.2 5.5 %shard_map.95 = bf16[192,1408]{1,0:T(8,128)(2,1)} custom-call(s32[8]{0:T(128)} %stack.114.places, bf16[128,4096]{1,0:T(8,128)(2,1)} %get-tuple-element.42.normed, bf16[128,4096]{1,0:T(8,128)(2,1)} %bitcast.53, f32[128,1280]{1,0:T(8,128)} %shard_map.94.begun, bf16[192,128]{1,0:T(8,128)(2,1)} %fusion.routing, bf16[128,128]{1,0:T(8,128)(2,1)} %broadcast_in_dim.26.flags, ...), custom_call_target="tpu_custom_call" | custom-call | flops 671088640 | bytes 5242880 | tf_op jit(solution)/shard_map/pallas_call | solution.py:358
  100.7 12.1 %all-to-all-start = ((bf16[48,4,1408]{2,1,0:T(4,128)(2,1)}), bf16[48,4,1408]{2,1,0:T(4,128)(2,1)S(1)}, u32[]{:S(2)}, u32[]{:S(2)}) async-start(bf16[48,4,1408]{2,1,0:T(4,128)(2,1)} %reshape.98), calls=%async_computation | async-start | bytes 1081344 | tf_op jit(solution)/shard_map/all_to_all | solution.py:517
  112.8 4.8 %collective-permute-start.10 = (bf16[8,128,512]{2,1,0:T(8,128)(2,1)S(1)}, bf16[8,128,512]{2,1,0:T(8,128)(2,1)S(1)}, u32[]{:S(2)}, u32[]{:S(2)}) collective-permute-start(bf16[8,128,512]{2,1,0:T(8,128)(2,1)S(1)} %copy-done.19), channel_id=1, source_target_pairs={{0,8},{8,0},{1,9},{9,1},{2,10},{10,2},{3,11},{11,3},{4,12},{12,4},... | collective-permute-start | bytes 3145736 | tf_op jit(solution)/shard_map/ppermute | solution.py:123
  119.1 22.6 %all-to-all-done = bf16[48,4,1408]{2,1,0:T(4,128)(2,1)S(1)} async-done(((bf16[48,4,1408]{2,1,0:T(4,128)(2,1)}), bf16[48,4,1408]{2,1,0:T(4,128)(2,1)S(1)}, u32[]{:S(2)}, u32[]{:S(2)}) %all-to-all-start) | async-done | bytes 540704 | tf_op jit(solution)/shard_map/all_to_all | solution.py:517
  142.6 5.5 %shard_map.96 = bf16[192,1280]{1,0:T(8,128)(2,1)} custom-call(s32[1]{0:T(128)} %bitcast.16.length, s32[192,1]{1,0:T(8,128)} %copy.14.place_col, s32[1,192]{1,0:T(1,128)} %bitcast.60, bf16[192,1408]{1,0:T(8,128)(2,1)} %reshape.99.got), custom_call_target="tpu_custom_call" | custom-call | flops 339738624 | bytes 983040 | tf_op jit(solution)/shard_map/pallas_call | solution.py:358
  150.0 5.0 %all-to-all-start.1 = ((bf16[48,4,1280]{2,1,0:T(4,128)(2,1)}), bf16[48,4,1280]{2,1,0:T(4,128)(2,1)S(1)}, u32[]{:S(2)}, u32[]{:S(2)}) async-start(bf16[48,4,1280]{2,1,0:T(4,128)(2,1)} %reshape.100), calls=%async_computation.1 | async-start | bytes 983040 | tf_op jit(solution)/shard_map/all_to_all | solution.py:517
  156.1 3.1 shard_map.97
  161.3 4.9 %collective-permute-start.12 = (bf16[6,128,512]{2,1,0:T(8,128)(2,1)}, bf16[6,128,512]{2,1,0:T(8,128)(2,1)S(1)}, u32[]{:S(2)}, u32[]{:S(2)}) collective-permute-start(bf16[6,128,512]{2,1,0:T(8,128)(2,1)} %get-tuple-element.57), channel_id=1, source_target_pairs={{0,6},{2,0},{4,2},{6,4},{1,7},{3,1},{5,3},{7,5},{8,14},{10,8},{12,... | collective-permute-start | bytes 2359304 | tf_op jit(solution)/shard_map/ppermute | solution.py:101
  166.2 15.0 %collective-permute-done.11.refs_3_ = bf16[6,128,512]{2,1,0:T(8,128)(2,1)S(1)} collective-permute-done((bf16[6,128,512]{2,1,0:T(8,128)(2,1)}, bf16[6,128,512]{2,1,0:T(8,128)(2,1)S(1)}, u32[]{:S(2)}, u32[]{:S(2)}) %collective-permute-start.11) | collective-permute-done | bytes 786464 | tf_op jit(solution)/shard_map/ppermute | solution.py:101
  183.2 5.1 %collective-permute-start.14 = (bf16[2,128,512]{2,1,0:T(8,128)(2,1)S(1)}, bf16[2,128,512]{2,1,0:T(8,128)(2,1)}, u32[]{:S(2)}, u32[]{:S(2)}) collective-permute-start(bf16[2,128,512]{2,1,0:T(8,128)(2,1)S(1)} %slice.30), channel_id=1, source_target_pairs={{0,6},{2,0},{4,2},{6,4},{1,7},{3,1},{5,3},{7,5},{8,14},{10,8},{12,... | collective-permute-start | bytes 786440 | tf_op jit(solution)/shard_map/ppermute | solution.py:101
  188.4 2.7 collective-permute-done.13.refs_5_
  192.7 5.7 %collective-permute-start.16 = (bf16[128,1280]{1,0:T(8,128)(2,1)S(1)}, bf16[128,1280]{1,0:T(8,128)(2,1)S(1)}, u32[]{:S(2)}, u32[]{:S(2)}) collective-permute-start(bf16[128,1280]{1,0:T(8,128)(2,1)S(1)} %convolution_convert_fusion.refs_7_.both), channel_id=1, source_target_pairs={{0,6},{2,0},{4,2},{6,4},{1,7},{3,1},{5,3},{7,5},{8,14},{10,8},{12,... | collective-permute-start | bytes 983048 | tf_op jit(solution)/shard_map/ppermute | solution.py:101
  198.4 4.8 %collective-permute-start.17 = (bf16[128,1280]{1,0:T(8,128)(2,1)S(1)}, bf16[128,1280]{1,0:T(8,128)(2,1)S(1)}, u32[]{:S(2)}, u32[]{:S(2)}) collective-permute-start(bf16[128,1280]{1,0:T(8,128)(2,1)S(1)} %convolution_convert_fusion.refs_7_.both), channel_id=1, source_target_pairs={{0,8},{8,0},{1,9},{9,1},{2,10},{10,2},{3,11},{11,3},{4,12},{12,4},... | collective-permute-start | bytes 983048 | tf_op jit(solution)/shard_map/ppermute | solution.py:123
  205.2 2.6 collective-permute-start.18
  207.8 3.4 %collective-permute-done.17.refs_10_ = bf16[128,1280]{1,0:T(8,128)(2,1)S(1)} collective-permute-done((bf16[128,1280]{1,0:T(8,128)(2,1)S(1)}, bf16[128,1280]{1,0:T(8,128)(2,1)S(1)}, u32[]{:S(2)}, u32[]{:S(2)}) %collective-permute-start.17) | collective-permute-done | bytes 327712 | tf_op jit(solution)/shard_map/ppermute | solution.py:123
  213.1 5.1 %collective-permute-start.20 = (bf16[128,1280]{1,0:T(8,128)(2,1)S(1)}, bf16[128,1280]{1,0:T(8,128)(2,1)S(1)}, u32[]{:S(2)}, u32[]{:S(2)}) collective-permute-start(bf16[128,1280]{1,0:T(8,128)(2,1)S(1)} %collective-permute-done.16.refs_9_), channel_id=1, source_target_pairs={{0,6},{2,0},{4,2},{6,4},{1,7},{3,1},{5,3},{7,5},{8,14},{10,8},{12,... | collective-permute-start | bytes 983048 | tf_op jit(solution)/shard_map/ppermute | solution.py:101
  224.9 4.4 %collective-permute-start.21 = (bf16[64,1280]{1,0:T(8,128)(2,1)S(1)}, bf16[64,1280]{1,0:T(8,128)(2,1)S(1)}, u32[]{:S(2)}, u32[]{:S(2)}) collective-permute-start(bf16[64,1280]{1,0:T(8,128)(2,1)S(1)} %slice.31), channel_id=1, source_target_pairs={{0,8},{8,0},{1,9},{9,1},{2,10},{10,2},{3,11},{11,3},{4,12},{12,4},... | collective-permute-start | bytes 491528 | tf_op jit(solution)/shard_map/ppermute | solution.py:123
  234.1 5.3 %collective-permute-done.22.refs_15_ = bf16[64,1280]{1,0:T(8,128)(2,1)S(1)} collective-permute-done((bf16[64,1280]{1,0:T(8,128)(2,1)S(1)}, bf16[64,1280]{1,0:T(8,128)(2,1)S(1)}, u32[]{:S(2)}, u32[]{:S(2)}) %collective-permute-start.22) | collective-permute-done | bytes 163872 | tf_op jit(solution)/shard_map/ppermute | solution.py:101
  244.3 6.4 %shard_map.98 = bf16[2688,128]{1,0:T(8,128)(2,1)} custom-call(bf16[2,4,128,512]{3,2,1,0:T(8,128)(2,1)} %get-tuple-element.58.keep.refs_0_, bf16[2,4,128,512]{3,2,1,0:T(8,128)(2,1)} %collective-permute-done.3.other.refs_1_, bf16[8,128,512]{2,1,0:T(8,128)(2,1)} %copy-done.6, bf16[6,128,512]{2,1,0:T(8,128)(2,1)} %copy-done.13, bf16[6,128,512]{2,1,0:T(8,128)(2,1)} %copy-done.14, ...), custom_call_target="tpu_custom_call" | custom-call | flops 1342177280 | bytes 7340032 | tf_op jit(solution)/shard_map/pallas_call | solution.py:358
  250.7 47.7 %all_to_all.20 = bf16[48,56,128]{2,1,0:T(8,128)(2,1)S(1)} all-to-all(bf16[48,56,128]{2,1,0:T(8,128)(2,1)} %bitcast.58), channel_id=1, replica_groups=mesh['z'=12,'yh'=4,'yl'=2,'x'=4,'core'=2] {'z','yh'}, dimensions={0} | all-to-all | bytes 1376256 | tf_op jit(solution)/shard_map/all_to_all | solution.py:517
  299.4 5.0 %all-to-all-start.3 = ((bf16[48,56,128]{2,1,0:T(8,128)(2,1)}), bf16[48,56,128]{2,1,0:T(8,128)(2,1)S(1)}, u32[]{:S(2)}, u32[]{:S(2)}) async-start(bf16[48,56,128]{2,1,0:T(8,128)(2,1)} %broadcast_in_dim.55), calls=%async_computation.3 | async-start | bytes 1376256 | tf_op jit(solution)/shard_map/all_to_all | solution.py:517
  305.1 10.2 %shard_map.99 = (bf16[128,4096]{1,0:T(8,128)(2,1)}, bf16[128,4096]{1,0:T(8,128)(2,1)}) custom-call(s32[16]{0:T(128)} %concatenate.28.places, bf16[128,1280]{1,0:T(8,128)(2,1)} %copy-done.7, bf16[128,4096]{1,0:T(8,128)(2,1)} %bitcast.56, bf16[128,4096]{1,0:T(8,128)(2,1)} %bitcast.54, bf16[256,1280]{1,0:T(8,128)(2,1)} %copy-done.2, ...), custom_call_target="tpu_custom_call" | custom-call | flops 1342177280 | bytes 10485760 | tf_op jit(solution)/shard_map/pallas_call | solution.py:358
  315.3 22.3 %all-to-all-done.3 = bf16[48,56,128]{2,1,0:T(8,128)(2,1)S(1)} async-done(((bf16[48,56,128]{2,1,0:T(8,128)(2,1)}), bf16[48,56,128]{2,1,0:T(8,128)(2,1)S(1)}, u32[]{:S(2)}, u32[]{:S(2)}) %all-to-all-start.3) | async-done | bytes 688160 | tf_op jit(solution)/shard_map/all_to_all | solution.py:517
  (143 shorter events, 69.4 us)
Async XLA Ops:
  2.7 22.0 %collective-permute-start = (bf16[256,1280]{1,0:T(8,128)(2,1)S(1)}, bf16[256,1280]{1,0:T(8,128)(2,1)S(1)}, u32[]{:S(2)}, u32[]{:S(2)}) collective-permute-start(bf16[256,1280]{1,0:T(8,128)(2,1)S(1)} %constant_dynamic-update-slice_fusion.refs_0_), channel_id=1, source_target_pairs={{0,1},{1,0},{2,3},{3,2},{4,5},{5,4},{6,7},{7,6},{8,9},{9,8},{10,11... | collective-permute-start | bytes 1966088 | tf_op jit(solution)/shard_map/ppermute | solution.py:127
  4.6 27.0 %collective-permute-start.2 = (bf16[256,1280]{1,0:T(8,128)(2,1)S(1)}, bf16[256,1280]{1,0:T(8,128)(2,1)}, u32[]{:S(2)}, u32[]{:S(2)}) collective-permute-start(bf16[256,1280]{1,0:T(8,128)(2,1)S(1)} %constant_dynamic-update-slice_fusion.refs_0_), channel_id=1, source_target_pairs={{0,8},{1,57},{8,16},{9,1},{16,24},{17,9},{24,32},{25,17},{32,40},{... | collective-permute-start | bytes 1966088 | tf_op jit(solution)/shard_map/ppermute | solution.py:119
  12.6 16.8 %collective-permute-start.3 = (bf16[2,4,128,512]{3,2,1,0:T(8,128)(2,1)}, bf16[2,4,128,512]{3,2,1,0:T(8,128)(2,1)}, u32[]{:S(2)}, u32[]{:S(2)}) collective-permute-start(bf16[2,4,128,512]{3,2,1,0:T(8,128)(2,1)} %get-tuple-element.40), channel_id=1, source_target_pairs={{0,1},{1,0},{2,3},{3,2},{4,5},{5,4},{6,7},{7,6},{8,9},{9,8},{10,11... | collective-permute-start | bytes 3145736 | tf_op jit(solution)/shard_map/ppermute | solution.py:127
  26.7 20.9 %collective-permute-start.1 = (bf16[512,1280]{1,0:T(8,128)(2,1)}, bf16[512,1280]{1,0:T(8,128)(2,1)S(1)}, u32[]{:S(2)}, u32[]{:S(2)}) collective-permute-start(bf16[512,1280]{1,0:T(8,128)(2,1)} %pad_maximum_fusion.2), channel_id=1, source_target_pairs={{0,2},{1,7},{2,4},{3,1},{4,6},{5,3},{6,0},{7,5},{8,10},{9,15},{10,... | collective-permute-start | bytes 3932168 | tf_op jit(solution)/shard_map/ppermute | solution.py:110
  29.4 89.0 %copy-start.27 = (s32[192]{0:T(256)}, s32[192]{0:T(256)S(1)}, u32[]{:S(2)}) copy-start(s32[192]{0:T(256)S(1)} %add.446) | copy-start | bytes 2308
  50.9 7.4 %collective-permute-start.5 = (bf16[768,1280]{1,0:T(8,128)(2,1)}, bf16[768,1280]{1,0:T(8,128)(2,1)}, u32[]{:S(2)}, u32[]{:S(2)}) collective-permute-start(bf16[768,1280]{1,0:T(8,128)(2,1)} %pad_maximum_fusion), channel_id=1, source_target_pairs={{0,1},{1,0},{2,3},{3,2},{4,5},{5,4},{6,7},{7,6},{8,9},{9,8},{10,11... | collective-permute-start | bytes 5898248 | tf_op jit(solution)/shard_map/ppermute | solution.py:127
  52.8 19.5 %collective-permute-start.6 = (bf16[512,1280]{1,0:T(8,128)(2,1)S(1)}, bf16[512,1280]{1,0:T(8,128)(2,1)S(1)}, u32[]{:S(2)}, u32[]{:S(2)}) collective-permute-start(bf16[512,1280]{1,0:T(8,128)(2,1)S(1)} %collective-permute-done.1.refs_2_), channel_id=1, source_target_pairs={{0,8},{1,57},{8,16},{9,1},{16,24},{17,9},{24,32},{25,17},{32,40},{... | collective-permute-start | bytes 3932168 | tf_op jit(solution)/shard_map/ppermute | solution.py:119
  55.7 13.9 %collective-permute-start.4 = (bf16[256,1280]{1,0:T(8,128)(2,1)}, bf16[256,1280]{1,0:T(8,128)(2,1)S(1)}, u32[]{:S(2)}, u32[]{:S(2)}) collective-permute-start(bf16[256,1280]{1,0:T(8,128)(2,1)} %slice.23), channel_id=1, source_target_pairs={{0,2},{1,7},{2,4},{3,1},{4,6},{5,3},{6,0},{7,5},{8,10},{9,15},{10,... | collective-permute-start | bytes 1966088 | tf_op jit(solution)/shard_map/ppermute | solution.py:110
  73.9 18.4 %collective-permute-start.8 = (bf16[768,1280]{1,0:T(8,128)(2,1)}, bf16[768,1280]{1,0:T(8,128)(2,1)}, u32[]{:S(2)}, u32[]{:S(2)}) collective-permute-start(bf16[768,1280]{1,0:T(8,128)(2,1)} %pad_maximum_fusion.1), channel_id=1, source_target_pairs={{0,1},{1,0},{2,3},{3,2},{4,5},{5,4},{6,7},{7,6},{8,9},{9,8},{10,11... | collective-permute-start | bytes 5898248 | tf_op jit(solution)/shard_map/ppermute | solution.py:127
  75.8 12.5 %collective-permute-start.7 = (bf16[256,1280]{1,0:T(8,128)(2,1)S(1)}, bf16[256,1280]{1,0:T(8,128)(2,1)S(1)}, u32[]{:S(2)}, u32[]{:S(2)}) collective-permute-start(bf16[256,1280]{1,0:T(8,128)(2,1)S(1)} %collective-permute-done.4.refs_1_.refs_6_), channel_id=1, source_target_pairs={{0,8},{1,57},{8,16},{9,1},{16,24},{17,9},{24,32},{25,17},{32,40},{... | collective-permute-start | bytes 1966088 | tf_op jit(solution)/shard_map/ppermute | solution.py:119
  88.3 4.0 %collective-permute-start.9 = (bf16[256,1280]{1,0:T(8,128)(2,1)S(1)}, bf16[256,1280]{1,0:T(8,128)(2,1)S(1)}, u32[]{:S(2)}, u32[]{:S(2)}) collective-permute-start(bf16[256,1280]{1,0:T(8,128)(2,1)S(1)} %collective-permute-done.7.refs_2_.refs_7_), channel_id=1, source_target_pairs={{0,1},{1,0},{2,3},{3,2},{4,5},{5,4},{6,7},{7,6},{8,9},{9,8},{10,11... | collective-permute-start | bytes 1966088 | tf_op jit(solution)/shard_map/ppermute | solution.py:127
  100.7 41.0 %all-to-all-start = ((bf16[48,4,1408]{2,1,0:T(4,128)(2,1)}), bf16[48,4,1408]{2,1,0:T(4,128)(2,1)S(1)}, u32[]{:S(2)}, u32[]{:S(2)}) async-start(bf16[48,4,1408]{2,1,0:T(4,128)(2,1)} %reshape.98), calls=%async_computation | async-start | bytes 1081344 | tf_op jit(solution)/shard_map/all_to_all | solution.py:517
  112.8 42.2 %collective-permute-start.10 = (bf16[8,128,512]{2,1,0:T(8,128)(2,1)S(1)}, bf16[8,128,512]{2,1,0:T(8,128)(2,1)S(1)}, u32[]{:S(2)}, u32[]{:S(2)}) collective-permute-start(bf16[8,128,512]{2,1,0:T(8,128)(2,1)S(1)} %copy-done.19), channel_id=1, source_target_pairs={{0,8},{8,0},{1,9},{9,1},{2,10},{10,2},{3,11},{11,3},{4,12},{12,4},... | collective-permute-start | bytes 3145736 | tf_op jit(solution)/shard_map/ppermute | solution.py:123
  150.0 42.3 %all-to-all-start.1 = ((bf16[48,4,1280]{2,1,0:T(4,128)(2,1)}), bf16[48,4,1280]{2,1,0:T(4,128)(2,1)S(1)}, u32[]{:S(2)}, u32[]{:S(2)}) async-start(bf16[48,4,1280]{2,1,0:T(4,128)(2,1)} %reshape.100), calls=%async_computation.1 | async-start | bytes 983040 | tf_op jit(solution)/shard_map/all_to_all | solution.py:517
  159.1 22.1 %collective-permute-start.11 = (bf16[6,128,512]{2,1,0:T(8,128)(2,1)}, bf16[6,128,512]{2,1,0:T(8,128)(2,1)S(1)}, u32[]{:S(2)}, u32[]{:S(2)}) collective-permute-start(bf16[6,128,512]{2,1,0:T(8,128)(2,1)} %get-tuple-element.56), channel_id=1, source_target_pairs={{0,2},{2,4},{4,6},{6,0},{1,3},{3,5},{5,7},{7,1},{8,10},{10,12},{12... | collective-permute-start | bytes 2359304 | tf_op jit(solution)/shard_map/ppermute | solution.py:101
  161.3 21.9 %collective-permute-start.12 = (bf16[6,128,512]{2,1,0:T(8,128)(2,1)}, bf16[6,128,512]{2,1,0:T(8,128)(2,1)S(1)}, u32[]{:S(2)}, u32[]{:S(2)}) collective-permute-start(bf16[6,128,512]{2,1,0:T(8,128)(2,1)} %get-tuple-element.57), channel_id=1, source_target_pairs={{0,6},{2,0},{4,2},{6,4},{1,7},{3,1},{5,3},{7,5},{8,14},{10,8},{12,... | collective-permute-start | bytes 2359304 | tf_op jit(solution)/shard_map/ppermute | solution.py:101
  181.3 9.8 %collective-permute-start.13 = (bf16[2,128,512]{2,1,0:T(8,128)(2,1)S(1)}, bf16[2,128,512]{2,1,0:T(8,128)(2,1)S(1)}, u32[]{:S(2)}, u32[]{:S(2)}) collective-permute-start(bf16[2,128,512]{2,1,0:T(8,128)(2,1)S(1)} %slice.29), channel_id=1, source_target_pairs={{0,2},{2,4},{4,6},{6,0},{1,3},{3,5},{5,7},{7,1},{8,10},{10,12},{12... | collective-permute-start | bytes 786440 | tf_op jit(solution)/shard_map/ppermute | solution.py:101
  183.2 9.1 %collective-permute-start.14 = (bf16[2,128,512]{2,1,0:T(8,128)(2,1)S(1)}, bf16[2,128,512]{2,1,0:T(8,128)(2,1)}, u32[]{:S(2)}, u32[]{:S(2)}) collective-permute-start(bf16[2,128,512]{2,1,0:T(8,128)(2,1)S(1)} %slice.30), channel_id=1, source_target_pairs={{0,6},{2,0},{4,2},{6,4},{1,7},{3,1},{5,3},{7,5},{8,14},{10,8},{12,... | collective-permute-start | bytes 786440 | tf_op jit(solution)/shard_map/ppermute | solution.py:101
  192.7 38.5 %copy-start.7 = (bf16[128,1280]{1,0:T(8,128)(2,1)}, bf16[128,1280]{1,0:T(8,128)(2,1)S(1)}, u32[]{:S(2)}) copy-start(bf16[128,1280]{1,0:T(8,128)(2,1)S(1)} %convolution_convert_fusion.refs_7_.both) | copy-start | bytes 983044
  192.7 12.4 %collective-permute-start.16 = (bf16[128,1280]{1,0:T(8,128)(2,1)S(1)}, bf16[128,1280]{1,0:T(8,128)(2,1)S(1)}, u32[]{:S(2)}, u32[]{:S(2)}) collective-permute-start(bf16[128,1280]{1,0:T(8,128)(2,1)S(1)} %convolution_convert_fusion.refs_7_.both), channel_id=1, source_target_pairs={{0,6},{2,0},{4,2},{6,4},{1,7},{3,1},{5,3},{7,5},{8,14},{10,8},{12,... | collective-permute-start | bytes 983048 | tf_op jit(solution)/shard_map/ppermute | solution.py:101
  198.4 12.8 %collective-permute-start.17 = (bf16[128,1280]{1,0:T(8,128)(2,1)S(1)}, bf16[128,1280]{1,0:T(8,128)(2,1)S(1)}, u32[]{:S(2)}, u32[]{:S(2)}) collective-permute-start(bf16[128,1280]{1,0:T(8,128)(2,1)S(1)} %convolution_convert_fusion.refs_7_.both), channel_id=1, source_target_pairs={{0,8},{8,0},{1,9},{9,1},{2,10},{10,2},{3,11},{11,3},{4,12},{12,4},... | collective-permute-start | bytes 983048 | tf_op jit(solution)/shard_map/ppermute | solution.py:123
  203.2 15.1 %collective-permute-start.15 = (bf16[128,1280]{1,0:T(8,128)(2,1)S(1)}, bf16[128,1280]{1,0:T(8,128)(2,1)S(1)}, u32[]{:S(2)}, u32[]{:S(2)}) collective-permute-start(bf16[128,1280]{1,0:T(8,128)(2,1)S(1)} %convolution_convert_fusion.refs_7_.both), channel_id=1, source_target_pairs={{0,2},{2,4},{4,6},{6,0},{1,3},{3,5},{5,7},{7,1},{8,10},{10,12},{12... | collective-permute-start | bytes 983048 | tf_op jit(solution)/shard_map/ppermute | solution.py:101
  205.2 15.2 %collective-permute-start.18 = (bf16[128,1280]{1,0:T(8,128)(2,1)S(1)}, bf16[128,1280]{1,0:T(8,128)(2,1)S(1)}, u32[]{:S(2)}, u32[]{:S(2)}) collective-permute-start(bf16[128,1280]{1,0:T(8,128)(2,1)S(1)} %collective-permute-done.16.refs_9_), channel_id=1, source_target_pairs={{0,8},{8,0},{1,9},{9,1},{2,10},{10,2},{3,11},{11,3},{4,12},{12,4},... | collective-permute-start | bytes 983048 | tf_op jit(solution)/shard_map/ppermute | solution.py:123
  211.2 10.2 %collective-permute-start.19 = (bf16[128,1280]{1,0:T(8,128)(2,1)S(1)}, bf16[128,1280]{1,0:T(8,128)(2,1)S(1)}, u32[]{:S(2)}, u32[]{:S(2)}) collective-permute-start(bf16[128,1280]{1,0:T(8,128)(2,1)S(1)} %collective-permute-done.17.refs_10_), channel_id=1, source_target_pairs={{0,2},{2,4},{4,6},{6,0},{1,3},{3,5},{5,7},{7,1},{8,10},{10,12},{12... | collective-permute-start | bytes 983048 | tf_op jit(solution)/shard_map/ppermute | solution.py:101
  213.1 9.7 %collective-permute-start.20 = (bf16[128,1280]{1,0:T(8,128)(2,1)S(1)}, bf16[128,1280]{1,0:T(8,128)(2,1)S(1)}, u32[]{:S(2)}, u32[]{:S(2)}) collective-permute-start(bf16[128,1280]{1,0:T(8,128)(2,1)S(1)} %collective-permute-done.16.refs_9_), channel_id=1, source_target_pairs={{0,6},{2,0},{4,2},{6,4},{1,7},{3,1},{5,3},{7,5},{8,14},{10,8},{12,... | collective-permute-start | bytes 983048 | tf_op jit(solution)/shard_map/ppermute | solution.py:101
  218.4 24.8 %collective-permute-start.24 = (bf16[384,1280]{1,0:T(8,128)(2,1)S(1)}, bf16[384,1280]{1,0:T(8,128)(2,1)S(1)}, u32[]{:S(2)}, u32[]{:S(2)}) collective-permute-start(bf16[384,1280]{1,0:T(8,128)(2,1)S(1)} %pad_maximum_fusion.4), channel_id=1, source_target_pairs={{0,1},{1,0},{2,3},{3,2},{4,5},{5,4},{6,7},{7,6},{8,9},{9,8},{10,11... | collective-permute-start | bytes 2949128 | tf_op jit(solution)/shard_map/ppermute | solution.py:127
  222.9 21.3 %collective-permute-start.25 = (bf16[384,1280]{1,0:T(8,128)(2,1)S(1)}, bf16[384,1280]{1,0:T(8,128)(2,1)}, u32[]{:S(2)}, u32[]{:S(2)}) collective-permute-start(bf16[384,1280]{1,0:T(8,128)(2,1)S(1)} %pad_maximum_fusion.5), channel_id=1, source_target_pairs={{0,1},{1,0},{2,3},{3,2},{4,5},{5,4},{6,7},{7,6},{8,9},{9,8},{10,11... | collective-permute-start | bytes 2949128 | tf_op jit(solution)/shard_map/ppermute | solution.py:127
  224.9 9.2 %collective-permute-start.21 = (bf16[64,1280]{1,0:T(8,128)(2,1)S(1)}, bf16[64,1280]{1,0:T(8,128)(2,1)S(1)}, u32[]{:S(2)}, u32[]{:S(2)}) collective-permute-start(bf16[64,1280]{1,0:T(8,128)(2,1)S(1)} %slice.31), channel_id=1, source_target_pairs={{0,8},{8,0},{1,9},{9,1},{2,10},{10,2},{3,11},{11,3},{4,12},{12,4},... | collective-permute-start | bytes 491528 | tf_op jit(solution)/shard_map/ppermute | solution.py:123
  229.3 10.2 %collective-permute-start.22 = (bf16[64,1280]{1,0:T(8,128)(2,1)S(1)}, bf16[64,1280]{1,0:T(8,128)(2,1)S(1)}, u32[]{:S(2)}, u32[]{:S(2)}) collective-permute-start(bf16[64,1280]{1,0:T(8,128)(2,1)S(1)} %slice.32), channel_id=1, source_target_pairs={{0,2},{2,4},{4,6},{6,0},{1,3},{3,5},{5,7},{7,1},{8,10},{10,12},{12... | collective-permute-start | bytes 491528 | tf_op jit(solution)/shard_map/ppermute | solution.py:101
  231.2 10.4 %collective-permute-start.23 = (bf16[128,1280]{1,0:T(8,128)(2,1)S(1)}, bf16[128,1280]{1,0:T(8,128)(2,1)S(1)}, u32[]{:S(2)}, u32[]{:S(2)}) collective-permute-start(bf16[128,1280]{1,0:T(8,128)(2,1)S(1)} %convolution_convert_fusion.refs_7_.both), channel_id=1, source_target_pairs={{0,1},{1,0},{2,3},{3,2},{4,5},{5,4},{6,7},{7,6},{8,9},{9,8},{10,11... | collective-permute-start | bytes 983048 | tf_op jit(solution)/shard_map/ppermute | solution.py:127
  239.5 3.7 %collective-permute-start.26 = (bf16[128,1280]{1,0:T(8,128)(2,1)S(1)}, bf16[128,1280]{1,0:T(8,128)(2,1)S(1)}, u32[]{:S(2)}, u32[]{:S(2)}) collective-permute-start(bf16[128,1280]{1,0:T(8,128)(2,1)S(1)} %pad_maximum_fusion.6), channel_id=1, source_target_pairs={{0,1},{1,0},{2,3},{3,2},{4,5},{5,4},{6,7},{7,6},{8,9},{9,8},{10,11... | collective-permute-start | bytes 983048 | tf_op jit(solution)/shard_map/ppermute | solution.py:127
  299.4 38.2 %all-to-all-start.3 = ((bf16[48,56,128]{2,1,0:T(8,128)(2,1)}), bf16[48,56,128]{2,1,0:T(8,128)(2,1)S(1)}, u32[]{:S(2)}, u32[]{:S(2)}) async-start(bf16[48,56,128]{2,1,0:T(8,128)(2,1)} %broadcast_in_dim.55), calls=%async_computation.3 | async-start | bytes 1376256 | tf_op jit(solution)/shard_map/all_to_all | solution.py:517
  (28 other events, 380.5 us)

commit v4 on v3

--- a/solution.py
+++ b/solution.py
@@ -23,11 +23,11 @@
     normed[...] = (values * lax.rsqrt(squares / width + 1e-05)).astype(jnp.bfloat16)
     number = 0
     for out in (keep, send):
-        for dy in range(out.shape[0]):
-            for dx in range(out.shape[1]):
+        for dx in range(out.shape[0]):
+            for dy in range(out.shape[1]):
                 columns = pl.ds(pl.multiple_of(places[number] * share, 128), share)
-                out[dy, dx, :, :share] = normed[:, columns]
-                out[dy, dx, :, share:] = cot[:, columns]
+                out[dx, dy, :, :share] = normed[:, columns]
+                out[dx, dy, :, share:] = cot[:, columns]
                 number += 1
 
 
@@ -134,132 +134,131 @@
     return ((yl * lax.axis_size("x") + x) * 2 + core).astype(jnp.int32)
 
 
-def label_blocks(groups):
-    arrays, pieces, places = [], [], []
-    for dc, array, parts in groups:
-        row = 0
-        for dx, dy, sub, rows in parts:
-            pieces.append((len(arrays), row, sub, rows))
-            places.append((dx % 4, dy, dc))
-            row += rows
-        arrays.append(array)
-    return (arrays, pieces, places)
-
-
 def place_all(offsets):
     return jnp.stack([place(*offset) for offset in offsets])
 
 
-def pack_kernel(keep, other, across, up, down):
-    half = across.shape[0] // 2
-    for out, dx, tail in ((up, 1, (keep[0, 2], other[0, 2])), (down, 3, (across[2], across[half + 2]))):
-        out[0] = keep[0, dx]
-        out[1] = other[0, dx]
-        out[2] = across[dx]
-        out[3] = across[half + dx]
-        out[4] = tail[0]
-        out[5] = tail[1]
-
-
-def spread_cols(keep, other, ahead):
+def pack_x_kernel(keep, other, up, down):
+    up[0] = keep[1]
+    up[1] = other[1]
+    up[2] = keep[2]
+    down[0] = keep[3]
+    down[1] = other[3]
+    down[2] = other[2]
+
+
+def pack_y_kernel(keep, other, up, down, far_up, far_down, out):
+    out[0] = keep[0, 1]
+    out[1] = other[0, 1]
+    out[2] = up[0, 1]
+    out[3] = up[1, 1]
+    out[4] = down[0, 1]
+    out[5] = down[1, 1]
+    out[6] = far_up[1]
+    out[7] = far_down[1]
+
+
+def spread_cols(keep, other, up, down):
     piece = keep.shape[2:]
-    across = swap_y(ahead)
-    up, down = call(
-        pack_kernel,
+    up = shift_x(up, 1)
+    down = shift_x(down, -1)
+    far_up = shift_x(up[2], 1)
+    far_down = shift_x(down[2], -1)
+    arrays = [keep, other, up, down, far_up, far_down]
+    packed = call(
+        pack_y_kernel,
         None,
-        [keep, other, across],
-        [jax.ShapeDtypeStruct((6, *piece), jnp.bfloat16)] * 2,
+        arrays,
+        jax.ShapeDtypeStruct((8, *piece), jnp.bfloat16),
         [],
         keep.size,
-        12 * keep.size,
-    )
-    up = shift_x(up, 1)
-    down = shift_x(down, -1)
-    far_up = shift_x(up[4:], 1)
-    far_down = shift_x(down[4:], -1)
-    sources = [(0, 0), (0, 1), (1, 0), (1, 1)]
-    arrays = [keep, other, across, up, down, far_up, far_down]
-    pieces = [(0, (0, 0), (0, 0, 0)), (1, (0, 0), (0, 0, 1))]
-    pieces += [(2, (0,), (0, 1, 0)), (2, (4,), (0, 1, 1))]
-    pieces += [(3, (number,), (3, *source)) for number, source in enumerate(sources)]
-    pieces += [(4, (number,), (1, *source)) for number, source in enumerate(sources)]
-    pieces += [(5, (number,), (2, *source)) for number, source in enumerate(sources[:2])]
-    pieces += [(6, (number,), (2, *source)) for number, source in enumerate(sources[2:])]
-    return (arrays, pieces)
+        4 * keep.size,
+    )
+    across = swap_y(packed)
+    here = [(0, (0,), 0, 0), (1, (0,), 0, 1), (2, (0,), 3, 0), (2, (1,), 3, 1)]
+    here += [(3, (0,), 1, 0), (3, (1,), 1, 1), (4, (), 2, 0), (5, (), 2, 1)]
+    pieces = [(which, (*index, 0), (dx, 0, dc)) for which, index, dx, dc in here]
+    pieces += [(6, (at,), (dx, 1, dc)) for at, (_, _, dx, dc) in enumerate(here)]
+    return (arrays + [across], pieces)
 
 
 def gather_weights(block, first_dot, beside):
-    rows = block.shape[0]
     sign = 1 - 2 * lax.axis_index("core")
+    near = along_x(block)
+    across = along_y(block)
     other_0 = swap_core(block)
-    across = along_y(block)
-    chip = jnp.concatenate([block, other_0], axis=0)
-    side = along_x(chip)
-    side, across, beside = lax.optimization_barrier((side, across, beside))
-    side_y = along_y(side)
-    far = along_x(side[:rows])
-    other_1 = swap_core(jnp.concatenate([side, across], axis=0))
+    next_block = along_x(other_0)
+    side_a = along_y(near)
+    far = along_x(near)
+    next_block, beside = lax.optimization_barrier((next_block, beside))
+    side_b = along_y(next_block)
+    far_y = along_x(side_a)
+    other_1 = swap_core(jnp.concatenate([near, next_block, across], axis=0))
     groups = [
         (block, [(0, 0, 0)]),
         (other_0, [(0, 0, 1)]),
-        (side, [(-sign, 0, 0), (-sign, 0, 1)]),
+        (near, [(-sign, 0, 0)]),
+        (next_block, [(-sign, 0, 1)]),
         (across, [(0, 1, 0)]),
         (other_1, [(sign, 0, 1), (sign, 0, 0), (0, 1, 1)]),
     ]
-    early = number_blocks(groups, rows)
+    early = number_blocks(groups, place)
     total = first_dot(beside, *early)
-    far, total = lax.optimization_barrier((far, total))
-    far_y = along_y(far)
-    other_2 = swap_core(jnp.concatenate([side_y, far], axis=0))
+    other_2 = swap_core(jnp.concatenate([side_a, side_b, far], axis=0))
+    far_y, total = lax.optimization_barrier((far_y, total))
     other_3 = swap_core(far_y)
     groups = [
-        (side_y, [(-sign, 1, 0), (-sign, 1, 1)]),
+        (side_a, [(-sign, 1, 0)]),
+        (side_b, [(-sign, 1, 1)]),
         (far, [(2, 0, 0)]),
         (far_y, [(2, 1, 0)]),
         (other_2, [(sign, 1, 1), (sign, 1, 0), (2, 0, 1)]),
         (other_3, [(2, 1, 1)]),
     ]
-    return (early, number_blocks(groups, rows), total, beside)
-
-
-def number_blocks(groups, rows):
+    return (early, number_blocks(groups, place), total, beside)
+
+
+def row_slot(dx, dy, dc):
+    return jnp.asarray((dc * 2 + dy) * 4 + dx % 4, jnp.int32)
+
+
+def gather_rows(block):
+    sign = 1 - 2 * lax.axis_index("core")
+    near = along_x(block)
+    across = swap_y(block)
+    other_0 = swap_core(block)
+    next_block = along_x(other_0)
+    side_a = along_x(across)
+    far = along_x(near)
+    side_b = swap_y(next_block)
+    far_y = along_x(side_a)
+    other_1 = swap_core(jnp.concatenate([near, next_block, across], axis=0))
+    other_2 = swap_core(jnp.concatenate([side_a, side_b, far, far_y], axis=0))
+    groups = [
+        (block, [(0, 0, 0)]),
+        (other_0, [(0, 0, 1)]),
+        (near, [(-sign, 0, 0)]),
+        (next_block, [(-sign, 0, 1)]),
+        (across, [(0, 1, 0)]),
+        (other_1, [(sign, 0, 1), (sign, 0, 0), (0, 1, 1)]),
+        (side_a, [(-sign, 1, 0)]),
+        (side_b, [(-sign, 1, 1)]),
+        (far, [(2, 0, 0)]),
+        (far_y, [(2, 1, 0)]),
+        (other_2, [(sign, 1, 1), (sign, 1, 0), (2, 0, 1), (2, 1, 1)]),
+    ]
+    return number_blocks(groups, row_slot)
+
+
+def number_blocks(groups, numbering):
     arrays, pieces, places = [], [], []
+    rows = groups[0][0].shape[0]
     for array, offsets in groups:
         for number, offset in enumerate(offsets):
             pieces.append((len(arrays), number * rows, 0, rows))
-            places.append(place(*offset))
+            places.append(numbering(*offset))
         arrays.append(array)
     return (arrays, pieces, jnp.stack(places))
-
-
-def gather_rows(block):
-    half = block.shape[0] // 2
-    full = 2 * half
-    left = shift_x(block, 1)
-    right = shift_x(block, -1)
-    across = swap_y(block)
-    other_0 = swap_core(block)
-    right_y = swap_y(right)
-    left_y = shift_x(across, 1)
-    far = shift_x(right, -1)
-    other_1 = swap_core(jnp.concatenate([left, right, across], axis=0))
-    far_y_a = swap_y(far[:half])
-    far_y_b = shift_x(left_y[half:], 1)
-    other_2 = swap_core(jnp.concatenate([right_y, left_y, far], axis=0))
-    other_3 = swap_core(jnp.concatenate([far_y_a, far_y_b], axis=0))
-    parts_1 = [(-1, 0, 0, full), (1, 0, 0, full), (0, 1, 0, full)]
-    parts_2 = [(1, 1, 0, full), (-1, 1, 0, full), (2, 0, 0, full)]
-    parts_3 = [(2, 1, 0, half), (2, 1, half, half)]
-    mine = [block, left, right, across, right_y, left_y, far, far_y_a, far_y_b]
-    own_parts = [(0, 0, 0, full)] + parts_1 + parts_2 + parts_3
-    groups = [(0, array, [part]) for array, part in zip(mine, own_parts)]
-    groups += [
-        (1, other_0, [(0, 0, 0, full)]),
-        (1, other_1, parts_1),
-        (1, other_2, parts_2),
-        (1, other_3, parts_3),
-    ]
-    return label_blocks(groups)
 
 
 def add_products(pieces, share, split, places, normed, cot, blocks, total, fresh):
@@ -331,15 +330,16 @@
     ).astype(jnp.bfloat16)
 
 
-def weight_grad_kernel(row_pieces, col_pieces, split, *refs):
+def weight_grad_kernel(row_pieces, col_pieces, split, slots, *refs):
     inputs, (out, rows_all, cols_all) = (refs[:-3], refs[-3:])
     col_count = 1 + max(which for which, _, _ in col_pieces)
     share = cols_all.shape[1] // 2
     count = inputs[0].shape[2]
     for which, index, to in col_pieces:
         cols_all[to : to + count, :] = inputs[which][index]
-    for which, row, to, rows in row_pieces:
-        rows_all[to : to + rows, :] = inputs[col_count + which][row : row + rows, :]
+    for number, (which, row, _, rows) in enumerate(row_pieces):
+        where = pl.ds(pl.multiple_of(slots[number] * count, 128), rows)
+        rows_all[where, :] = inputs[col_count + which][row : row + rows, :]
     first = contract_rows(cols_all[:, :share], rows_all[:, :split]).astype(jnp.bfloat16)
     second = contract_rows(cols_all[:, share:], rows_all[:, split:]).astype(jnp.bfloat16)
     step = 128
@@ -401,8 +401,8 @@
 
     width = qkv_width + out_width
     share = model_width // owners
-    order = [(dx, dy, dc) for dc in range(2) for dy in range(2) for dx in range(4)]
-    piece = jax.ShapeDtypeStruct((2, 4, row_count, 2 * share), jnp.bfloat16)
+    order = [(dx, dy, dc) for dc in range(2) for dx in range(4) for dy in range(2)]
+    piece = jax.ShapeDtypeStruct((4, 2, row_count, 2 * share), jnp.bfloat16)
     normed_b, keep, send = call(
         prepare_kernel,
         place_all(order),
@@ -419,7 +419,15 @@
     slot_ids = jnp.arange(slot_count, dtype=jnp.int32)[None, :]
     position = ((source_ids - my_start) % groups + groups * slot_ids).reshape(total_slots)
     other = swap_core(send)
-    ahead = jnp.concatenate([keep[1], other[1]], axis=0)
+    up, down = call(
+        pack_x_kernel,
+        None,
+        [keep, other],
+        [jax.ShapeDtypeStruct((3, *piece.shape[1:]), jnp.bfloat16)] * 2,
+        [],
+        keep.size,
+        6 * keep.size,
+    )
 
     def first_dot(beside, arrays, pieces, places):
         return call(
@@ -435,9 +443,9 @@
     early, late, begun, beside = gather_weights(
         jnp.concatenate([qkv_weight, out_weight], axis=1),
         first_dot,
-        (normed_b, keep, other, ahead, flag_cols, routing, position),
-    )
-    normed_b, keep, other, ahead, flag_cols, routing, position = beside
+        (normed_b, keep, other, up, down, flag_cols, routing, position),
+    )
+    normed_b, keep, other, up, down, flag_cols, routing, position = beside
     slots = call(
         functools.partial(project_kernel, late[1], share, qkv_width),
         late[2],
@@ -450,9 +458,9 @@
     blocks = [*early[0], *late[0]]
     pieces = early[1] + [(len(early[0]) + which, *rest) for which, *rest in late[1]]
     places = jnp.concatenate([early[2], late[2]])
-    slots, keep, other, ahead = lax.optimization_barrier((slots, keep, other, ahead))
+    slots, keep, other, up, down = lax.optimization_barrier((slots, keep, other, up, down))
     got = swap_dp(slots.reshape(groups, slot_count, width + 128))
-    cols, col_pieces = spread_cols(keep, other, ahead)
+    cols, col_pieces = spread_cols(keep, other, up, down)
     got = got.reshape(total_slots, width + 128)
     both = call(
         functools.partial(attention_kernel, QH),
@@ -466,17 +474,15 @@
     back = swap_dp(both.reshape(groups, slot_count, width))
     back, cols = lax.optimization_barrier((back, cols))
     both_rows = from_slots(back)
-    row_blocks, row_pieces, row_offsets = gather_rows(both_rows)
-    at = {offset: number * row_count for number, offset in enumerate(order)}
-    row_pieces = [
-        (which, row, at[offset] + sub, rows)
-        for (which, row, sub, rows), offset in zip(row_pieces, row_offsets)
+    row_blocks, row_pieces, row_slots = gather_rows(both_rows)
+    col_pieces = [
+        (which, index, ((dc * 2 + dy) * 4 + dx) * row_count)
+        for which, index, (dx, dy, dc) in col_pieces
     ]
-    col_pieces = [(which, index, at[offset]) for which, index, offset in col_pieces]
     each = -(-share * width // (128 * 8 * groups)) * 8
     partial = call(
         functools.partial(weight_grad_kernel, row_pieces, col_pieces, qkv_width),
-        None,
+        row_slots,
         [*cols, *row_blocks],
         jax.ShapeDtypeStruct((groups * each, 128), jnp.bfloat16),
         [

time: 342 us -> 332 us (0.971)
  waiting for transfers between devices: 114 us -> 96.8 us
  starting transfers between devices: 106 us -> 111 us
    ppermute x4 -> x3, waiting for transfers between devices: 4.19 us -> 31.9 us  [swap_y(): return lax.ppermute(array, 'yl', [(0, 1), (1, 0)])]
    ppermute x2 -> x9, starting transfers between devices: 3.82 us -> 25.5 us  [along_x(): return lax.ppermute(array, ('x', 'core'), pairs)]
    all_to_all x3, waiting for transfers between devices: 44.9 us -> 26.7 us  [swap_dp(): return lax.all_to_all(array, DP, split_axis=0, concat_axis=0, tiled=True)]
    ppermute x9 -> x4, starting transfers between devices: 30.7 us -> 14.2 us  [shift_x(): lax.ppermute(array, 'x', [(i, (i + step) % size) for i in range(size)])]
    ppermute x2 -> x9, waiting for transfers between devices: 22.4 us -> 12.6 us  [along_x(): return lax.ppermute(array, ('x', 'core'), pairs)]
    ppermute x3, waiting for transfers between devices: 13.3 us -> 4.88 us  [along_y(): return lax.ppermute(array, ('yh', 'yl', 'core'), pairs)]
    ppermute x9 -> x4, waiting for transfers between devices: 26.1 us -> 18 us  [shift_x(): lax.ppermute(array, 'x', [(i, (i + step) % size) for i in range(size)])]
    all_to_all x3, starting transfers between devices: 22.2 us -> 30.1 us  [swap_dp(): return lax.all_to_all(array, DP, split_axis=0, concat_axis=0, tiled=True)]
  transfers between devices with their start and end apart: 30 -> 30, of which waited for: 16 -> 15; matrix products, arithmetic and copies ran while one was open for 4% -> 5% of each run, Pallas kernels for 8% -> 9%
where the time goes in v4:
time: 332 us; the launch traced here: 330 us
  starting transfers between devices  111 us (33%)
  waiting for transfers between devices  96.8 us (29%)
  blocking collectives  46 us (14%)
  Pallas kernels  44.8 us (13%)
  local copies, waits for them, and re-layouts  22.5 us (7%)
  other arithmetic  7.38 us (2%)
    all_to_all x1, blocking collectives, swap_dp(): return lax.all_to_all(array, DP, split_axis=0, concat_axis=0, tiled=True)  46 us
    pallas_call x9, Pallas kernels, call(): pl.pallas_call(kernel, out_shape=out_shape, in_specs=smem + [vmem] * len(...  44.8 us
    ppermute x3, waiting for transfers between devices, swap_y(): return lax.ppermute(array, 'yl', [(0, 1), (1, 0)])  31.9 us
    all_to_all x3, starting transfers between devices, swap_dp(): return lax.all_to_all(array, DP, split_axis=0, concat_axis=0, tiled=True)  30.1 us
    all_to_all x3, waiting for transfers between devices, swap_dp(): return lax.all_to_all(array, DP, split_axis=0, concat_axis=0, tiled=True)  26.7 us
    ppermute x9, starting transfers between devices, along_x(): return lax.ppermute(array, ('x', 'core'), pairs)  25.5 us
    ppermute x8, starting transfers between devices, swap_core(): return lax.ppermute(array, 'core', [(0, 1), (1, 0)])  24.8 us
    ppermute x4, waiting for transfers between devices, shift_x(): lax.ppermute(array, 'x', [(i, (i + step) % size) for i in range(size)])  18 us
  transfers between devices with their start and end apart: 30, of which 15 were waited for; matrix products, arithmetic and copies ran while one was open for 5% of the time, Pallas kernels for 9%

profile of v4, /device:TPU:8, one launch (start us, length us, event | category | flops | bytes accessed | tf_op | source)
XLA Modules:
  0.0 330.4 jit_solution(16071433218838942517)
XLA Ops:
  6.1 3.4 %collective-permute-start.3 = (bf16[256,1280]{1,0:T(8,128)(2,1)}, bf16[256,1280]{1,0:T(8,128)(2,1)S(1)}, u32[]{:S(2)}, u32[]{:S(2)}) collective-permute-start(bf16[256,1280]{1,0:T(8,128)(2,1)} %constant_dynamic-update-slice_fusion.refs_0_), channel_id=1, source_target_pairs={{0,2},{1,7},{2,4},{3,1},{4,6},{5,3},{6,0},{7,5},{8,10},{9,15},{10,... | collective-permute-start | bytes 1966088 | tf_op jit(solution)/shard_map/ppermute | solution.py:110
  9.5 3.5 %collective-permute-start.6 = (bf16[256,1280]{1,0:T(8,128)(2,1)}, bf16[256,1280]{1,0:T(8,128)(2,1)S(1)}, u32[]{:S(2)}, u32[]{:S(2)}) collective-permute-start(bf16[256,1280]{1,0:T(8,128)(2,1)} %constant_dynamic-update-slice_fusion.refs_0_), channel_id=1, source_target_pairs={{0,8},{1,57},{8,16},{9,1},{16,24},{17,9},{24,32},{25,17},{32,40},{... | collective-permute-start | bytes 1966088 | tf_op jit(solution)/shard_map/ppermute | solution.py:119
  13.7 3.8 %shard_map.93 = (bf16[128,4096]{1,0:T(8,128)(2,1)}, bf16[4,2,128,512]{3,2,1,0:T(8,128)(2,1)}, bf16[4,2,128,512]{3,2,1,0:T(8,128)(2,1)}) custom-call(s32[16]{0:T(128)} %stack.149.places, bf16[128,4096]{1,0:T(8,128)(2,1)} %bitcast.63, bf16[128,4096]{1,0:T(8,128)(2,1)} %bitcast.59), custom_call_target="tpu_custom_call" | custom-call | flops 2097152 | bytes 5242880 | tf_op jit(solution)/shard_map/pallas_call | solution.py:358
  17.5 8.5 %collective-permute-start.2 = (bf16[4,2,128,512]{3,2,1,0:T(8,128)(2,1)}, bf16[4,2,128,512]{3,2,1,0:T(8,128)(2,1)S(1)}, u32[]{:S(2)}, u32[]{:S(2)}) collective-permute-start(bf16[4,2,128,512]{3,2,1,0:T(8,128)(2,1)} %get-tuple-element.41), channel_id=1, source_target_pairs={{0,1},{1,0},{2,3},{3,2},{4,5},{5,4},{6,7},{7,6},{8,9},{9,8},{10,11... | collective-permute-start | bytes 3145736 | tf_op jit(solution)/shard_map/ppermute | solution.py:127
  28.0 3.6 %collective-permute-start.1 = (bf16[256,1280]{1,0:T(8,128)(2,1)}, bf16[256,1280]{1,0:T(8,128)(2,1)S(1)}, u32[]{:S(2)}, u32[]{:S(2)}) collective-permute-start(bf16[256,1280]{1,0:T(8,128)(2,1)} %collective-permute-done.refs_1_), channel_id=1, source_target_pairs={{0,2},{1,7},{2,4},{3,1},{4,6},{5,3},{6,0},{7,5},{8,10},{9,15},{10,... | collective-permute-start | bytes 1966088 | tf_op jit(solution)/shard_map/ppermute | solution.py:110
  46.1 4.1 %collective-permute-start.7 = (bf16[768,1280]{1,0:T(8,128)(2,1)}, bf16[768,1280]{1,0:T(8,128)(2,1)}, u32[]{:S(2)}, u32[]{:S(2)}) collective-permute-start(bf16[768,1280]{1,0:T(8,128)(2,1)} %pad_maximum_fusion), channel_id=1, source_target_pairs={{0,1},{1,0},{2,3},{3,2},{4,5},{5,4},{6,7},{7,6},{8,9},{9,8},{10,11... | collective-permute-start | bytes 5898248 | tf_op jit(solution)/shard_map/ppermute | solution.py:127
  50.3 4.9 %collective-permute-done.8.refs_1_.refs_7_ = bf16[256,1280]{1,0:T(8,128)(2,1)S(1)} collective-permute-done((bf16[256,1280]{1,0:T(8,128)(2,1)S(1)}, bf16[256,1280]{1,0:T(8,128)(2,1)S(1)}, u32[]{:S(2)}, u32[]{:S(2)}) %collective-permute-start.8) | collective-permute-done | bytes 655392 | tf_op jit(solution)/shard_map/ppermute | solution.py:119
  64.2 4.9 %shard_map.95.begun = f32[128,1280]{1,0:T(8,128)} custom-call(s32[8]{0:T(128)} %stack.151.places, bf16[128,4096]{1,0:T(8,128)(2,1)} %get-tuple-element.45.normed, bf16[128,4096]{1,0:T(8,128)(2,1)} %bitcast.60, bf16[256,1280]{1,0:T(8,128)(2,1)} %constant_dynamic-update-slice_fusion.refs_0_, bf16[256,1280]{1,0:T(8,128)(2,1)} %collective-permute-done.refs_1_, ...), custom_call_target="tpu_custom_call" | custom-call | flops 671088640 | bytes 5242880 | tf_op jit(solution)/shard_map/pallas_call | solution.py:358
  69.1 5.4 %collective-permute-done.5.refs_3_.refs_9_ = bf16[256,1280]{1,0:T(8,128)(2,1)S(1)} collective-permute-done((bf16[256,1280]{1,0:T(8,128)(2,1)}, bf16[256,1280]{1,0:T(8,128)(2,1)S(1)}, u32[]{:S(2)}, u32[]{:S(2)}) %collective-permute-start.5) | collective-permute-done | bytes 655392 | tf_op jit(solution)/shard_map/ppermute | solution.py:110
  80.6 5.5 %shard_map.96 = bf16[192,1408]{1,0:T(8,128)(2,1)} custom-call(s32[8]{0:T(128)} %stack.150.places, bf16[128,4096]{1,0:T(8,128)(2,1)} %get-tuple-element.45.normed, bf16[128,4096]{1,0:T(8,128)(2,1)} %bitcast.61, f32[128,1280]{1,0:T(8,128)} %shard_map.95.begun, bf16[192,128]{1,0:T(8,128)(2,1)} %fusion.routing, bf16[128,128]{1,0:T(8,128)(2,1)} %broadcast_in_dim.26.flags, ...), custom_call_target="tpu_custom_call" | custom-call | flops 671088640 | bytes 5242880 | tf_op jit(solution)/shard_map/pallas_call | solution.py:358
  88.1 14.6 %all-to-all-start = ((bf16[48,4,1408]{2,1,0:T(4,128)(2,1)}), bf16[48,4,1408]{2,1,0:T(4,128)(2,1)S(1)}, u32[]{:S(2)}, u32[]{:S(2)}) async-start(bf16[48,4,1408]{2,1,0:T(4,128)(2,1)} %reshape.98), calls=%async_computation | async-start | bytes 1081344 | tf_op jit(solution)/shard_map/all_to_all | solution.py:523
  104.7 5.1 %collective-permute-start.13 = (bf16[3,2,128,512]{3,2,1,0:T(8,128)(2,1)S(1)}, bf16[3,2,128,512]{3,2,1,0:T(8,128)(2,1)S(1)}, u32[]{:S(2)}, u32[]{:S(2)}) collective-permute-start(bf16[3,2,128,512]{3,2,1,0:T(8,128)(2,1)S(1)} %copy-done.27), channel_id=1, source_target_pairs={{0,6},{2,0},{4,2},{6,4},{1,7},{3,1},{5,3},{7,5},{8,14},{10,8},{12,... | collective-permute-start | bytes 2359304 | tf_op jit(solution)/shard_map/ppermute | solution.py:101
  111.2 14.1 %collective-permute-done.12.up.refs_2_ = bf16[3,2,128,512]{3,2,1,0:T(8,128)(2,1)S(1)} collective-permute-done((bf16[3,2,128,512]{3,2,1,0:T(8,128)(2,1)}, bf16[3,2,128,512]{3,2,1,0:T(8,128)(2,1)S(1)}, u32[]{:S(2)}, u32[]{:S(2)}) %collective-permute-start.12) | collective-permute-done | bytes 786464 | tf_op jit(solution)/shard_map/ppermute | solution.py:101
  127.3 4.3 %all-to-all-done = bf16[48,4,1408]{2,1,0:T(4,128)(2,1)S(1)} async-done(((bf16[48,4,1408]{2,1,0:T(4,128)(2,1)}), bf16[48,4,1408]{2,1,0:T(4,128)(2,1)S(1)}, u32[]{:S(2)}, u32[]{:S(2)}) %all-to-all-start) | async-done | bytes 540704 | tf_op jit(solution)/shard_map/all_to_all | solution.py:523
  132.5 5.5 %shard_map.97 = bf16[192,1280]{1,0:T(8,128)(2,1)} custom-call(s32[1]{0:T(128)} %bitcast.24.length, s32[192,1]{1,0:T(8,128)} %copy.14.place_col, s32[1,192]{1,0:T(1,128)} %bitcast.68, bf16[192,1408]{1,0:T(8,128)(2,1)} %reshape.99.got), custom_call_target="tpu_custom_call" | custom-call | flops 339738624 | bytes 983040 | tf_op jit(solution)/shard_map/pallas_call | solution.py:358
  140.0 10.3 %all-to-all-start.1 = ((bf16[48,4,1280]{2,1,0:T(4,128)(2,1)}), bf16[48,4,1280]{2,1,0:T(4,128)(2,1)S(1)}, u32[]{:S(2)}, u32[]{:S(2)}) async-start(bf16[48,4,1280]{2,1,0:T(4,128)(2,1)} %reshape.100), calls=%async_computation.1 | async-start | bytes 983040 | tf_op jit(solution)/shard_map/all_to_all | solution.py:523
  150.4 5.3 %collective-permute-start.15 = (bf16[2,128,512]{2,1,0:T(8,128)(2,1)S(1)}, bf16[2,128,512]{2,1,0:T(8,128)(2,1)S(1)}, u32[]{:S(2)}, u32[]{:S(2)}) collective-permute-start(bf16[2,128,512]{2,1,0:T(8,128)(2,1)S(1)} %slice_bitcast_fusion), channel_id=1, source_target_pairs={{0,6},{2,0},{4,2},{6,4},{1,7},{3,1},{5,3},{7,5},{8,14},{10,8},{12,... | collective-permute-start | bytes 786440 | tf_op jit(solution)/shard_map/ppermute | solution.py:101
  155.7 3.8 %collective-permute-done.15.far_down.refs_5_ = bf16[2,128,512]{2,1,0:T(8,128)(2,1)S(1)} collective-permute-done((bf16[2,128,512]{2,1,0:T(8,128)(2,1)S(1)}, bf16[2,128,512]{2,1,0:T(8,128)(2,1)S(1)}, u32[]{:S(2)}, u32[]{:S(2)}) %collective-permute-start.15) | collective-permute-done | bytes 262176 | tf_op jit(solution)/shard_map/ppermute | solution.py:101
  160.2 3.2 shard_map.98
  163.4 3.6 %collective-permute-start.16 = (bf16[8,128,512]{2,1,0:T(8,128)(2,1)}, bf16[8,128,512]{2,1,0:T(8,128)(2,1)S(1)}, u32[]{:S(2)}, u32[]{:S(2)}) collective-permute-start(bf16[8,128,512]{2,1,0:T(8,128)(2,1)} %shard_map.98), channel_id=1, source_target_pairs={{0,8},{8,0},{1,9},{9,1},{2,10},{10,2},{3,11},{11,3},{4,12},{12,4},... | collective-permute-start | bytes 3145736 | tf_op jit(solution)/shard_map/ppermute | solution.py:123
  167.0 24.4 %collective-permute-done.16.refs_6_ = bf16[8,128,512]{2,1,0:T(8,128)(2,1)S(1)} collective-permute-done((bf16[8,128,512]{2,1,0:T(8,128)(2,1)}, bf16[8,128,512]{2,1,0:T(8,128)(2,1)S(1)}, u32[]{:S(2)}, u32[]{:S(2)}) %collective-permute-start.16) | collective-permute-done | bytes 1048608 | tf_op jit(solution)/shard_map/ppermute | solution.py:123
  198.4 3.5 %collective-permute-start.19 = (bf16[128,1280]{1,0:T(8,128)(2,1)S(1)}, bf16[128,1280]{1,0:T(8,128)(2,1)S(1)}, u32[]{:S(2)}, u32[]{:S(2)}) collective-permute-start(bf16[128,1280]{1,0:T(8,128)(2,1)S(1)} %collective-permute-done.17.refs_8_), channel_id=1, source_target_pairs={{0,2},{1,7},{2,4},{3,1},{4,6},{5,3},{6,0},{7,5},{8,10},{9,15},{10,... | collective-permute-start | bytes 983048 | tf_op jit(solution)/shard_map/ppermute | solution.py:110
  201.9 3.8 %collective-permute-done.20.refs_11_ = bf16[128,1280]{1,0:T(8,128)(2,1)S(1)} collective-permute-done((bf16[128,1280]{1,0:T(8,128)(2,1)S(1)}, bf16[128,1280]{1,0:T(8,128)(2,1)S(1)}, u32[]{:S(2)}, u32[]{:S(2)}) %collective-permute-start.20) | collective-permute-done | bytes 327712 | tf_op jit(solution)/shard_map/ppermute | solution.py:123
  207.7 3.2 collective-permute-start.24
  210.9 3.1 collective-permute-start.23
  215.9 3.2 collective-permute-start.25
  219.4 3.7 %collective-permute-done.23.refs_14_ = bf16[128,1280]{1,0:T(8,128)(2,1)S(1)} collective-permute-done((bf16[128,1280]{1,0:T(8,128)(2,1)S(1)}, bf16[128,1280]{1,0:T(8,128)(2,1)S(1)}, u32[]{:S(2)}, u32[]{:S(2)}) %collective-permute-start.23) | collective-permute-done | bytes 327712 | tf_op jit(solution)/shard_map/ppermute | solution.py:123
  235.0 6.8 %shard_map.99 = bf16[2688,128]{1,0:T(8,128)(2,1)} custom-call(s32[16]{0:T(128)} %stack.140.slots, bf16[4,2,128,512]{3,2,1,0:T(8,128)(2,1)} %get-tuple-element.60.keep.refs_0_, bf16[4,2,128,512]{3,2,1,0:T(8,128)(2,1)} %copy-done, bf16[3,2,128,512]{3,2,1,0:T(8,128)(2,1)} %copy-done.6, bf16[3,2,128,512]{3,2,1,0:T(8,128)(2,1)} %copy-done.7, ...), custom_call_target="tpu_custom_call" | custom-call | flops 1342177280 | bytes 7340032 | tf_op jit(solution)/shard_map/pallas_call | solution.py:358
  241.8 46.0 %all_to_all.20 = bf16[48,56,128]{2,1,0:T(8,128)(2,1)S(1)} all-to-all(bf16[48,56,128]{2,1,0:T(8,128)(2,1)} %bitcast.66), channel_id=1, replica_groups=mesh['z'=12,'yh'=4,'yl'=2,'x'=4,'core'=2] {'z','yh'}, dimensions={0} | all-to-all | bytes 1376256 | tf_op jit(solution)/shard_map/all_to_all | solution.py:523
  288.9 5.2 %all-to-all-start.3 = ((bf16[48,56,128]{2,1,0:T(8,128)(2,1)}), bf16[48,56,128]{2,1,0:T(8,128)(2,1)S(1)}, u32[]{:S(2)}, u32[]{:S(2)}) async-start(bf16[48,56,128]{2,1,0:T(8,128)(2,1)} %broadcast_in_dim.55), calls=%async_computation.3 | async-start | bytes 1376256 | tf_op jit(solution)/shard_map/all_to_all | solution.py:523
  294.7 10.2 %shard_map.100 = (bf16[128,4096]{1,0:T(8,128)(2,1)}, bf16[128,4096]{1,0:T(8,128)(2,1)}) custom-call(s32[16]{0:T(128)} %concatenate.19.places, bf16[128,1280]{1,0:T(8,128)(2,1)} %copy-done.8, bf16[128,4096]{1,0:T(8,128)(2,1)} %bitcast.64, bf16[128,4096]{1,0:T(8,128)(2,1)} %bitcast.62, bf16[256,1280]{1,0:T(8,128)(2,1)} %constant_dynamic-update-slice_fusion.refs_0_, ...), custom_call_target="tpu_custom_call" | custom-call | flops 1342177280 | bytes 10485760 | tf_op jit(solution)/shard_map/pallas_call | solution.py:358
  304.8 22.5 %all-to-all-done.3 = bf16[48,56,128]{2,1,0:T(8,128)(2,1)S(1)} async-done(((bf16[48,56,128]{2,1,0:T(8,128)(2,1)}), bf16[48,56,128]{2,1,0:T(8,128)(2,1)S(1)}, u32[]{:S(2)}, u32[]{:S(2)}) %all-to-all-start.3) | async-done | bytes 688160 | tf_op jit(solution)/shard_map/all_to_all | solution.py:523
  (135 shorter events, 76.0 us)
Async XLA Ops:
  4.2 23.8 %collective-permute-start = (bf16[256,1280]{1,0:T(8,128)(2,1)}, bf16[256,1280]{1,0:T(8,128)(2,1)}, u32[]{:S(2)}, u32[]{:S(2)}) collective-permute-start(bf16[256,1280]{1,0:T(8,128)(2,1)} %constant_dynamic-update-slice_fusion.refs_0_), channel_id=1, source_target_pairs={{0,1},{1,0},{2,3},{3,2},{4,5},{5,4},{6,7},{7,6},{8,9},{9,8},{10,11... | collective-permute-start | bytes 1966088 | tf_op jit(solution)/shard_map/ppermute | solution.py:127
  6.1 26.2 %collective-permute-start.3 = (bf16[256,1280]{1,0:T(8,128)(2,1)}, bf16[256,1280]{1,0:T(8,128)(2,1)S(1)}, u32[]{:S(2)}, u32[]{:S(2)}) collective-permute-start(bf16[256,1280]{1,0:T(8,128)(2,1)} %constant_dynamic-update-slice_fusion.refs_0_), channel_id=1, source_target_pairs={{0,2},{1,7},{2,4},{3,1},{4,6},{5,3},{6,0},{7,5},{8,10},{9,15},{10,... | collective-permute-start | bytes 1966088 | tf_op jit(solution)/shard_map/ppermute | solution.py:110
  9.5 35.1 %collective-permute-start.6 = (bf16[256,1280]{1,0:T(8,128)(2,1)}, bf16[256,1280]{1,0:T(8,128)(2,1)S(1)}, u32[]{:S(2)}, u32[]{:S(2)}) collective-permute-start(bf16[256,1280]{1,0:T(8,128)(2,1)} %constant_dynamic-update-slice_fusion.refs_0_), channel_id=1, source_target_pairs={{0,8},{1,57},{8,16},{9,1},{16,24},{17,9},{24,32},{25,17},{32,40},{... | collective-permute-start | bytes 1966088 | tf_op jit(solution)/shard_map/ppermute | solution.py:119
  17.5 18.7 %collective-permute-start.2 = (bf16[4,2,128,512]{3,2,1,0:T(8,128)(2,1)}, bf16[4,2,128,512]{3,2,1,0:T(8,128)(2,1)S(1)}, u32[]{:S(2)}, u32[]{:S(2)}) collective-permute-start(bf16[4,2,128,512]{3,2,1,0:T(8,128)(2,1)} %get-tuple-element.41), channel_id=1, source_target_pairs={{0,1},{1,0},{2,3},{3,2},{4,5},{5,4},{6,7},{7,6},{8,9},{9,8},{10,11... | collective-permute-start | bytes 3145736 | tf_op jit(solution)/shard_map/ppermute | solution.py:127
  27.9 82.6 %copy-start.25 = (s32[192]{0:T(256)}, s32[192]{0:T(256)S(1)}, u32[]{:S(2)}) copy-start(s32[192]{0:T(256)S(1)} %add.484) | copy-start | bytes 2308
  28.0 13.9 %collective-permute-start.1 = (bf16[256,1280]{1,0:T(8,128)(2,1)}, bf16[256,1280]{1,0:T(8,128)(2,1)S(1)}, u32[]{:S(2)}, u32[]{:S(2)}) collective-permute-start(bf16[256,1280]{1,0:T(8,128)(2,1)} %collective-permute-done.refs_1_), channel_id=1, source_target_pairs={{0,2},{1,7},{2,4},{3,1},{4,6},{5,3},{6,0},{7,5},{8,10},{9,15},{10,... | collective-permute-start | bytes 1966088 | tf_op jit(solution)/shard_map/ppermute | solution.py:110
  32.3 18.0 %collective-permute-start.4 = (bf16[256,1280]{1,0:T(8,128)(2,1)S(1)}, bf16[256,1280]{1,0:T(8,128)(2,1)}, u32[]{:S(2)}, u32[]{:S(2)}) collective-permute-start(bf16[256,1280]{1,0:T(8,128)(2,1)S(1)} %collective-permute-done.3.refs_2_), channel_id=1, source_target_pairs={{0,8},{1,57},{8,16},{9,1},{16,24},{17,9},{24,32},{25,17},{32,40},{... | collective-permute-start | bytes 1966088 | tf_op jit(solution)/shard_map/ppermute | solution.py:119
  34.2 16.0 %collective-permute-start.9 = (bf16[256,1280]{1,0:T(8,128)(2,1)S(1)}, bf16[256,1280]{1,0:T(8,128)(2,1)}, u32[]{:S(2)}, u32[]{:S(2)}) collective-permute-start(bf16[256,1280]{1,0:T(8,128)(2,1)S(1)} %collective-permute-done.3.refs_2_), channel_id=1, source_target_pairs={{0,2},{1,7},{2,4},{3,1},{4,6},{5,3},{6,0},{7,5},{8,10},{9,15},{10,... | collective-permute-start | bytes 1966088 | tf_op jit(solution)/shard_map/ppermute | solution.py:110
  42.7 12.5 %collective-permute-start.8 = (bf16[256,1280]{1,0:T(8,128)(2,1)S(1)}, bf16[256,1280]{1,0:T(8,128)(2,1)S(1)}, u32[]{:S(2)}, u32[]{:S(2)}) collective-permute-start(bf16[256,1280]{1,0:T(8,128)(2,1)S(1)} %collective-permute-done.1.refs_3_), channel_id=1, source_target_pairs={{0,8},{1,57},{8,16},{9,1},{16,24},{17,9},{24,32},{25,17},{32,40},{... | collective-permute-start | bytes 1966088 | tf_op jit(solution)/shard_map/ppermute | solution.py:119
  46.1 18.0 %collective-permute-start.7 = (bf16[768,1280]{1,0:T(8,128)(2,1)}, bf16[768,1280]{1,0:T(8,128)(2,1)}, u32[]{:S(2)}, u32[]{:S(2)}) collective-permute-start(bf16[768,1280]{1,0:T(8,128)(2,1)} %pad_maximum_fusion), channel_id=1, source_target_pairs={{0,1},{1,0},{2,3},{3,2},{4,5},{5,4},{6,7},{7,6},{8,9},{9,8},{10,11... | collective-permute-start | bytes 5898248 | tf_op jit(solution)/shard_map/ppermute | solution.py:127
  58.7 19.8 %collective-permute-start.10 = (bf16[768,1280]{1,0:T(8,128)(2,1)}, bf16[768,1280]{1,0:T(8,128)(2,1)S(1)}, u32[]{:S(2)}, u32[]{:S(2)}) collective-permute-start(bf16[768,1280]{1,0:T(8,128)(2,1)} %pad_maximum_fusion.1), channel_id=1, source_target_pairs={{0,1},{1,0},{2,3},{3,2},{4,5},{5,4},{6,7},{7,6},{8,9},{9,8},{10,11... | collective-permute-start | bytes 5898248 | tf_op jit(solution)/shard_map/ppermute | solution.py:127
  60.6 13.9 %collective-permute-start.5 = (bf16[256,1280]{1,0:T(8,128)(2,1)}, bf16[256,1280]{1,0:T(8,128)(2,1)S(1)}, u32[]{:S(2)}, u32[]{:S(2)}) collective-permute-start(bf16[256,1280]{1,0:T(8,128)(2,1)} %collective-permute-done.4.refs_0_.refs_6_), channel_id=1, source_target_pairs={{0,2},{1,7},{2,4},{3,1},{4,6},{5,3},{6,0},{7,5},{8,10},{9,15},{10,... | collective-permute-start | bytes 1966088 | tf_op jit(solution)/shard_map/ppermute | solution.py:110
  74.5 4.0 %collective-permute-start.11 = (bf16[256,1280]{1,0:T(8,128)(2,1)S(1)}, bf16[256,1280]{1,0:T(8,128)(2,1)S(1)}, u32[]{:S(2)}, u32[]{:S(2)}) collective-permute-start(bf16[256,1280]{1,0:T(8,128)(2,1)S(1)} %collective-permute-done.5.refs_3_.refs_9_), channel_id=1, source_target_pairs={{0,1},{1,0},{2,3},{3,2},{4,5},{5,4},{6,7},{7,6},{8,9},{9,8},{10,11... | collective-permute-start | bytes 1966088 | tf_op jit(solution)/shard_map/ppermute | solution.py:127
  88.1 43.4 %all-to-all-start = ((bf16[48,4,1408]{2,1,0:T(4,128)(2,1)}), bf16[48,4,1408]{2,1,0:T(4,128)(2,1)S(1)}, u32[]{:S(2)}, u32[]{:S(2)}) async-start(bf16[48,4,1408]{2,1,0:T(4,128)(2,1)} %reshape.98), calls=%async_computation | async-start | bytes 1081344 | tf_op jit(solution)/shard_map/all_to_all | solution.py:523
  102.7 22.6 %collective-permute-start.12 = (bf16[3,2,128,512]{3,2,1,0:T(8,128)(2,1)}, bf16[3,2,128,512]{3,2,1,0:T(8,128)(2,1)S(1)}, u32[]{:S(2)}, u32[]{:S(2)}) collective-permute-start(bf16[3,2,128,512]{3,2,1,0:T(8,128)(2,1)} %get-tuple-element.58), channel_id=1, source_target_pairs={{0,2},{2,4},{4,6},{6,0},{1,3},{3,5},{5,7},{7,1},{8,10},{10,12},{12... | collective-permute-start | bytes 2359304 | tf_op jit(solution)/shard_map/ppermute | solution.py:101
  104.7 45.6 %collective-permute-start.13 = (bf16[3,2,128,512]{3,2,1,0:T(8,128)(2,1)S(1)}, bf16[3,2,128,512]{3,2,1,0:T(8,128)(2,1)S(1)}, u32[]{:S(2)}, u32[]{:S(2)}) collective-permute-start(bf16[3,2,128,512]{3,2,1,0:T(8,128)(2,1)S(1)} %copy-done.27), channel_id=1, source_target_pairs={{0,6},{2,0},{4,2},{6,4},{1,7},{3,1},{5,3},{7,5},{8,14},{10,8},{12,... | collective-permute-start | bytes 2359304 | tf_op jit(solution)/shard_map/ppermute | solution.py:101
  125.4 30.3 %collective-permute-start.14 = (bf16[2,128,512]{2,1,0:T(8,128)(2,1)S(1)}, bf16[2,128,512]{2,1,0:T(8,128)(2,1)S(1)}, u32[]{:S(2)}, u32[]{:S(2)}) collective-permute-start(bf16[2,128,512]{2,1,0:T(8,128)(2,1)S(1)} %slice_bitcast_fusion.1), channel_id=1, source_target_pairs={{0,2},{2,4},{4,6},{6,0},{1,3},{3,5},{5,7},{7,1},{8,10},{10,12},{12... | collective-permute-start | bytes 786440 | tf_op jit(solution)/shard_map/ppermute | solution.py:101
  140.0 51.4 %all-to-all-start.1 = ((bf16[48,4,1280]{2,1,0:T(4,128)(2,1)}), bf16[48,4,1280]{2,1,0:T(4,128)(2,1)S(1)}, u32[]{:S(2)}, u32[]{:S(2)}) async-start(bf16[48,4,1280]{2,1,0:T(4,128)(2,1)} %reshape.100), calls=%async_computation.1 | async-start | bytes 983040 | tf_op jit(solution)/shard_map/all_to_all | solution.py:523
  150.4 41.1 %copy-start.23 = (bf16[192,128]{1,0:T(8,128)(2,1)S(1)}, bf16[192,128]{1,0:T(8,128)(2,1)}, u32[]{:S(2)}) copy-start(bf16[192,128]{1,0:T(8,128)(2,1)} %fusion.routing) | copy-start | bytes 147460
  150.4 9.1 %collective-permute-start.15 = (bf16[2,128,512]{2,1,0:T(8,128)(2,1)S(1)}, bf16[2,128,512]{2,1,0:T(8,128)(2,1)S(1)}, u32[]{:S(2)}, u32[]{:S(2)}) collective-permute-start(bf16[2,128,512]{2,1,0:T(8,128)(2,1)S(1)} %slice_bitcast_fusion), channel_id=1, source_target_pairs={{0,6},{2,0},{4,2},{6,4},{1,7},{3,1},{5,3},{7,5},{8,14},{10,8},{12,... | collective-permute-start | bytes 786440 | tf_op jit(solution)/shard_map/ppermute | solution.py:101
  163.4 28.0 %collective-permute-start.16 = (bf16[8,128,512]{2,1,0:T(8,128)(2,1)}, bf16[8,128,512]{2,1,0:T(8,128)(2,1)S(1)}, u32[]{:S(2)}, u32[]{:S(2)}) collective-permute-start(bf16[8,128,512]{2,1,0:T(8,128)(2,1)} %shard_map.98), channel_id=1, source_target_pairs={{0,8},{8,0},{1,9},{9,1},{2,10},{10,2},{3,11},{11,3},{4,12},{12,4},... | collective-permute-start | bytes 3145736 | tf_op jit(solution)/shard_map/ppermute | solution.py:123
  191.8 6.6 %collective-permute-start.17 = (bf16[128,1280]{1,0:T(8,128)(2,1)S(1)}, bf16[128,1280]{1,0:T(8,128)(2,1)S(1)}, u32[]{:S(2)}, u32[]{:S(2)}) collective-permute-start(bf16[128,1280]{1,0:T(8,128)(2,1)S(1)} %convolution_convert_fusion.refs_7_.both), channel_id=1, source_target_pairs={{0,1},{1,0},{2,3},{3,2},{4,5},{5,4},{6,7},{7,6},{8,9},{9,8},{10,11... | collective-permute-start | bytes 983048 | tf_op jit(solution)/shard_map/ppermute | solution.py:127
  193.7 12.0 %collective-permute-start.20 = (bf16[128,1280]{1,0:T(8,128)(2,1)S(1)}, bf16[128,1280]{1,0:T(8,128)(2,1)S(1)}, u32[]{:S(2)}, u32[]{:S(2)}) collective-permute-start(bf16[128,1280]{1,0:T(8,128)(2,1)S(1)} %convolution_convert_fusion.refs_7_.both), channel_id=1, source_target_pairs={{0,8},{8,0},{1,9},{9,1},{2,10},{10,2},{3,11},{11,3},{4,12},{12,4},... | collective-permute-start | bytes 983048 | tf_op jit(solution)/shard_map/ppermute | solution.py:123
  196.4 11.2 %collective-permute-start.18 = (bf16[128,1280]{1,0:T(8,128)(2,1)S(1)}, bf16[128,1280]{1,0:T(8,128)(2,1)S(1)}, u32[]{:S(2)}, u32[]{:S(2)}) collective-permute-start(bf16[128,1280]{1,0:T(8,128)(2,1)S(1)} %convolution_convert_fusion.refs_7_.both), channel_id=1, source_target_pairs={{0,2},{1,7},{2,4},{3,1},{4,6},{5,3},{6,0},{7,5},{8,10},{9,15},{10,... | collective-permute-start | bytes 983048 | tf_op jit(solution)/shard_map/ppermute | solution.py:110
  198.4 12.5 %collective-permute-start.19 = (bf16[128,1280]{1,0:T(8,128)(2,1)S(1)}, bf16[128,1280]{1,0:T(8,128)(2,1)S(1)}, u32[]{:S(2)}, u32[]{:S(2)}) collective-permute-start(bf16[128,1280]{1,0:T(8,128)(2,1)S(1)} %collective-permute-done.17.refs_8_), channel_id=1, source_target_pairs={{0,2},{1,7},{2,4},{3,1},{4,6},{5,3},{6,0},{7,5},{8,10},{9,15},{10,... | collective-permute-start | bytes 983048 | tf_op jit(solution)/shard_map/ppermute | solution.py:110
  205.7 10.2 %collective-permute-start.22 = (bf16[128,1280]{1,0:T(8,128)(2,1)S(1)}, bf16[128,1280]{1,0:T(8,128)(2,1)S(1)}, u32[]{:S(2)}, u32[]{:S(2)}) collective-permute-start(bf16[128,1280]{1,0:T(8,128)(2,1)S(1)} %collective-permute-done.20.refs_11_), channel_id=1, source_target_pairs={{0,2},{1,7},{2,4},{3,1},{4,6},{5,3},{6,0},{7,5},{8,10},{9,15},{10,... | collective-permute-start | bytes 983048 | tf_op jit(solution)/shard_map/ppermute | solution.py:110
  207.7 11.7 %collective-permute-start.24 = (bf16[128,1280]{1,0:T(8,128)(2,1)S(1)}, bf16[128,1280]{1,0:T(8,128)(2,1)S(1)}, u32[]{:S(2)}, u32[]{:S(2)}) collective-permute-start(bf16[128,1280]{1,0:T(8,128)(2,1)S(1)} %collective-permute-done.18.refs_9_), channel_id=1, source_target_pairs={{0,2},{1,7},{2,4},{3,1},{4,6},{5,3},{6,0},{7,5},{8,10},{9,15},{10,... | collective-permute-start | bytes 983048 | tf_op jit(solution)/shard_map/ppermute | solution.py:110
  210.9 12.3 %collective-permute-start.23 = (bf16[128,1280]{1,0:T(8,128)(2,1)S(1)}, bf16[128,1280]{1,0:T(8,128)(2,1)S(1)}, u32[]{:S(2)}, u32[]{:S(2)}) collective-permute-start(bf16[128,1280]{1,0:T(8,128)(2,1)S(1)} %collective-permute-done.19.refs_10_), channel_id=1, source_target_pairs={{0,8},{8,0},{1,9},{9,1},{2,10},{10,2},{3,11},{11,3},{4,12},{12,4},... | collective-permute-start | bytes 983048 | tf_op jit(solution)/shard_map/ppermute | solution.py:123
  215.9 10.2 %collective-permute-start.25 = (bf16[128,1280]{1,0:T(8,128)(2,1)S(1)}, bf16[128,1280]{1,0:T(8,128)(2,1)S(1)}, u32[]{:S(2)}, u32[]{:S(2)}) collective-permute-start(bf16[128,1280]{1,0:T(8,128)(2,1)S(1)} %collective-permute-done.22.refs_13_), channel_id=1, source_target_pairs={{0,2},{1,7},{2,4},{3,1},{4,6},{5,3},{6,0},{7,5},{8,10},{9,15},{10,... | collective-permute-start | bytes 983048 | tf_op jit(solution)/shard_map/ppermute | solution.py:110
  227.3 6.7 %collective-permute-start.26 = (bf16[512,1280]{1,0:T(8,128)(2,1)}, bf16[512,1280]{1,0:T(8,128)(2,1)}, u32[]{:S(2)}, u32[]{:S(2)}) collective-permute-start(bf16[512,1280]{1,0:T(8,128)(2,1)} %pad_maximum_fusion.2), channel_id=1, source_target_pairs={{0,1},{1,0},{2,3},{3,2},{4,5},{5,4},{6,7},{7,6},{8,9},{9,8},{10,11... | collective-permute-start | bytes 3932168 | tf_op jit(solution)/shard_map/ppermute | solution.py:127
  229.4 4.6 %collective-permute-start.21 = (bf16[384,1280]{1,0:T(8,128)(2,1)S(1)}, bf16[384,1280]{1,0:T(8,128)(2,1)S(1)}, u32[]{:S(2)}, u32[]{:S(2)}) collective-permute-start(bf16[384,1280]{1,0:T(8,128)(2,1)S(1)} %pad_maximum_fusion.3), channel_id=1, source_target_pairs={{0,1},{1,0},{2,3},{3,2},{4,5},{5,4},{6,7},{7,6},{8,9},{9,8},{10,11... | collective-permute-start | bytes 2949128 | tf_op jit(solution)/shard_map/ppermute | solution.py:127
  288.9 38.4 %all-to-all-start.3 = ((bf16[48,56,128]{2,1,0:T(8,128)(2,1)}), bf16[48,56,128]{2,1,0:T(8,128)(2,1)S(1)}, u32[]{:S(2)}, u32[]{:S(2)}) async-start(bf16[48,56,128]{2,1,0:T(8,128)(2,1)} %broadcast_in_dim.55), calls=%async_computation.3 | async-start | bytes 1376256 | tf_op jit(solution)/shard_map/all_to_all | solution.py:523
  (27 other events, 351.8 us)

commit v5 on v4

--- a/solution.py
+++ b/solution.py
@@ -138,6 +138,11 @@
     return jnp.stack([place(*offset) for offset in offsets])
 
 
+def join_kernel(first, second, out):
+    out[:, : first.shape[1]] = first[...]
+    out[:, first.shape[1] :] = second[...]
+
+
 def pack_x_kernel(keep, other, up, down):
     up[0] = keep[1]
     up[1] = other[1]
@@ -190,7 +195,6 @@
     next_block = along_x(other_0)
     side_a = along_y(near)
     far = along_x(near)
-    next_block, beside = lax.optimization_barrier((next_block, beside))
     side_b = along_y(next_block)
     far_y = along_x(side_a)
     other_1 = swap_core(jnp.concatenate([near, next_block, across], axis=0))
@@ -203,9 +207,9 @@
         (other_1, [(sign, 0, 1), (sign, 0, 0), (0, 1, 1)]),
     ]
     early = number_blocks(groups, place)
+    side_b, beside = lax.optimization_barrier((side_b, beside))
     total = first_dot(beside, *early)
     other_2 = swap_core(jnp.concatenate([side_a, side_b, far], axis=0))
-    far_y, total = lax.optimization_barrier((far_y, total))
     other_3 = swap_core(far_y)
     groups = [
         (side_a, [(-sign, 1, 0)]),
@@ -441,7 +445,15 @@
         )
 
     early, late, begun, beside = gather_weights(
-        jnp.concatenate([qkv_weight, out_weight], axis=1),
+        call(
+            join_kernel,
+            None,
+            [qkv_weight, out_weight],
+            jax.ShapeDtypeStruct((share, width), jnp.bfloat16),
+            [],
+            share * width,
+            4 * share * width,
+        ),
         first_dot,
         (normed_b, keep, other, up, down, flag_cols, routing, position),
     )

time: 332 us -> 334 us (level)
  waiting for transfers between devices: 96.8 us -> 104 us
  local copies, waits for them, and re-layouts: 22.5 us -> 17.2 us
    ppermute x9, waiting for transfers between devices: 12.6 us -> 22.9 us  [along_x(): return lax.ppermute(array, ('x', 'core'), pairs)]
    unnamed x59 -> x52, local copies, waits for them, and re-layouts: 8.47 us -> 4.96 us
    pallas_call x9 -> x10, Pallas kernels: 44.8 us -> 46.8 us  [call(): pl.pallas_call(kernel, out_shape=out_shape, in_specs=smem + [vmem] * len(...]
  transfers between devices with their start and end apart: 30 -> 30, of which waited for: 15 -> 14; matrix products, arithmetic and copies ran while one was open for 5% -> 5% of each run, Pallas kernels for 9% -> 9%
where the time goes in v5:
time: 334 us; the launch traced here: 332 us
  starting transfers between devices  109 us (33%)
  waiting for transfers between devices  104 us (31%)
  Pallas kernels  46.8 us (14%)
  blocking collectives  45.9 us (14%)
  local copies, waits for them, and re-layouts  17.2 us (5%)
  other arithmetic  7.56 us (2%)
    pallas_call x10, Pallas kernels, call(): pl.pallas_call(kernel, out_shape=out_shape, in_specs=smem + [vmem] * len(...  46.8 us
    all_to_all x1, blocking collectives, swap_dp(): return lax.all_to_all(array, DP, split_axis=0, concat_axis=0, tiled=True)  45.9 us
    ppermute x3, waiting for transfers between devices, swap_y(): return lax.ppermute(array, 'yl', [(0, 1), (1, 0)])  31.9 us
    all_to_all x3, starting transfers between devices, swap_dp(): return lax.all_to_all(array, DP, split_axis=0, concat_axis=0, tiled=True)  30.5 us
    all_to_all x3, waiting for transfers between devices, swap_dp(): return lax.all_to_all(array, DP, split_axis=0, concat_axis=0, tiled=True)  26.2 us
    ppermute x9, starting transfers between devices, along_x(): return lax.ppermute(array, ('x', 'core'), pairs)  24.9 us
    ppermute x9, waiting for transfers between devices, along_x(): return lax.ppermute(array, ('x', 'core'), pairs)  22.9 us
    ppermute x8, starting transfers between devices, swap_core(): return lax.ppermute(array, 'core', [(0, 1), (1, 0)])  22.5 us
  transfers between devices with their start and end apart: 30, of which 14 were waited for; matrix products, arithmetic and copies ran while one was open for 5% of the time, Pallas kernels for 9%

profile of v5, /device:TPU:8, one launch (start us, length us, event | category | flops | bytes accessed | tf_op | source)
XLA Modules:
  0.0 331.9 jit_solution(7940319430552345960)
XLA Ops:
  4.6 3.4 %collective-permute-start.4 = (bf16[256,1280]{1,0:T(8,128)(2,1)}, bf16[256,1280]{1,0:T(8,128)(2,1)S(1)}, u32[]{:S(2)}, u32[]{:S(2)}) collective-permute-start(bf16[256,1280]{1,0:T(8,128)(2,1)} %shard_map.93.refs_0_), channel_id=1, source_target_pairs={{0,2},{1,7},{2,4},{3,1},{4,6},{5,3},{6,0},{7,5},{8,10},{9,15},{10,... | collective-permute-start | bytes 1966088 | tf_op jit(solution)/shard_map/ppermute | solution.py:110
  8.0 3.5 %collective-permute-start.5 = (bf16[256,1280]{1,0:T(8,128)(2,1)}, bf16[256,1280]{1,0:T(8,128)(2,1)S(1)}, u32[]{:S(2)}, u32[]{:S(2)}) collective-permute-start(bf16[256,1280]{1,0:T(8,128)(2,1)} %shard_map.93.refs_0_), channel_id=1, source_target_pairs={{0,8},{1,57},{8,16},{9,1},{16,24},{17,9},{24,32},{25,17},{32,40},{... | collective-permute-start | bytes 1966088 | tf_op jit(solution)/shard_map/ppermute | solution.py:119
  12.2 3.8 %shard_map.94 = (bf16[128,4096]{1,0:T(8,128)(2,1)}, bf16[4,2,128,512]{3,2,1,0:T(8,128)(2,1)}, bf16[4,2,128,512]{3,2,1,0:T(8,128)(2,1)}) custom-call(s32[16]{0:T(128)} %stack.149.places, bf16[128,4096]{1,0:T(8,128)(2,1)} %bitcast.63, bf16[128,4096]{1,0:T(8,128)(2,1)} %bitcast.59), custom_call_target="tpu_custom_call" | custom-call | flops 2097152 | bytes 5242880 | tf_op jit(solution)/shard_map/pallas_call | solution.py:362
  16.0 8.5 %collective-permute-start.3 = (bf16[4,2,128,512]{3,2,1,0:T(8,128)(2,1)}, bf16[4,2,128,512]{3,2,1,0:T(8,128)(2,1)S(1)}, u32[]{:S(2)}, u32[]{:S(2)}) collective-permute-start(bf16[4,2,128,512]{3,2,1,0:T(8,128)(2,1)} %get-tuple-element.39), channel_id=1, source_target_pairs={{0,1},{1,0},{2,3},{3,2},{4,5},{5,4},{6,7},{7,6},{8,9},{9,8},{10,11... | collective-permute-start | bytes 3145736 | tf_op jit(solution)/shard_map/ppermute | solution.py:127
  26.2 3.6 %collective-permute-start.1 = (bf16[256,1280]{1,0:T(8,128)(2,1)}, bf16[256,1280]{1,0:T(8,128)(2,1)S(1)}, u32[]{:S(2)}, u32[]{:S(2)}) collective-permute-start(bf16[256,1280]{1,0:T(8,128)(2,1)} %collective-permute-done.refs_1_), channel_id=1, source_target_pairs={{0,2},{1,7},{2,4},{3,1},{4,6},{5,3},{6,0},{7,5},{8,10},{9,15},{10,... | collective-permute-start | bytes 1966088 | tf_op jit(solution)/shard_map/ppermute | solution.py:110
  34.0 6.0 %collective-permute-done.1.refs_3_ = bf16[256,1280]{1,0:T(8,128)(2,1)S(1)} collective-permute-done((bf16[256,1280]{1,0:T(8,128)(2,1)}, bf16[256,1280]{1,0:T(8,128)(2,1)S(1)}, u32[]{:S(2)}, u32[]{:S(2)}) %collective-permute-start.1) | collective-permute-done | bytes 655392 | tf_op jit(solution)/shard_map/ppermute | solution.py:110
  60.6 11.5 %collective-permute-done.9.refs_3_.refs_9_ = bf16[256,1280]{1,0:T(8,128)(2,1)S(1)} collective-permute-done((bf16[256,1280]{1,0:T(8,128)(2,1)}, bf16[256,1280]{1,0:T(8,128)(2,1)S(1)}, u32[]{:S(2)}, u32[]{:S(2)}) %collective-permute-start.9) | collective-permute-done | bytes 655392 | tf_op jit(solution)/shard_map/ppermute | solution.py:110
  75.4 4.9 %shard_map.96.begun = f32[128,1280]{1,0:T(8,128)} custom-call(s32[8]{0:T(128)} %stack.151.places, bf16[128,4096]{1,0:T(8,128)(2,1)} %get-tuple-element.43.normed, bf16[128,4096]{1,0:T(8,128)(2,1)} %bitcast.60, bf16[256,1280]{1,0:T(8,128)(2,1)} %shard_map.93.refs_0_, bf16[256,1280]{1,0:T(8,128)(2,1)} %collective-permute-done.refs_1_, ...), custom_call_target="tpu_custom_call" | custom-call | flops 671088640 | bytes 5242880 | tf_op jit(solution)/shard_map/pallas_call | solution.py:362
  81.6 5.5 %shard_map.97 = bf16[192,1408]{1,0:T(8,128)(2,1)} custom-call(s32[8]{0:T(128)} %stack.150.places, bf16[128,4096]{1,0:T(8,128)(2,1)} %get-tuple-element.43.normed, bf16[128,4096]{1,0:T(8,128)(2,1)} %bitcast.61, f32[128,1280]{1,0:T(8,128)} %shard_map.96.begun, bf16[192,128]{1,0:T(8,128)(2,1)} %fusion.routing, bf16[128,128]{1,0:T(8,128)(2,1)} %broadcast_in_dim.26.flags, ...), custom_call_target="tpu_custom_call" | custom-call | flops 671088640 | bytes 5242880 | tf_op jit(solution)/shard_map/pallas_call | solution.py:362
  89.1 14.6 %all-to-all-start = ((bf16[48,4,1408]{2,1,0:T(4,128)(2,1)}), bf16[48,4,1408]{2,1,0:T(4,128)(2,1)S(1)}, u32[]{:S(2)}, u32[]{:S(2)}) async-start(bf16[48,4,1408]{2,1,0:T(4,128)(2,1)} %reshape.98), calls=%async_computation | async-start | bytes 1081344 | tf_op jit(solution)/shard_map/all_to_all | solution.py:535
  105.6 5.1 %collective-permute-start.13 = (bf16[3,2,128,512]{3,2,1,0:T(8,128)(2,1)}, bf16[3,2,128,512]{3,2,1,0:T(8,128)(2,1)S(1)}, u32[]{:S(2)}, u32[]{:S(2)}) collective-permute-start(bf16[3,2,128,512]{3,2,1,0:T(8,128)(2,1)} %get-tuple-element.55), channel_id=1, source_target_pairs={{0,6},{2,0},{4,2},{6,4},{1,7},{3,1},{5,3},{7,5},{8,14},{10,8},{12,... | collective-permute-start | bytes 2359304 | tf_op jit(solution)/shard_map/ppermute | solution.py:101
  112.1 14.5 %collective-permute-done.12.up.refs_2_ = bf16[3,2,128,512]{3,2,1,0:T(8,128)(2,1)S(1)} collective-permute-done((bf16[3,2,128,512]{3,2,1,0:T(8,128)(2,1)}, bf16[3,2,128,512]{3,2,1,0:T(8,128)(2,1)S(1)}, u32[]{:S(2)}, u32[]{:S(2)}) %collective-permute-start.12) | collective-permute-done | bytes 786464 | tf_op jit(solution)/shard_map/ppermute | solution.py:101
  128.6 3.9 %all-to-all-done = bf16[48,4,1408]{2,1,0:T(4,128)(2,1)S(1)} async-done(((bf16[48,4,1408]{2,1,0:T(4,128)(2,1)}), bf16[48,4,1408]{2,1,0:T(4,128)(2,1)S(1)}, u32[]{:S(2)}, u32[]{:S(2)}) %all-to-all-start) | async-done | bytes 540704 | tf_op jit(solution)/shard_map/all_to_all | solution.py:535
  133.3 5.5 %shard_map.98 = bf16[192,1280]{1,0:T(8,128)(2,1)} custom-call(s32[1]{0:T(128)} %bitcast.24.length, s32[192,1]{1,0:T(8,128)} %copy.14.place_col, s32[1,192]{1,0:T(1,128)} %bitcast.68, bf16[192,1408]{1,0:T(8,128)(2,1)} %reshape.99.got), custom_call_target="tpu_custom_call" | custom-call | flops 339738624 | bytes 983040 | tf_op jit(solution)/shard_map/pallas_call | solution.py:362
  140.8 10.7 %all-to-all-start.1 = ((bf16[48,4,1280]{2,1,0:T(4,128)(2,1)}), bf16[48,4,1280]{2,1,0:T(4,128)(2,1)S(1)}, u32[]{:S(2)}, u32[]{:S(2)}) async-start(bf16[48,4,1280]{2,1,0:T(4,128)(2,1)} %reshape.100), calls=%async_computation.1 | async-start | bytes 983040 | tf_op jit(solution)/shard_map/all_to_all | solution.py:535
  151.6 5.3 %collective-permute-start.15 = (bf16[2,128,512]{2,1,0:T(8,128)(2,1)S(1)}, bf16[2,128,512]{2,1,0:T(8,128)(2,1)S(1)}, u32[]{:S(2)}, u32[]{:S(2)}) collective-permute-start(bf16[2,128,512]{2,1,0:T(8,128)(2,1)S(1)} %slice_bitcast_fusion), channel_id=1, source_target_pairs={{0,6},{2,0},{4,2},{6,4},{1,7},{3,1},{5,3},{7,5},{8,14},{10,8},{12,... | collective-permute-start | bytes 786440 | tf_op jit(solution)/shard_map/ppermute | solution.py:101
  156.9 4.2 %collective-permute-done.15.far_down.refs_5_ = bf16[2,128,512]{2,1,0:T(8,128)(2,1)S(1)} collective-permute-done((bf16[2,128,512]{2,1,0:T(8,128)(2,1)S(1)}, bf16[2,128,512]{2,1,0:T(8,128)(2,1)S(1)}, u32[]{:S(2)}, u32[]{:S(2)}) %collective-permute-start.15) | collective-permute-done | bytes 262176 | tf_op jit(solution)/shard_map/ppermute | solution.py:101
  161.8 3.2 shard_map.99
  165.0 3.6 %collective-permute-start.16 = (bf16[8,128,512]{2,1,0:T(8,128)(2,1)}, bf16[8,128,512]{2,1,0:T(8,128)(2,1)S(1)}, u32[]{:S(2)}, u32[]{:S(2)}) collective-permute-start(bf16[8,128,512]{2,1,0:T(8,128)(2,1)} %shard_map.99), channel_id=1, source_target_pairs={{0,8},{8,0},{1,9},{9,1},{2,10},{10,2},{3,11},{11,3},{4,12},{12,4},... | collective-permute-start | bytes 3145736 | tf_op jit(solution)/shard_map/ppermute | solution.py:123
  168.5 24.6 %collective-permute-done.16.refs_6_ = bf16[8,128,512]{2,1,0:T(8,128)(2,1)S(1)} collective-permute-done((bf16[8,128,512]{2,1,0:T(8,128)(2,1)}, bf16[8,128,512]{2,1,0:T(8,128)(2,1)S(1)}, u32[]{:S(2)}, u32[]{:S(2)}) %collective-permute-start.16) | collective-permute-done | bytes 1048608 | tf_op jit(solution)/shard_map/ppermute | solution.py:123
  200.2 3.5 %collective-permute-start.19 = (bf16[128,1280]{1,0:T(8,128)(2,1)S(1)}, bf16[128,1280]{1,0:T(8,128)(2,1)S(1)}, u32[]{:S(2)}, u32[]{:S(2)}) collective-permute-start(bf16[128,1280]{1,0:T(8,128)(2,1)S(1)} %collective-permute-done.17.refs_8_), channel_id=1, source_target_pairs={{0,2},{1,7},{2,4},{3,1},{4,6},{5,3},{6,0},{7,5},{8,10},{9,15},{10,... | collective-permute-start | bytes 983048 | tf_op jit(solution)/shard_map/ppermute | solution.py:110
  203.7 3.7 %collective-permute-done.20.refs_11_ = bf16[128,1280]{1,0:T(8,128)(2,1)S(1)} collective-permute-done((bf16[128,1280]{1,0:T(8,128)(2,1)S(1)}, bf16[128,1280]{1,0:T(8,128)(2,1)S(1)}, u32[]{:S(2)}, u32[]{:S(2)}) %collective-permute-start.20) | collective-permute-done | bytes 327712 | tf_op jit(solution)/shard_map/ppermute | solution.py:123
  209.4 3.1 collective-permute-start.24
  212.5 3.2 collective-permute-start.23
  217.6 3.1 collective-permute-start.25
  221.1 3.6 %collective-permute-done.23.refs_14_ = bf16[128,1280]{1,0:T(8,128)(2,1)S(1)} collective-permute-done((bf16[128,1280]{1,0:T(8,128)(2,1)S(1)}, bf16[128,1280]{1,0:T(8,128)(2,1)S(1)}, u32[]{:S(2)}, u32[]{:S(2)}) %collective-permute-start.23) | collective-permute-done | bytes 327712 | tf_op jit(solution)/shard_map/ppermute | solution.py:123
  224.7 3.1 collective-permute-done.25.refs_16_
  236.7 6.8 %shard_map.100 = bf16[2688,128]{1,0:T(8,128)(2,1)} custom-call(s32[16]{0:T(128)} %stack.140.slots, bf16[4,2,128,512]{3,2,1,0:T(8,128)(2,1)} %get-tuple-element.56.keep.refs_0_, bf16[4,2,128,512]{3,2,1,0:T(8,128)(2,1)} %copy-done, bf16[3,2,128,512]{3,2,1,0:T(8,128)(2,1)} %copy-done.5, bf16[3,2,128,512]{3,2,1,0:T(8,128)(2,1)} %copy-done.6, ...), custom_call_target="tpu_custom_call" | custom-call | flops 1342177280 | bytes 7340032 | tf_op jit(solution)/shard_map/pallas_call | solution.py:362
  243.5 45.9 %all_to_all.20 = bf16[48,56,128]{2,1,0:T(8,128)(2,1)S(1)} all-to-all(bf16[48,56,128]{2,1,0:T(8,128)(2,1)} %bitcast.66), channel_id=1, replica_groups=mesh['z'=12,'yh'=4,'yl'=2,'x'=4,'core'=2] {'z','yh'}, dimensions={0} | all-to-all | bytes 1376256 | tf_op jit(solution)/shard_map/all_to_all | solution.py:535
  290.4 5.2 %all-to-all-start.3 = ((bf16[48,56,128]{2,1,0:T(8,128)(2,1)}), bf16[48,56,128]{2,1,0:T(8,128)(2,1)S(1)}, u32[]{:S(2)}, u32[]{:S(2)}) async-start(bf16[48,56,128]{2,1,0:T(8,128)(2,1)} %broadcast_in_dim.55), calls=%async_computation.3 | async-start | bytes 1376256 | tf_op jit(solution)/shard_map/all_to_all | solution.py:535
  296.3 10.2 %shard_map.101 = (bf16[128,4096]{1,0:T(8,128)(2,1)}, bf16[128,4096]{1,0:T(8,128)(2,1)}) custom-call(s32[16]{0:T(128)} %concatenate.16.places, bf16[128,1280]{1,0:T(8,128)(2,1)} %copy-done.7, bf16[128,4096]{1,0:T(8,128)(2,1)} %bitcast.64, bf16[128,4096]{1,0:T(8,128)(2,1)} %bitcast.62, bf16[256,1280]{1,0:T(8,128)(2,1)} %shard_map.93.refs_0_, ...), custom_call_target="tpu_custom_call" | custom-call | flops 1342177280 | bytes 10485760 | tf_op jit(solution)/shard_map/pallas_call | solution.py:362
  306.5 22.3 %all-to-all-done.3 = bf16[48,56,128]{2,1,0:T(8,128)(2,1)S(1)} async-done(((bf16[48,56,128]{2,1,0:T(8,128)(2,1)}), bf16[48,56,128]{2,1,0:T(8,128)(2,1)S(1)}, u32[]{:S(2)}, u32[]{:S(2)}) %all-to-all-start.3) | async-done | bytes 688160 | tf_op jit(solution)/shard_map/all_to_all | solution.py:535
  (128 shorter events, 71.1 us)
Async XLA Ops:
  2.6 23.6 %collective-permute-start = (bf16[256,1280]{1,0:T(8,128)(2,1)}, bf16[256,1280]{1,0:T(8,128)(2,1)}, u32[]{:S(2)}, u32[]{:S(2)}) collective-permute-start(bf16[256,1280]{1,0:T(8,128)(2,1)} %shard_map.93.refs_0_), channel_id=1, source_target_pairs={{0,1},{1,0},{2,3},{3,2},{4,5},{5,4},{6,7},{7,6},{8,9},{9,8},{10,11... | collective-permute-start | bytes 1966088 | tf_op jit(solution)/shard_map/ppermute | solution.py:127
  4.6 25.6 %collective-permute-start.4 = (bf16[256,1280]{1,0:T(8,128)(2,1)}, bf16[256,1280]{1,0:T(8,128)(2,1)S(1)}, u32[]{:S(2)}, u32[]{:S(2)}) collective-permute-start(bf16[256,1280]{1,0:T(8,128)(2,1)} %shard_map.93.refs_0_), channel_id=1, source_target_pairs={{0,2},{1,7},{2,4},{3,1},{4,6},{5,3},{6,0},{7,5},{8,10},{9,15},{10,... | collective-permute-start | bytes 1966088 | tf_op jit(solution)/shard_map/ppermute | solution.py:110
  8.0 38.5 %collective-permute-start.5 = (bf16[256,1280]{1,0:T(8,128)(2,1)}, bf16[256,1280]{1,0:T(8,128)(2,1)S(1)}, u32[]{:S(2)}, u32[]{:S(2)}) collective-permute-start(bf16[256,1280]{1,0:T(8,128)(2,1)} %shard_map.93.refs_0_), channel_id=1, source_target_pairs={{0,8},{1,57},{8,16},{9,1},{16,24},{17,9},{24,32},{25,17},{32,40},{... | collective-permute-start | bytes 1966088 | tf_op jit(solution)/shard_map/ppermute | solution.py:119
  16.0 26.6 %collective-permute-start.3 = (bf16[4,2,128,512]{3,2,1,0:T(8,128)(2,1)}, bf16[4,2,128,512]{3,2,1,0:T(8,128)(2,1)S(1)}, u32[]{:S(2)}, u32[]{:S(2)}) collective-permute-start(bf16[4,2,128,512]{3,2,1,0:T(8,128)(2,1)} %get-tuple-element.39), channel_id=1, source_target_pairs={{0,1},{1,0},{2,3},{3,2},{4,5},{5,4},{6,7},{7,6},{8,9},{9,8},{10,11... | collective-permute-start | bytes 3145736 | tf_op jit(solution)/shard_map/ppermute | solution.py:127
  26.2 13.9 %collective-permute-start.1 = (bf16[256,1280]{1,0:T(8,128)(2,1)}, bf16[256,1280]{1,0:T(8,128)(2,1)S(1)}, u32[]{:S(2)}, u32[]{:S(2)}) collective-permute-start(bf16[256,1280]{1,0:T(8,128)(2,1)} %collective-permute-done.refs_1_), channel_id=1, source_target_pairs={{0,2},{1,7},{2,4},{3,1},{4,6},{5,3},{6,0},{7,5},{8,10},{9,15},{10,... | collective-permute-start | bytes 1966088 | tf_op jit(solution)/shard_map/ppermute | solution.py:110
  30.0 81.3 %copy-start.23 = (s32[192]{0:T(256)}, s32[192]{0:T(256)S(1)}, u32[]{:S(2)}) copy-start(s32[192]{0:T(256)S(1)} %add.484) | copy-start | bytes 2308
  30.2 45.2 %copy-start.2 = (bf16[256,1280]{1,0:T(8,128)(2,1)}, bf16[256,1280]{1,0:T(8,128)(2,1)S(1)}, u32[]{:S(2)}) copy-start(bf16[256,1280]{1,0:T(8,128)(2,1)S(1)} %collective-permute-done.4.refs_2_) | copy-start | bytes 1966084
  30.2 23.2 %collective-permute-start.7 = (bf16[256,1280]{1,0:T(8,128)(2,1)S(1)}, bf16[256,1280]{1,0:T(8,128)(2,1)}, u32[]{:S(2)}, u32[]{:S(2)}) collective-permute-start(bf16[256,1280]{1,0:T(8,128)(2,1)S(1)} %collective-permute-done.4.refs_2_), channel_id=1, source_target_pairs={{0,8},{1,57},{8,16},{9,1},{16,24},{17,9},{24,32},{25,17},{32,40},{... | collective-permute-start | bytes 1966088 | tf_op jit(solution)/shard_map/ppermute | solution.py:119
  32.1 21.3 %collective-permute-start.8 = (bf16[256,1280]{1,0:T(8,128)(2,1)S(1)}, bf16[256,1280]{1,0:T(8,128)(2,1)}, u32[]{:S(2)}, u32[]{:S(2)}) collective-permute-start(bf16[256,1280]{1,0:T(8,128)(2,1)S(1)} %collective-permute-done.4.refs_2_), channel_id=1, source_target_pairs={{0,2},{1,7},{2,4},{3,1},{4,6},{5,3},{6,0},{7,5},{8,10},{9,15},{10,... | collective-permute-start | bytes 1966088 | tf_op jit(solution)/shard_map/ppermute | solution.py:110
  40.1 12.6 %collective-permute-start.2 = (bf16[256,1280]{1,0:T(8,128)(2,1)S(1)}, bf16[256,1280]{1,0:T(8,128)(2,1)}, u32[]{:S(2)}, u32[]{:S(2)}) collective-permute-start(bf16[256,1280]{1,0:T(8,128)(2,1)S(1)} %collective-permute-done.1.refs_3_), channel_id=1, source_target_pairs={{0,8},{1,57},{8,16},{9,1},{16,24},{17,9},{24,32},{25,17},{32,40},{... | collective-permute-start | bytes 1966088 | tf_op jit(solution)/shard_map/ppermute | solution.py:119
  47.9 27.4 %collective-permute-start.6 = (bf16[768,1280]{1,0:T(8,128)(2,1)}, bf16[768,1280]{1,0:T(8,128)(2,1)}, u32[]{:S(2)}, u32[]{:S(2)}) collective-permute-start(bf16[768,1280]{1,0:T(8,128)(2,1)} %pad_maximum_fusion), channel_id=1, source_target_pairs={{0,1},{1,0},{2,3},{3,2},{4,5},{5,4},{6,7},{7,6},{8,9},{9,8},{10,11... | collective-permute-start | bytes 5898248 | tf_op jit(solution)/shard_map/ppermute | solution.py:127
  56.3 24.1 %collective-permute-start.10 = (bf16[768,1280]{1,0:T(8,128)(2,1)}, bf16[768,1280]{1,0:T(8,128)(2,1)S(1)}, u32[]{:S(2)}, u32[]{:S(2)}) collective-permute-start(bf16[768,1280]{1,0:T(8,128)(2,1)} %pad_maximum_fusion.1), channel_id=1, source_target_pairs={{0,1},{1,0},{2,3},{3,2},{4,5},{5,4},{6,7},{7,6},{8,9},{9,8},{10,11... | collective-permute-start | bytes 5898248 | tf_op jit(solution)/shard_map/ppermute | solution.py:127
  58.2 13.9 %collective-permute-start.9 = (bf16[256,1280]{1,0:T(8,128)(2,1)}, bf16[256,1280]{1,0:T(8,128)(2,1)S(1)}, u32[]{:S(2)}, u32[]{:S(2)}) collective-permute-start(bf16[256,1280]{1,0:T(8,128)(2,1)} %collective-permute-done.7.refs_0_.refs_6_), channel_id=1, source_target_pairs={{0,2},{1,7},{2,4},{3,1},{4,6},{5,3},{6,0},{7,5},{8,10},{9,15},{10,... | collective-permute-start | bytes 1966088 | tf_op jit(solution)/shard_map/ppermute | solution.py:110
  72.1 8.2 %collective-permute-start.11 = (bf16[256,1280]{1,0:T(8,128)(2,1)S(1)}, bf16[256,1280]{1,0:T(8,128)(2,1)}, u32[]{:S(2)}, u32[]{:S(2)}) collective-permute-start(bf16[256,1280]{1,0:T(8,128)(2,1)S(1)} %collective-permute-done.9.refs_3_.refs_9_), channel_id=1, source_target_pairs={{0,1},{1,0},{2,3},{3,2},{4,5},{5,4},{6,7},{7,6},{8,9},{9,8},{10,11... | collective-permute-start | bytes 1966088 | tf_op jit(solution)/shard_map/ppermute | solution.py:127
  89.1 43.4 %all-to-all-start = ((bf16[48,4,1408]{2,1,0:T(4,128)(2,1)}), bf16[48,4,1408]{2,1,0:T(4,128)(2,1)S(1)}, u32[]{:S(2)}, u32[]{:S(2)}) async-start(bf16[48,4,1408]{2,1,0:T(4,128)(2,1)} %reshape.98), calls=%async_computation | async-start | bytes 1081344 | tf_op jit(solution)/shard_map/all_to_all | solution.py:535
  103.6 23.0 %collective-permute-start.12 = (bf16[3,2,128,512]{3,2,1,0:T(8,128)(2,1)}, bf16[3,2,128,512]{3,2,1,0:T(8,128)(2,1)S(1)}, u32[]{:S(2)}, u32[]{:S(2)}) collective-permute-start(bf16[3,2,128,512]{3,2,1,0:T(8,128)(2,1)} %get-tuple-element.54), channel_id=1, source_target_pairs={{0,2},{2,4},{4,6},{6,0},{1,3},{3,5},{5,7},{7,1},{8,10},{10,12},{12... | collective-permute-start | bytes 2359304 | tf_op jit(solution)/shard_map/ppermute | solution.py:101
  105.6 46.0 %collective-permute-start.13 = (bf16[3,2,128,512]{3,2,1,0:T(8,128)(2,1)}, bf16[3,2,128,512]{3,2,1,0:T(8,128)(2,1)S(1)}, u32[]{:S(2)}, u32[]{:S(2)}) collective-permute-start(bf16[3,2,128,512]{3,2,1,0:T(8,128)(2,1)} %get-tuple-element.55), channel_id=1, source_target_pairs={{0,6},{2,0},{4,2},{6,4},{1,7},{3,1},{5,3},{7,5},{8,14},{10,8},{12,... | collective-permute-start | bytes 2359304 | tf_op jit(solution)/shard_map/ppermute | solution.py:101
  126.6 30.2 %collective-permute-start.14 = (bf16[2,128,512]{2,1,0:T(8,128)(2,1)S(1)}, bf16[2,128,512]{2,1,0:T(8,128)(2,1)S(1)}, u32[]{:S(2)}, u32[]{:S(2)}) collective-permute-start(bf16[2,128,512]{2,1,0:T(8,128)(2,1)S(1)} %slice_bitcast_fusion.1), channel_id=1, source_target_pairs={{0,2},{2,4},{4,6},{6,0},{1,3},{3,5},{5,7},{7,1},{8,10},{10,12},{12... | collective-permute-start | bytes 786440 | tf_op jit(solution)/shard_map/ppermute | solution.py:101
  140.8 52.3 %all-to-all-start.1 = ((bf16[48,4,1280]{2,1,0:T(4,128)(2,1)}), bf16[48,4,1280]{2,1,0:T(4,128)(2,1)S(1)}, u32[]{:S(2)}, u32[]{:S(2)}) async-start(bf16[48,4,1280]{2,1,0:T(4,128)(2,1)} %reshape.100), calls=%async_computation.1 | async-start | bytes 983040 | tf_op jit(solution)/shard_map/all_to_all | solution.py:535
  151.6 9.5 %collective-permute-start.15 = (bf16[2,128,512]{2,1,0:T(8,128)(2,1)S(1)}, bf16[2,128,512]{2,1,0:T(8,128)(2,1)S(1)}, u32[]{:S(2)}, u32[]{:S(2)}) collective-permute-start(bf16[2,128,512]{2,1,0:T(8,128)(2,1)S(1)} %slice_bitcast_fusion), channel_id=1, source_target_pairs={{0,6},{2,0},{4,2},{6,4},{1,7},{3,1},{5,3},{7,5},{8,14},{10,8},{12,... | collective-permute-start | bytes 786440 | tf_op jit(solution)/shard_map/ppermute | solution.py:101
  165.0 28.1 %collective-permute-start.16 = (bf16[8,128,512]{2,1,0:T(8,128)(2,1)}, bf16[8,128,512]{2,1,0:T(8,128)(2,1)S(1)}, u32[]{:S(2)}, u32[]{:S(2)}) collective-permute-start(bf16[8,128,512]{2,1,0:T(8,128)(2,1)} %shard_map.99), channel_id=1, source_target_pairs={{0,8},{8,0},{1,9},{9,1},{2,10},{10,2},{3,11},{11,3},{4,12},{12,4},... | collective-permute-start | bytes 3145736 | tf_op jit(solution)/shard_map/ppermute | solution.py:123
  193.5 6.7 %collective-permute-start.17 = (bf16[128,1280]{1,0:T(8,128)(2,1)S(1)}, bf16[128,1280]{1,0:T(8,128)(2,1)S(1)}, u32[]{:S(2)}, u32[]{:S(2)}) collective-permute-start(bf16[128,1280]{1,0:T(8,128)(2,1)S(1)} %convolution_convert_fusion.refs_7_.both), channel_id=1, source_target_pairs={{0,1},{1,0},{2,3},{3,2},{4,5},{5,4},{6,7},{7,6},{8,9},{9,8},{10,11... | collective-permute-start | bytes 983048 | tf_op jit(solution)/shard_map/ppermute | solution.py:127
  195.4 12.0 %collective-permute-start.20 = (bf16[128,1280]{1,0:T(8,128)(2,1)S(1)}, bf16[128,1280]{1,0:T(8,128)(2,1)S(1)}, u32[]{:S(2)}, u32[]{:S(2)}) collective-permute-start(bf16[128,1280]{1,0:T(8,128)(2,1)S(1)} %convolution_convert_fusion.refs_7_.both), channel_id=1, source_target_pairs={{0,8},{8,0},{1,9},{9,1},{2,10},{10,2},{3,11},{11,3},{4,12},{12,4},... | collective-permute-start | bytes 983048 | tf_op jit(solution)/shard_map/ppermute | solution.py:123
  198.3 11.1 %collective-permute-start.18 = (bf16[128,1280]{1,0:T(8,128)(2,1)S(1)}, bf16[128,1280]{1,0:T(8,128)(2,1)S(1)}, u32[]{:S(2)}, u32[]{:S(2)}) collective-permute-start(bf16[128,1280]{1,0:T(8,128)(2,1)S(1)} %convolution_convert_fusion.refs_7_.both), channel_id=1, source_target_pairs={{0,2},{1,7},{2,4},{3,1},{4,6},{5,3},{6,0},{7,5},{8,10},{9,15},{10,... | collective-permute-start | bytes 983048 | tf_op jit(solution)/shard_map/ppermute | solution.py:110
  200.2 12.3 %collective-permute-start.19 = (bf16[128,1280]{1,0:T(8,128)(2,1)S(1)}, bf16[128,1280]{1,0:T(8,128)(2,1)S(1)}, u32[]{:S(2)}, u32[]{:S(2)}) collective-permute-start(bf16[128,1280]{1,0:T(8,128)(2,1)S(1)} %collective-permute-done.17.refs_8_), channel_id=1, source_target_pairs={{0,2},{1,7},{2,4},{3,1},{4,6},{5,3},{6,0},{7,5},{8,10},{9,15},{10,... | collective-permute-start | bytes 983048 | tf_op jit(solution)/shard_map/ppermute | solution.py:110
  207.4 10.2 %collective-permute-start.22 = (bf16[128,1280]{1,0:T(8,128)(2,1)S(1)}, bf16[128,1280]{1,0:T(8,128)(2,1)S(1)}, u32[]{:S(2)}, u32[]{:S(2)}) collective-permute-start(bf16[128,1280]{1,0:T(8,128)(2,1)S(1)} %collective-permute-done.20.refs_11_), channel_id=1, source_target_pairs={{0,2},{1,7},{2,4},{3,1},{4,6},{5,3},{6,0},{7,5},{8,10},{9,15},{10,... | collective-permute-start | bytes 983048 | tf_op jit(solution)/shard_map/ppermute | solution.py:110
  209.4 11.7 %collective-permute-start.24 = (bf16[128,1280]{1,0:T(8,128)(2,1)S(1)}, bf16[128,1280]{1,0:T(8,128)(2,1)S(1)}, u32[]{:S(2)}, u32[]{:S(2)}) collective-permute-start(bf16[128,1280]{1,0:T(8,128)(2,1)S(1)} %collective-permute-done.18.refs_9_), channel_id=1, source_target_pairs={{0,2},{1,7},{2,4},{3,1},{4,6},{5,3},{6,0},{7,5},{8,10},{9,15},{10,... | collective-permute-start | bytes 983048 | tf_op jit(solution)/shard_map/ppermute | solution.py:110
  212.5 12.2 %collective-permute-start.23 = (bf16[128,1280]{1,0:T(8,128)(2,1)S(1)}, bf16[128,1280]{1,0:T(8,128)(2,1)S(1)}, u32[]{:S(2)}, u32[]{:S(2)}) collective-permute-start(bf16[128,1280]{1,0:T(8,128)(2,1)S(1)} %collective-permute-done.19.refs_10_), channel_id=1, source_target_pairs={{0,8},{8,0},{1,9},{9,1},{2,10},{10,2},{3,11},{11,3},{4,12},{12,4},... | collective-permute-start | bytes 983048 | tf_op jit(solution)/shard_map/ppermute | solution.py:123
  217.6 10.2 %collective-permute-start.25 = (bf16[128,1280]{1,0:T(8,128)(2,1)S(1)}, bf16[128,1280]{1,0:T(8,128)(2,1)S(1)}, u32[]{:S(2)}, u32[]{:S(2)}) collective-permute-start(bf16[128,1280]{1,0:T(8,128)(2,1)S(1)} %collective-permute-done.22.refs_13_), channel_id=1, source_target_pairs={{0,2},{1,7},{2,4},{3,1},{4,6},{5,3},{6,0},{7,5},{8,10},{9,15},{10,... | collective-permute-start | bytes 983048 | tf_op jit(solution)/shard_map/ppermute | solution.py:110
  229.0 6.7 %collective-permute-start.26 = (bf16[512,1280]{1,0:T(8,128)(2,1)}, bf16[512,1280]{1,0:T(8,128)(2,1)}, u32[]{:S(2)}, u32[]{:S(2)}) collective-permute-start(bf16[512,1280]{1,0:T(8,128)(2,1)} %pad_maximum_fusion.2), channel_id=1, source_target_pairs={{0,1},{1,0},{2,3},{3,2},{4,5},{5,4},{6,7},{7,6},{8,9},{9,8},{10,11... | collective-permute-start | bytes 3932168 | tf_op jit(solution)/shard_map/ppermute | solution.py:127
  231.1 4.6 %collective-permute-start.21 = (bf16[384,1280]{1,0:T(8,128)(2,1)S(1)}, bf16[384,1280]{1,0:T(8,128)(2,1)S(1)}, u32[]{:S(2)}, u32[]{:S(2)}) collective-permute-start(bf16[384,1280]{1,0:T(8,128)(2,1)S(1)} %pad_maximum_fusion.3), channel_id=1, source_target_pairs={{0,1},{1,0},{2,3},{3,2},{4,5},{5,4},{6,7},{7,6},{8,9},{9,8},{10,11... | collective-permute-start | bytes 2949128 | tf_op jit(solution)/shard_map/ppermute | solution.py:127
  290.4 38.4 %all-to-all-start.3 = ((bf16[48,56,128]{2,1,0:T(8,128)(2,1)}), bf16[48,56,128]{2,1,0:T(8,128)(2,1)S(1)}, u32[]{:S(2)}, u32[]{:S(2)}) async-start(bf16[48,56,128]{2,1,0:T(8,128)(2,1)} %broadcast_in_dim.55), calls=%async_computation.3 | async-start | bytes 1376256 | tf_op jit(solution)/shard_map/all_to_all | solution.py:535
  (24 other events, 363.7 us)

commit v6 on v5

--- a/solution.py
+++ b/solution.py
@@ -334,18 +334,25 @@
     ).astype(jnp.bfloat16)
 
 
-def weight_grad_kernel(row_pieces, col_pieces, split, slots, *refs):
-    inputs, (out, rows_all, cols_all) = (refs[:-3], refs[-3:])
-    col_count = 1 + max(which for which, _, _ in col_pieces)
-    share = cols_all.shape[1] // 2
-    count = inputs[0].shape[2]
+def turn_kernel(col_pieces, *refs):
+    inputs, out = (refs[:-1], refs[-1])
     for which, index, to in col_pieces:
-        cols_all[to : to + count, :] = inputs[which][index]
+        piece = inputs[which][index]
+        out[:, to : to + piece.shape[0]] = piece.T
+
+
+def weight_grad_kernel(row_pieces, split, slots, turned, *refs):
+    inputs, (out, rows_all) = (refs[:-2], refs[-2:])
+    share = turned.shape[0] // 2
     for number, (which, row, _, rows) in enumerate(row_pieces):
-        where = pl.ds(pl.multiple_of(slots[number] * count, 128), rows)
-        rows_all[where, :] = inputs[col_count + which][row : row + rows, :]
-    first = contract_rows(cols_all[:, :share], rows_all[:, :split]).astype(jnp.bfloat16)
-    second = contract_rows(cols_all[:, share:], rows_all[:, split:]).astype(jnp.bfloat16)
+        where = pl.ds(pl.multiple_of(slots[number] * rows, 128), rows)
+        rows_all[where, :] = inputs[which][row : row + rows, :]
+    first = jnp.dot(
+        turned[:share, :], rows_all[:, :split], preferred_element_type=jnp.float32
+    ).astype(jnp.bfloat16)
+    second = jnp.dot(
+        turned[share:, :], rows_all[:, split:], preferred_element_type=jnp.float32
+    ).astype(jnp.bfloat16)
     step = 128
     width = rows_all.shape[1]
     for at in range(0, width, step):
@@ -484,23 +491,29 @@
         4 * total_slots * width,
     )
     back = swap_dp(both.reshape(groups, slot_count, width))
-    back, cols = lax.optimization_barrier((back, cols))
-    both_rows = from_slots(back)
-    row_blocks, row_pieces, row_slots = gather_rows(both_rows)
     col_pieces = [
         (which, index, ((dc * 2 + dy) * 4 + dx) * row_count)
         for which, index, (dx, dy, dc) in col_pieces
     ]
+    turned = call(
+        functools.partial(turn_kernel, col_pieces),
+        None,
+        cols,
+        jax.ShapeDtypeStruct((2 * share, owners * row_count), jnp.bfloat16),
+        [],
+        owners * row_count * share,
+        8 * owners * row_count * share,
+    )
+    back, turned = lax.optimization_barrier((back, turned))
+    both_rows = from_slots(back)
+    row_blocks, row_pieces, row_slots = gather_rows(both_rows)
     each = -(-share * width // (128 * 8 * groups)) * 8
     partial = call(
-        functools.partial(weight_grad_kernel, row_pieces, col_pieces, qkv_width),
+        functools.partial(weight_grad_kernel, row_pieces, qkv_width),
         row_slots,
-        [*cols, *row_blocks],
+        [turned, *row_blocks],
         jax.ShapeDtypeStruct((groups * each, 128), jnp.bfloat16),
-        [
-            pltpu.VMEM((owners * row_count, width), jnp.bfloat16),
-            pltpu.VMEM((owners * row_count, 2 * share), jnp.bfloat16),
-        ],
+        [pltpu.VMEM((owners * row_count, width), jnp.bfloat16)],
         2 * owners * row_count * width * share,
         2 * owners * row_count * (width + 2 * share),
     )

time: 334 us -> 339 us (1.015)
  Pallas kernels: 46.8 us -> 50.2 us
    pallas_call x10 -> x11, Pallas kernels: 46.8 us -> 50.2 us  [call(): pl.pallas_call(kernel, out_shape=out_shape, in_specs=smem + [vmem] * len(...]
    unnamed x52 -> x54, local copies, waits for them, and re-layouts: 4.96 us -> 6.86 us
  transfers between devices with their start and end apart: 30 -> 30, of which waited for: 14 -> 14; matrix products, arithmetic and copies ran while one was open for 5% -> 4% of each run, Pallas kernels for 9% -> 10%
where the time goes in v6:
time: 339 us; the launch traced here: 337 us
  starting transfers between devices  109 us (32%)
  waiting for transfers between devices  104 us (31%)
  Pallas kernels  50.2 us (15%)
  blocking collectives  45.9 us (14%)
  local copies, waits for them, and re-layouts  18.8 us (6%)
  other arithmetic  7.44 us (2%)
    pallas_call x11, Pallas kernels, call(): pl.pallas_call(kernel, out_shape=out_shape, in_specs=smem + [vmem] * len(...  50.2 us
    all_to_all x1, blocking collectives, swap_dp(): return lax.all_to_all(array, DP, split_axis=0, concat_axis=0, tiled=True)  45.9 us
    ppermute x3, waiting for transfers between devices, swap_y(): return lax.ppermute(array, 'yl', [(0, 1), (1, 0)])  31.9 us
    all_to_all x3, starting transfers between devices, swap_dp(): return lax.all_to_all(array, DP, split_axis=0, concat_axis=0, tiled=True)  30.5 us
    all_to_all x3, waiting for transfers between devices, swap_dp(): return lax.all_to_all(array, DP, split_axis=0, concat_axis=0, tiled=True)  26.3 us
    ppermute x9, starting transfers between devices, along_x(): return lax.ppermute(array, ('x', 'core'), pairs)  24.9 us
    ppermute x9, waiting for transfers between devices, along_x(): return lax.ppermute(array, ('x', 'core'), pairs)  22.9 us
    ppermute x8, starting transfers between devices, swap_core(): return lax.ppermute(array, 'core', [(0, 1), (1, 0)])  22.5 us
  transfers between devices with their start and end apart: 30, of which 14 were waited for; matrix products, arithmetic and copies ran while one was open for 4% of the time, Pallas kernels for 10%

profile of v6, /device:TPU:8, one launch (start us, length us, event | category | flops | bytes accessed | tf_op | source)
XLA Modules:
  0.0 337.2 jit_solution(98396590470764636)
XLA Ops:
  4.5 3.4 %collective-permute-start.4 = (bf16[256,1280]{1,0:T(8,128)(2,1)}, bf16[256,1280]{1,0:T(8,128)(2,1)S(1)}, u32[]{:S(2)}, u32[]{:S(2)}) collective-permute-start(bf16[256,1280]{1,0:T(8,128)(2,1)} %shard_map.93.refs_0_), channel_id=1, source_target_pairs={{0,2},{1,7},{2,4},{3,1},{4,6},{5,3},{6,0},{7,5},{8,10},{9,15},{10,... | collective-permute-start | bytes 1966088 | tf_op jit(solution)/shard_map/ppermute | solution.py:110
  7.9 3.5 %collective-permute-start.5 = (bf16[256,1280]{1,0:T(8,128)(2,1)}, bf16[256,1280]{1,0:T(8,128)(2,1)S(1)}, u32[]{:S(2)}, u32[]{:S(2)}) collective-permute-start(bf16[256,1280]{1,0:T(8,128)(2,1)} %shard_map.93.refs_0_), channel_id=1, source_target_pairs={{0,8},{1,57},{8,16},{9,1},{16,24},{17,9},{24,32},{25,17},{32,40},{... | collective-permute-start | bytes 1966088 | tf_op jit(solution)/shard_map/ppermute | solution.py:119
  12.1 3.8 %shard_map.94 = (bf16[128,4096]{1,0:T(8,128)(2,1)}, bf16[4,2,128,512]{3,2,1,0:T(8,128)(2,1)}, bf16[4,2,128,512]{3,2,1,0:T(8,128)(2,1)}) custom-call(s32[16]{0:T(128)} %stack.149.places, bf16[128,4096]{1,0:T(8,128)(2,1)} %bitcast.63, bf16[128,4096]{1,0:T(8,128)(2,1)} %bitcast.59), custom_call_target="tpu_custom_call" | custom-call | flops 2097152 | bytes 5242880 | tf_op jit(solution)/shard_map/pallas_call | solution.py:369
  15.9 8.5 %collective-permute-start.3 = (bf16[4,2,128,512]{3,2,1,0:T(8,128)(2,1)}, bf16[4,2,128,512]{3,2,1,0:T(8,128)(2,1)S(1)}, u32[]{:S(2)}, u32[]{:S(2)}) collective-permute-start(bf16[4,2,128,512]{3,2,1,0:T(8,128)(2,1)} %get-tuple-element.33), channel_id=1, source_target_pairs={{0,1},{1,0},{2,3},{3,2},{4,5},{5,4},{6,7},{7,6},{8,9},{9,8},{10,11... | collective-permute-start | bytes 3145736 | tf_op jit(solution)/shard_map/ppermute | solution.py:127
  26.1 3.6 %collective-permute-start.1 = (bf16[256,1280]{1,0:T(8,128)(2,1)}, bf16[256,1280]{1,0:T(8,128)(2,1)S(1)}, u32[]{:S(2)}, u32[]{:S(2)}) collective-permute-start(bf16[256,1280]{1,0:T(8,128)(2,1)} %collective-permute-done.refs_1_), channel_id=1, source_target_pairs={{0,2},{1,7},{2,4},{3,1},{4,6},{5,3},{6,0},{7,5},{8,10},{9,15},{10,... | collective-permute-start | bytes 1966088 | tf_op jit(solution)/shard_map/ppermute | solution.py:110
  33.9 6.0 %collective-permute-done.1.refs_3_ = bf16[256,1280]{1,0:T(8,128)(2,1)S(1)} collective-permute-done((bf16[256,1280]{1,0:T(8,128)(2,1)}, bf16[256,1280]{1,0:T(8,128)(2,1)S(1)}, u32[]{:S(2)}, u32[]{:S(2)}) %collective-permute-start.1) | collective-permute-done | bytes 655392 | tf_op jit(solution)/shard_map/ppermute | solution.py:110
  60.5 11.5 %collective-permute-done.9.refs_3_.refs_9_ = bf16[256,1280]{1,0:T(8,128)(2,1)S(1)} collective-permute-done((bf16[256,1280]{1,0:T(8,128)(2,1)}, bf16[256,1280]{1,0:T(8,128)(2,1)S(1)}, u32[]{:S(2)}, u32[]{:S(2)}) %collective-permute-start.9) | collective-permute-done | bytes 655392 | tf_op jit(solution)/shard_map/ppermute | solution.py:110
  75.2 4.9 %shard_map.96.begun = f32[128,1280]{1,0:T(8,128)} custom-call(s32[8]{0:T(128)} %stack.151.places, bf16[128,4096]{1,0:T(8,128)(2,1)} %get-tuple-element.37.normed, bf16[128,4096]{1,0:T(8,128)(2,1)} %bitcast.60, bf16[256,1280]{1,0:T(8,128)(2,1)} %shard_map.93.refs_0_, bf16[256,1280]{1,0:T(8,128)(2,1)} %collective-permute-done.refs_1_, ...), custom_call_target="tpu_custom_call" | custom-call | flops 671088640 | bytes 5242880 | tf_op jit(solution)/shard_map/pallas_call | solution.py:369
  81.4 5.4 %shard_map.97 = bf16[192,1408]{1,0:T(8,128)(2,1)} custom-call(s32[8]{0:T(128)} %stack.150.places, bf16[128,4096]{1,0:T(8,128)(2,1)} %get-tuple-element.37.normed, bf16[128,4096]{1,0:T(8,128)(2,1)} %bitcast.61, f32[128,1280]{1,0:T(8,128)} %shard_map.96.begun, bf16[192,128]{1,0:T(8,128)(2,1)} %fusion.routing, bf16[128,128]{1,0:T(8,128)(2,1)} %broadcast_in_dim.26.flags, ...), custom_call_target="tpu_custom_call" | custom-call | flops 671088640 | bytes 5242880 | tf_op jit(solution)/shard_map/pallas_call | solution.py:369
  88.8 14.6 %all-to-all-start = ((bf16[48,4,1408]{2,1,0:T(4,128)(2,1)}), bf16[48,4,1408]{2,1,0:T(4,128)(2,1)S(1)}, u32[]{:S(2)}, u32[]{:S(2)}) async-start(bf16[48,4,1408]{2,1,0:T(4,128)(2,1)} %reshape.98), calls=%async_computation | async-start | bytes 1081344 | tf_op jit(solution)/shard_map/all_to_all | solution.py:548
  105.3 5.1 %collective-permute-start.13 = (bf16[3,2,128,512]{3,2,1,0:T(8,128)(2,1)}, bf16[3,2,128,512]{3,2,1,0:T(8,128)(2,1)S(1)}, u32[]{:S(2)}, u32[]{:S(2)}) collective-permute-start(bf16[3,2,128,512]{3,2,1,0:T(8,128)(2,1)} %get-tuple-element.49), channel_id=1, source_target_pairs={{0,6},{2,0},{4,2},{6,4},{1,7},{3,1},{5,3},{7,5},{8,14},{10,8},{12,... | collective-permute-start | bytes 2359304 | tf_op jit(solution)/shard_map/ppermute | solution.py:101
  111.8 14.6 %collective-permute-done.12.up.refs_2_ = bf16[3,2,128,512]{3,2,1,0:T(8,128)(2,1)S(1)} collective-permute-done((bf16[3,2,128,512]{3,2,1,0:T(8,128)(2,1)}, bf16[3,2,128,512]{3,2,1,0:T(8,128)(2,1)S(1)}, u32[]{:S(2)}, u32[]{:S(2)}) %collective-permute-start.12) | collective-permute-done | bytes 786464 | tf_op jit(solution)/shard_map/ppermute | solution.py:101
  128.3 3.9 %all-to-all-done = bf16[48,4,1408]{2,1,0:T(4,128)(2,1)S(1)} async-done(((bf16[48,4,1408]{2,1,0:T(4,128)(2,1)}), bf16[48,4,1408]{2,1,0:T(4,128)(2,1)S(1)}, u32[]{:S(2)}, u32[]{:S(2)}) %all-to-all-start) | async-done | bytes 540704 | tf_op jit(solution)/shard_map/all_to_all | solution.py:548
  133.0 5.4 %shard_map.98 = bf16[192,1280]{1,0:T(8,128)(2,1)} custom-call(s32[1]{0:T(128)} %bitcast.24.length, s32[192,1]{1,0:T(8,128)} %copy.14.place_col, s32[1,192]{1,0:T(1,128)} %bitcast.68, bf16[192,1408]{1,0:T(8,128)(2,1)} %reshape.99.got), custom_call_target="tpu_custom_call" | custom-call | flops 339738624 | bytes 983040 | tf_op jit(solution)/shard_map/pallas_call | solution.py:369
  140.4 10.7 %all-to-all-start.1 = ((bf16[48,4,1280]{2,1,0:T(4,128)(2,1)}), bf16[48,4,1280]{2,1,0:T(4,128)(2,1)S(1)}, u32[]{:S(2)}, u32[]{:S(2)}) async-start(bf16[48,4,1280]{2,1,0:T(4,128)(2,1)} %reshape.100), calls=%async_computation.1 | async-start | bytes 983040 | tf_op jit(solution)/shard_map/all_to_all | solution.py:548
  151.2 5.1 %collective-permute-start.15 = (bf16[2,128,512]{2,1,0:T(8,128)(2,1)S(1)}, bf16[2,128,512]{2,1,0:T(8,128)(2,1)S(1)}, u32[]{:S(2)}, u32[]{:S(2)}) collective-permute-start(bf16[2,128,512]{2,1,0:T(8,128)(2,1)S(1)} %slice_bitcast_fusion), channel_id=1, source_target_pairs={{0,6},{2,0},{4,2},{6,4},{1,7},{3,1},{5,3},{7,5},{8,14},{10,8},{12,... | collective-permute-start | bytes 786440 | tf_op jit(solution)/shard_map/ppermute | solution.py:101
  156.4 4.2 %collective-permute-done.15.far_down.refs_5_ = bf16[2,128,512]{2,1,0:T(8,128)(2,1)S(1)} collective-permute-done((bf16[2,128,512]{2,1,0:T(8,128)(2,1)S(1)}, bf16[2,128,512]{2,1,0:T(8,128)(2,1)S(1)}, u32[]{:S(2)}, u32[]{:S(2)}) %collective-permute-start.15) | collective-permute-done | bytes 262176 | tf_op jit(solution)/shard_map/ppermute | solution.py:101
  161.3 3.2 shard_map.99
  164.4 3.7 %collective-permute-start.16 = (bf16[8,128,512]{2,1,0:T(8,128)(2,1)}, bf16[8,128,512]{2,1,0:T(8,128)(2,1)S(1)}, u32[]{:S(2)}, u32[]{:S(2)}) collective-permute-start(bf16[8,128,512]{2,1,0:T(8,128)(2,1)} %shard_map.99), channel_id=1, source_target_pairs={{0,8},{8,0},{1,9},{9,1},{2,10},{10,2},{3,11},{11,3},{4,12},{12,4},... | collective-permute-start | bytes 3145736 | tf_op jit(solution)/shard_map/ppermute | solution.py:123
  168.1 24.6 %collective-permute-done.16.refs_6_ = bf16[8,128,512]{2,1,0:T(8,128)(2,1)S(1)} collective-permute-done((bf16[8,128,512]{2,1,0:T(8,128)(2,1)}, bf16[8,128,512]{2,1,0:T(8,128)(2,1)S(1)}, u32[]{:S(2)}, u32[]{:S(2)}) %collective-permute-start.16) | collective-permute-done | bytes 1048608 | tf_op jit(solution)/shard_map/ppermute | solution.py:123
  193.7 4.5 %shard_map.100.turned = bf16[512,2048]{1,0:T(8,128)(2,1)} custom-call(bf16[4,2,128,512]{3,2,1,0:T(8,128)(2,1)} %get-tuple-element.46.keep.refs_0_, bf16[4,2,128,512]{3,2,1,0:T(8,128)(2,1)} %copy-done, bf16[3,2,128,512]{3,2,1,0:T(8,128)(2,1)} %copy-done.5, bf16[3,2,128,512]{3,2,1,0:T(8,128)(2,1)} %copy-done.6, bf16[2,128,512]{2,1,0:T(8,128)(2,1)} %copy-done.19, ...), custom_call_target="tpu_custom_call" | custom-call | flops 524288 | bytes 4194304 | tf_op jit(solution)/shard_map/pallas_call | solution.py:369
  205.3 3.5 %collective-permute-start.19 = (bf16[128,1280]{1,0:T(8,128)(2,1)S(1)}, bf16[128,1280]{1,0:T(8,128)(2,1)S(1)}, u32[]{:S(2)}, u32[]{:S(2)}) collective-permute-start(bf16[128,1280]{1,0:T(8,128)(2,1)S(1)} %collective-permute-done.17.refs_1_), channel_id=1, source_target_pairs={{0,2},{1,7},{2,4},{3,1},{4,6},{5,3},{6,0},{7,5},{8,10},{9,15},{10,... | collective-permute-start | bytes 983048 | tf_op jit(solution)/shard_map/ppermute | solution.py:110
  208.8 3.8 %collective-permute-done.20.refs_4_ = bf16[128,1280]{1,0:T(8,128)(2,1)S(1)} collective-permute-done((bf16[128,1280]{1,0:T(8,128)(2,1)S(1)}, bf16[128,1280]{1,0:T(8,128)(2,1)S(1)}, u32[]{:S(2)}, u32[]{:S(2)}) %collective-permute-start.20) | collective-permute-done | bytes 327712 | tf_op jit(solution)/shard_map/ppermute | solution.py:123
  214.5 3.1 collective-permute-start.24
  217.6 3.2 collective-permute-start.23
  226.2 3.5 %collective-permute-done.23.refs_7_ = bf16[128,1280]{1,0:T(8,128)(2,1)S(1)} collective-permute-done((bf16[128,1280]{1,0:T(8,128)(2,1)S(1)}, bf16[128,1280]{1,0:T(8,128)(2,1)S(1)}, u32[]{:S(2)}, u32[]{:S(2)}) %collective-permute-start.23) | collective-permute-done | bytes 327712 | tf_op jit(solution)/shard_map/ppermute | solution.py:123
  229.8 3.1 collective-permute-done.25.refs_9_
  242.9 5.9 %shard_map.101 = bf16[2688,128]{1,0:T(8,128)(2,1)} custom-call(s32[16]{0:T(128)} %stack.140.slots, bf16[512,2048]{1,0:T(8,128)(2,1)} %shard_map.100.turned, bf16[128,1280]{1,0:T(8,128)(2,1)} %copy-done.7, bf16[128,1280]{1,0:T(8,128)(2,1)} %copy-done.23, bf16[128,1280]{1,0:T(8,128)(2,1)} %copy-done.16, bf16[128,1280]{1,0:T(8,128)(2,1)} %copy-done.17, ...), custom_call_target="tpu_custom_call" | custom-call | flops 1342177280 | bytes 7340032 | tf_op jit(solution)/shard_map/pallas_call | solution.py:369
  248.7 45.9 %all_to_all.20 = bf16[48,56,128]{2,1,0:T(8,128)(2,1)S(1)} all-to-all(bf16[48,56,128]{2,1,0:T(8,128)(2,1)} %bitcast.66), channel_id=1, replica_groups=mesh['z'=12,'yh'=4,'yl'=2,'x'=4,'core'=2] {'z','yh'}, dimensions={0} | all-to-all | bytes 1376256 | tf_op jit(solution)/shard_map/all_to_all | solution.py:548
  295.7 5.2 %all-to-all-start.3 = ((bf16[48,56,128]{2,1,0:T(8,128)(2,1)}), bf16[48,56,128]{2,1,0:T(8,128)(2,1)S(1)}, u32[]{:S(2)}, u32[]{:S(2)}) async-start(bf16[48,56,128]{2,1,0:T(8,128)(2,1)} %broadcast_in_dim.55), calls=%async_computation.3 | async-start | bytes 1376256 | tf_op jit(solution)/shard_map/all_to_all | solution.py:548
  301.5 10.2 %shard_map.102 = (bf16[128,4096]{1,0:T(8,128)(2,1)}, bf16[128,4096]{1,0:T(8,128)(2,1)}) custom-call(s32[16]{0:T(128)} %concatenate.16.places, bf16[128,1280]{1,0:T(8,128)(2,1)} %copy-done.7, bf16[128,4096]{1,0:T(8,128)(2,1)} %bitcast.64, bf16[128,4096]{1,0:T(8,128)(2,1)} %bitcast.62, bf16[256,1280]{1,0:T(8,128)(2,1)} %shard_map.93.refs_0_, ...), custom_call_target="tpu_custom_call" | custom-call | flops 1342177280 | bytes 10485760 | tf_op jit(solution)/shard_map/pallas_call | solution.py:369
  311.8 22.4 %all-to-all-done.3 = bf16[48,56,128]{2,1,0:T(8,128)(2,1)S(1)} async-done(((bf16[48,56,128]{2,1,0:T(8,128)(2,1)}), bf16[48,56,128]{2,1,0:T(8,128)(2,1)S(1)}, u32[]{:S(2)}, u32[]{:S(2)}) %all-to-all-start.3) | async-done | bytes 688160 | tf_op jit(solution)/shard_map/all_to_all | solution.py:548
  (131 shorter events, 75.9 us)
Async XLA Ops:
  2.6 23.4 %collective-permute-start = (bf16[256,1280]{1,0:T(8,128)(2,1)}, bf16[256,1280]{1,0:T(8,128)(2,1)}, u32[]{:S(2)}, u32[]{:S(2)}) collective-permute-start(bf16[256,1280]{1,0:T(8,128)(2,1)} %shard_map.93.refs_0_), channel_id=1, source_target_pairs={{0,1},{1,0},{2,3},{3,2},{4,5},{5,4},{6,7},{7,6},{8,9},{9,8},{10,11... | collective-permute-start | bytes 1966088 | tf_op jit(solution)/shard_map/ppermute | solution.py:127
  4.5 25.5 %collective-permute-start.4 = (bf16[256,1280]{1,0:T(8,128)(2,1)}, bf16[256,1280]{1,0:T(8,128)(2,1)S(1)}, u32[]{:S(2)}, u32[]{:S(2)}) collective-permute-start(bf16[256,1280]{1,0:T(8,128)(2,1)} %shard_map.93.refs_0_), channel_id=1, source_target_pairs={{0,2},{1,7},{2,4},{3,1},{4,6},{5,3},{6,0},{7,5},{8,10},{9,15},{10,... | collective-permute-start | bytes 1966088 | tf_op jit(solution)/shard_map/ppermute | solution.py:110
  7.9 38.4 %collective-permute-start.5 = (bf16[256,1280]{1,0:T(8,128)(2,1)}, bf16[256,1280]{1,0:T(8,128)(2,1)S(1)}, u32[]{:S(2)}, u32[]{:S(2)}) collective-permute-start(bf16[256,1280]{1,0:T(8,128)(2,1)} %shard_map.93.refs_0_), channel_id=1, source_target_pairs={{0,8},{1,57},{8,16},{9,1},{16,24},{17,9},{24,32},{25,17},{32,40},{... | collective-permute-start | bytes 1966088 | tf_op jit(solution)/shard_map/ppermute | solution.py:119
  15.9 26.6 %collective-permute-start.3 = (bf16[4,2,128,512]{3,2,1,0:T(8,128)(2,1)}, bf16[4,2,128,512]{3,2,1,0:T(8,128)(2,1)S(1)}, u32[]{:S(2)}, u32[]{:S(2)}) collective-permute-start(bf16[4,2,128,512]{3,2,1,0:T(8,128)(2,1)} %get-tuple-element.33), channel_id=1, source_target_pairs={{0,1},{1,0},{2,3},{3,2},{4,5},{5,4},{6,7},{7,6},{8,9},{9,8},{10,11... | collective-permute-start | bytes 3145736 | tf_op jit(solution)/shard_map/ppermute | solution.py:127
  26.1 13.9 %collective-permute-start.1 = (bf16[256,1280]{1,0:T(8,128)(2,1)}, bf16[256,1280]{1,0:T(8,128)(2,1)S(1)}, u32[]{:S(2)}, u32[]{:S(2)}) collective-permute-start(bf16[256,1280]{1,0:T(8,128)(2,1)} %collective-permute-done.refs_1_), channel_id=1, source_target_pairs={{0,2},{1,7},{2,4},{3,1},{4,6},{5,3},{6,0},{7,5},{8,10},{9,15},{10,... | collective-permute-start | bytes 1966088 | tf_op jit(solution)/shard_map/ppermute | solution.py:110
  29.9 81.1 %copy-start.24 = (s32[192]{0:T(256)}, s32[192]{0:T(256)S(1)}, u32[]{:S(2)}) copy-start(s32[192]{0:T(256)S(1)} %add.484) | copy-start | bytes 2308
  30.0 45.1 %copy-start.2 = (bf16[256,1280]{1,0:T(8,128)(2,1)}, bf16[256,1280]{1,0:T(8,128)(2,1)S(1)}, u32[]{:S(2)}) copy-start(bf16[256,1280]{1,0:T(8,128)(2,1)S(1)} %collective-permute-done.4.refs_2_) | copy-start | bytes 1966084
  30.1 23.2 %collective-permute-start.7 = (bf16[256,1280]{1,0:T(8,128)(2,1)S(1)}, bf16[256,1280]{1,0:T(8,128)(2,1)}, u32[]{:S(2)}, u32[]{:S(2)}) collective-permute-start(bf16[256,1280]{1,0:T(8,128)(2,1)S(1)} %collective-permute-done.4.refs_2_), channel_id=1, source_target_pairs={{0,8},{1,57},{8,16},{9,1},{16,24},{17,9},{24,32},{25,17},{32,40},{... | collective-permute-start | bytes 1966088 | tf_op jit(solution)/shard_map/ppermute | solution.py:119
  32.0 21.3 %collective-permute-start.8 = (bf16[256,1280]{1,0:T(8,128)(2,1)S(1)}, bf16[256,1280]{1,0:T(8,128)(2,1)}, u32[]{:S(2)}, u32[]{:S(2)}) collective-permute-start(bf16[256,1280]{1,0:T(8,128)(2,1)S(1)} %collective-permute-done.4.refs_2_), channel_id=1, source_target_pairs={{0,2},{1,7},{2,4},{3,1},{4,6},{5,3},{6,0},{7,5},{8,10},{9,15},{10,... | collective-permute-start | bytes 1966088 | tf_op jit(solution)/shard_map/ppermute | solution.py:110
  40.0 12.6 %collective-permute-start.2 = (bf16[256,1280]{1,0:T(8,128)(2,1)S(1)}, bf16[256,1280]{1,0:T(8,128)(2,1)}, u32[]{:S(2)}, u32[]{:S(2)}) collective-permute-start(bf16[256,1280]{1,0:T(8,128)(2,1)S(1)} %collective-permute-done.1.refs_3_), channel_id=1, source_target_pairs={{0,8},{1,57},{8,16},{9,1},{16,24},{17,9},{24,32},{25,17},{32,40},{... | collective-permute-start | bytes 1966088 | tf_op jit(solution)/shard_map/ppermute | solution.py:119
  47.8 27.4 %collective-permute-start.6 = (bf16[768,1280]{1,0:T(8,128)(2,1)}, bf16[768,1280]{1,0:T(8,128)(2,1)}, u32[]{:S(2)}, u32[]{:S(2)}) collective-permute-start(bf16[768,1280]{1,0:T(8,128)(2,1)} %pad_maximum_fusion), channel_id=1, source_target_pairs={{0,1},{1,0},{2,3},{3,2},{4,5},{5,4},{6,7},{7,6},{8,9},{9,8},{10,11... | collective-permute-start | bytes 5898248 | tf_op jit(solution)/shard_map/ppermute | solution.py:127
  56.1 24.0 %collective-permute-start.10 = (bf16[768,1280]{1,0:T(8,128)(2,1)}, bf16[768,1280]{1,0:T(8,128)(2,1)S(1)}, u32[]{:S(2)}, u32[]{:S(2)}) collective-permute-start(bf16[768,1280]{1,0:T(8,128)(2,1)} %pad_maximum_fusion.1), channel_id=1, source_target_pairs={{0,1},{1,0},{2,3},{3,2},{4,5},{5,4},{6,7},{7,6},{8,9},{9,8},{10,11... | collective-permute-start | bytes 5898248 | tf_op jit(solution)/shard_map/ppermute | solution.py:127
  58.0 13.9 %collective-permute-start.9 = (bf16[256,1280]{1,0:T(8,128)(2,1)}, bf16[256,1280]{1,0:T(8,128)(2,1)S(1)}, u32[]{:S(2)}, u32[]{:S(2)}) collective-permute-start(bf16[256,1280]{1,0:T(8,128)(2,1)} %collective-permute-done.7.refs_0_.refs_6_), channel_id=1, source_target_pairs={{0,2},{1,7},{2,4},{3,1},{4,6},{5,3},{6,0},{7,5},{8,10},{9,15},{10,... | collective-permute-start | bytes 1966088 | tf_op jit(solution)/shard_map/ppermute | solution.py:110
  71.9 8.1 %collective-permute-start.11 = (bf16[256,1280]{1,0:T(8,128)(2,1)S(1)}, bf16[256,1280]{1,0:T(8,128)(2,1)}, u32[]{:S(2)}, u32[]{:S(2)}) collective-permute-start(bf16[256,1280]{1,0:T(8,128)(2,1)S(1)} %collective-permute-done.9.refs_3_.refs_9_), channel_id=1, source_target_pairs={{0,1},{1,0},{2,3},{3,2},{4,5},{5,4},{6,7},{7,6},{8,9},{9,8},{10,11... | collective-permute-start | bytes 1966088 | tf_op jit(solution)/shard_map/ppermute | solution.py:127
  88.8 43.4 %all-to-all-start = ((bf16[48,4,1408]{2,1,0:T(4,128)(2,1)}), bf16[48,4,1408]{2,1,0:T(4,128)(2,1)S(1)}, u32[]{:S(2)}, u32[]{:S(2)}) async-start(bf16[48,4,1408]{2,1,0:T(4,128)(2,1)} %reshape.98), calls=%async_computation | async-start | bytes 1081344 | tf_op jit(solution)/shard_map/all_to_all | solution.py:548
  103.3 23.0 %collective-permute-start.12 = (bf16[3,2,128,512]{3,2,1,0:T(8,128)(2,1)}, bf16[3,2,128,512]{3,2,1,0:T(8,128)(2,1)S(1)}, u32[]{:S(2)}, u32[]{:S(2)}) collective-permute-start(bf16[3,2,128,512]{3,2,1,0:T(8,128)(2,1)} %get-tuple-element.48), channel_id=1, source_target_pairs={{0,2},{2,4},{4,6},{6,0},{1,3},{3,5},{5,7},{7,1},{8,10},{10,12},{12... | collective-permute-start | bytes 2359304 | tf_op jit(solution)/shard_map/ppermute | solution.py:101
  105.3 45.9 %collective-permute-start.13 = (bf16[3,2,128,512]{3,2,1,0:T(8,128)(2,1)}, bf16[3,2,128,512]{3,2,1,0:T(8,128)(2,1)S(1)}, u32[]{:S(2)}, u32[]{:S(2)}) collective-permute-start(bf16[3,2,128,512]{3,2,1,0:T(8,128)(2,1)} %get-tuple-element.49), channel_id=1, source_target_pairs={{0,6},{2,0},{4,2},{6,4},{1,7},{3,1},{5,3},{7,5},{8,14},{10,8},{12,... | collective-permute-start | bytes 2359304 | tf_op jit(solution)/shard_map/ppermute | solution.py:101
  126.3 30.0 %collective-permute-start.14 = (bf16[2,128,512]{2,1,0:T(8,128)(2,1)S(1)}, bf16[2,128,512]{2,1,0:T(8,128)(2,1)S(1)}, u32[]{:S(2)}, u32[]{:S(2)}) collective-permute-start(bf16[2,128,512]{2,1,0:T(8,128)(2,1)S(1)} %slice_bitcast_fusion.1), channel_id=1, source_target_pairs={{0,2},{2,4},{4,6},{6,0},{1,3},{3,5},{5,7},{7,1},{8,10},{10,12},{12... | collective-permute-start | bytes 786440 | tf_op jit(solution)/shard_map/ppermute | solution.py:101
  140.4 57.8 %all-to-all-start.1 = ((bf16[48,4,1280]{2,1,0:T(4,128)(2,1)}), bf16[48,4,1280]{2,1,0:T(4,128)(2,1)S(1)}, u32[]{:S(2)}, u32[]{:S(2)}) async-start(bf16[48,4,1280]{2,1,0:T(4,128)(2,1)} %reshape.100), calls=%async_computation.1 | async-start | bytes 983040 | tf_op jit(solution)/shard_map/all_to_all | solution.py:548
  151.2 9.4 %collective-permute-start.15 = (bf16[2,128,512]{2,1,0:T(8,128)(2,1)S(1)}, bf16[2,128,512]{2,1,0:T(8,128)(2,1)S(1)}, u32[]{:S(2)}, u32[]{:S(2)}) collective-permute-start(bf16[2,128,512]{2,1,0:T(8,128)(2,1)S(1)} %slice_bitcast_fusion), channel_id=1, source_target_pairs={{0,6},{2,0},{4,2},{6,4},{1,7},{3,1},{5,3},{7,5},{8,14},{10,8},{12,... | collective-permute-start | bytes 786440 | tf_op jit(solution)/shard_map/ppermute | solution.py:101
  164.4 28.3 %collective-permute-start.16 = (bf16[8,128,512]{2,1,0:T(8,128)(2,1)}, bf16[8,128,512]{2,1,0:T(8,128)(2,1)S(1)}, u32[]{:S(2)}, u32[]{:S(2)}) collective-permute-start(bf16[8,128,512]{2,1,0:T(8,128)(2,1)} %shard_map.99), channel_id=1, source_target_pairs={{0,8},{8,0},{1,9},{9,1},{2,10},{10,2},{3,11},{11,3},{4,12},{12,4},... | collective-permute-start | bytes 3145736 | tf_op jit(solution)/shard_map/ppermute | solution.py:123
  198.6 6.7 %collective-permute-start.17 = (bf16[128,1280]{1,0:T(8,128)(2,1)S(1)}, bf16[128,1280]{1,0:T(8,128)(2,1)S(1)}, u32[]{:S(2)}, u32[]{:S(2)}) collective-permute-start(bf16[128,1280]{1,0:T(8,128)(2,1)S(1)} %convolution_convert_fusion.refs_0_.both), channel_id=1, source_target_pairs={{0,1},{1,0},{2,3},{3,2},{4,5},{5,4},{6,7},{7,6},{8,9},{9,8},{10,11... | collective-permute-start | bytes 983048 | tf_op jit(solution)/shard_map/ppermute | solution.py:127
  200.5 12.0 %collective-permute-start.20 = (bf16[128,1280]{1,0:T(8,128)(2,1)S(1)}, bf16[128,1280]{1,0:T(8,128)(2,1)S(1)}, u32[]{:S(2)}, u32[]{:S(2)}) collective-permute-start(bf16[128,1280]{1,0:T(8,128)(2,1)S(1)} %convolution_convert_fusion.refs_0_.both), channel_id=1, source_target_pairs={{0,8},{8,0},{1,9},{9,1},{2,10},{10,2},{3,11},{11,3},{4,12},{12,4},... | collective-permute-start | bytes 983048 | tf_op jit(solution)/shard_map/ppermute | solution.py:123
  203.3 11.1 %collective-permute-start.18 = (bf16[128,1280]{1,0:T(8,128)(2,1)S(1)}, bf16[128,1280]{1,0:T(8,128)(2,1)S(1)}, u32[]{:S(2)}, u32[]{:S(2)}) collective-permute-start(bf16[128,1280]{1,0:T(8,128)(2,1)S(1)} %convolution_convert_fusion.refs_0_.both), channel_id=1, source_target_pairs={{0,2},{1,7},{2,4},{3,1},{4,6},{5,3},{6,0},{7,5},{8,10},{9,15},{10,... | collective-permute-start | bytes 983048 | tf_op jit(solution)/shard_map/ppermute | solution.py:110
  205.3 12.3 %collective-permute-start.19 = (bf16[128,1280]{1,0:T(8,128)(2,1)S(1)}, bf16[128,1280]{1,0:T(8,128)(2,1)S(1)}, u32[]{:S(2)}, u32[]{:S(2)}) collective-permute-start(bf16[128,1280]{1,0:T(8,128)(2,1)S(1)} %collective-permute-done.17.refs_1_), channel_id=1, source_target_pairs={{0,2},{1,7},{2,4},{3,1},{4,6},{5,3},{6,0},{7,5},{8,10},{9,15},{10,... | collective-permute-start | bytes 983048 | tf_op jit(solution)/shard_map/ppermute | solution.py:110
  212.5 10.2 %collective-permute-start.22 = (bf16[128,1280]{1,0:T(8,128)(2,1)S(1)}, bf16[128,1280]{1,0:T(8,128)(2,1)S(1)}, u32[]{:S(2)}, u32[]{:S(2)}) collective-permute-start(bf16[128,1280]{1,0:T(8,128)(2,1)S(1)} %collective-permute-done.20.refs_4_), channel_id=1, source_target_pairs={{0,2},{1,7},{2,4},{3,1},{4,6},{5,3},{6,0},{7,5},{8,10},{9,15},{10,... | collective-permute-start | bytes 983048 | tf_op jit(solution)/shard_map/ppermute | solution.py:110
  214.5 11.7 %collective-permute-start.24 = (bf16[128,1280]{1,0:T(8,128)(2,1)S(1)}, bf16[128,1280]{1,0:T(8,128)(2,1)S(1)}, u32[]{:S(2)}, u32[]{:S(2)}) collective-permute-start(bf16[128,1280]{1,0:T(8,128)(2,1)S(1)} %collective-permute-done.18.refs_2_), channel_id=1, source_target_pairs={{0,2},{1,7},{2,4},{3,1},{4,6},{5,3},{6,0},{7,5},{8,10},{9,15},{10,... | collective-permute-start | bytes 983048 | tf_op jit(solution)/shard_map/ppermute | solution.py:110
  217.6 12.2 %collective-permute-start.23 = (bf16[128,1280]{1,0:T(8,128)(2,1)S(1)}, bf16[128,1280]{1,0:T(8,128)(2,1)S(1)}, u32[]{:S(2)}, u32[]{:S(2)}) collective-permute-start(bf16[128,1280]{1,0:T(8,128)(2,1)S(1)} %collective-permute-done.19.refs_3_), channel_id=1, source_target_pairs={{0,8},{8,0},{1,9},{9,1},{2,10},{10,2},{3,11},{11,3},{4,12},{12,4},... | collective-permute-start | bytes 983048 | tf_op jit(solution)/shard_map/ppermute | solution.py:123
  222.7 10.2 %collective-permute-start.25 = (bf16[128,1280]{1,0:T(8,128)(2,1)S(1)}, bf16[128,1280]{1,0:T(8,128)(2,1)S(1)}, u32[]{:S(2)}, u32[]{:S(2)}) collective-permute-start(bf16[128,1280]{1,0:T(8,128)(2,1)S(1)} %collective-permute-done.22.refs_6_), channel_id=1, source_target_pairs={{0,2},{1,7},{2,4},{3,1},{4,6},{5,3},{6,0},{7,5},{8,10},{9,15},{10,... | collective-permute-start | bytes 983048 | tf_op jit(solution)/shard_map/ppermute | solution.py:110
  234.0 6.8 %collective-permute-start.26 = (bf16[512,1280]{1,0:T(8,128)(2,1)}, bf16[512,1280]{1,0:T(8,128)(2,1)S(1)}, u32[]{:S(2)}, u32[]{:S(2)}) collective-permute-start(bf16[512,1280]{1,0:T(8,128)(2,1)} %pad_maximum_fusion.2), channel_id=1, source_target_pairs={{0,1},{1,0},{2,3},{3,2},{4,5},{5,4},{6,7},{7,6},{8,9},{9,8},{10,11... | collective-permute-start | bytes 3932168 | tf_op jit(solution)/shard_map/ppermute | solution.py:127
  236.3 4.6 %collective-permute-start.21 = (bf16[384,1280]{1,0:T(8,128)(2,1)S(1)}, bf16[384,1280]{1,0:T(8,128)(2,1)S(1)}, u32[]{:S(2)}, u32[]{:S(2)}) collective-permute-start(bf16[384,1280]{1,0:T(8,128)(2,1)S(1)} %pad_maximum_fusion.3), channel_id=1, source_target_pairs={{0,1},{1,0},{2,3},{3,2},{4,5},{5,4},{6,7},{7,6},{8,9},{9,8},{10,11... | collective-permute-start | bytes 2949128 | tf_op jit(solution)/shard_map/ppermute | solution.py:127
  295.7 38.4 %all-to-all-start.3 = ((bf16[48,56,128]{2,1,0:T(8,128)(2,1)}), bf16[48,56,128]{2,1,0:T(8,128)(2,1)S(1)}, u32[]{:S(2)}, u32[]{:S(2)}) async-start(bf16[48,56,128]{2,1,0:T(8,128)(2,1)} %broadcast_in_dim.55), calls=%async_computation.3 | async-start | bytes 1376256 | tf_op jit(solution)/shard_map/all_to_all | solution.py:548
  (25 other events, 319.1 us)
